TPU v7x, 32 devices: a whole 2x2x4 slice. The times are simulated.
32 devices in a mesh: groups: 2 (over y), ctx: 4 (over z), mp: 4 (over x, core).
Axes of the slice: x: 2, y: 2, z: 4, core: 2. Of those that a mesh axis runs over, the one named last changes fastest.
Arguments:
- streams: bfloat16 [3, 2048, 4096], P(None, ('groups', 'ctx'), 'mp'), parts along dimension 1, may hold values from -6 to 6
- short_filter: float32 [3, 3, 4096], P(None, None, 'mp'), may hold values from -3 to 3
- mode_params: float32 [2, 4096, 8], P(None, 'mp'), may hold values from -2 to 2, as said below
- out_weight: bfloat16 [4096, 4096], P('mp', 'ctx'), may hold values from -0.09375 to 0.09375
- norm_gain: float32 [4096], P('mp'), may hold values from 0.5 to 1.5
- unembed: bfloat16 [4096, 512], P('mp'), may hold values from -40 to 40
- native: int32 [2048], P(('groups', 'ctx')), parts along dimension 0, may hold values from 0 to 511
- mut_pos: int32 [512], P('groups'), parts along dimension 0, may hold values from 0 to 1023
- mut_ids: int32 [512], P('groups'), parts along dimension 0, may hold values from 0 to 511
Outputs:
- loglik: float32 [2048], P(('groups', 'ctx')), parts along dimension 0
- scores: float32 [512], P('groups'), parts along dimension 0
There are 2 independent parts, one for each index of `groups`. A program takes and returns all parts, laid end to end along the dimension named above; an argument that names none is the same for every part. Nothing has to cross between parts.
Inputs may be any that keep to these rules, and one draw needn't show every extreme that they name: mode_params[0] holds positive decay rates, mode_params[1] residues.
All inputs are finite; a program needn't handle non-finite values.
Results may differ from a plain program's by a relative error of at most 0.0065.
Values may be sent and summed in bfloat16 or wider, within the bound.
No kernel may reach another device: no remote copies, remote signals or barrier semaphores. Data moves between devices by JAX's collectives and lax.ppermute only.
A program may use at most 192 MiB of HBM per device.

v0:
```python
import functools

import jax
import jax.numpy as jnp
from jax import lax
from jax.experimental import pallas as pl
from jax.experimental.pallas import tpu as pltpu
from jax.sharding import PartitionSpec as P


F32 = jnp.float32
BF16 = jnp.bfloat16
LANES = 128
SUBS = 8
EPS = 1e-05


def swap(value, axis, bit):
    count = lax.axis_size(axis)
    return lax.ppermute(value, axis, [(i, i ^ bit) for i in range(count)])


def mix(taps, now, back1, back2):
    return taps[0] * now + taps[1] * back1 + taps[2] * back2


def rounded(value):
    return value.astype(BF16).astype(F32)


def taps_of(filt_ref, stream, cols):
    return [filt_ref[stream, j : j + 1, cols] for j in range(3)]


def lane_slice(tile):
    return pl.ds(pl.multiple_of(tile * LANES, LANES), LANES)


def behind(value):
    sub = lax.broadcasted_iota(jnp.int32, value.shape, 0)
    return jnp.where(sub == 0, 0.0, pltpu.roll(value, 1, 0))


def spread_modes(mode_ref, cols, modes):
    decay = [jnp.broadcast_to(mode_ref[0, m : m + 1, cols], (SUBS, LANES)) for m in range(modes)]
    return decay, [jnp.exp(-d) for d in decay]


def running(state, decay, steps):
    sub = lax.broadcasted_iota(jnp.int32, state.shape, 0)
    for reach in (1, 2, 4):
        power = jnp.exp(-decay * float(steps * reach))
        state = state + jnp.where(sub < reach, 0.0, power * pltpu.roll(state, reach, 0))
    return state


def end_kernel(
    steps, modes, x_any, filt_any, mode_any, nat_any, prod_ref, gate_ref, msg_ref, filt_ref, mode_ref,
    held, nat_ref, xs, sems, side_sems
):
    rows = steps * SUBS
    tiles = held.shape[0]
    base = 2 * modes

    def fetch(tile):
        return pltpu.make_async_copy(x_any.at[1:3, :, lane_slice(tile)], held.at[tile], sems.at[tile])

    sides = [
        pltpu.make_async_copy(src, dst, side_sems.at[k])
        for k, (src, dst) in enumerate(
            ((filt_any, filt_ref), (mode_any, mode_ref), (nat_any, nat_ref), (x_any.at[0], gate_ref))
        )
    ]
    fetch(0).start()
    for side in sides[:3]:
        side.start()

    @pl.loop(1, tiles)
    def _(tile):
        fetch(tile).start()

    sides[3].start()
    for side in sides[:3]:
        side.wait()

    @pl.loop(0, tiles)
    def _(tile):
        cols = lane_slice(tile)
        sub = lax.broadcasted_iota(jnp.int32, (SUBS, LANES), 0)
        decay, fall = spread_modes(mode_ref, cols, modes)
        taps = [taps_of(filt_ref, i, cols) for i in (1, 2)]
        fetch(tile).wait()
        for i in range(2):
            xs[i] = held[tile, i].astype(F32)

        def at(i, t):
            return xs[i, pl.ds(t, SUBS, stride=steps), :]

        back2 = [behind(at(i, steps - 2)) for i in range(2)]
        back1 = [behind(at(i, steps - 1)) for i in range(2)]
        state = [jnp.zeros((SUBS, LANES), F32) for _ in range(modes)]
        for t in range(steps):
            now = [at(i, t) for i in range(2)]
            mixed = [mix(taps[i], now[i], back1[i], back2[i]) for i in range(2)]
            back2, back1 = back1, now
            prod = rounded(mixed[0] * mixed[1])
            if t < 2:
                prod = jnp.where(sub == 0, 0.0, prod)
            prod_ref[t * SUBS : (t + 1) * SUBS, cols] = prod
            state = [f * s + prod for f, s in zip(fall, state)]
        ends = [running(state[m], decay[m], steps)[SUBS - 1 : SUBS, :] for m in range(modes)]
        end = jnp.concatenate(ends, axis=0)
        high = rounded(end)
        edge = [xs[0, 0:2, :], xs[1, 0:2, :], xs[0, rows - 2 : rows, :], xs[1, rows - 2 : rows, :]]
        msg_ref[0 : base + 8, cols] = jnp.concatenate([high, end - high] + edge, axis=0).astype(BF16)

    sides[3].wait()
    width = gate_ref.shape[1]
    ids = nat_ref[...]
    empty = jnp.zeros((1, width - 2 * rows), jnp.int32)
    ids = jnp.concatenate([ids // 256, ids % 256, empty], axis=1).astype(F32)
    head = gate_ref[0:16, :].astype(F32)
    tail = gate_ref[rows - 16 : rows, :].astype(F32)
    other = jnp.concatenate([tail[14:16, :], head[0:2, :], ids, jnp.zeros((3, width), F32)], axis=0)
    msg_ref[base + 8 : base + 16, :] = other.astype(BF16)


def local_kernel(steps, modes, filt_ref, mode_ref, prod_ref, x_ref, y_ref, gate_ref, start_ref, xs, gs):
    @pl.loop(0, x_ref.shape[1] // LANES)
    def _(tile):
        cols = lane_slice(tile)
        decay, fall = spread_modes(mode_ref, cols, modes)
        res = [jnp.broadcast_to(mode_ref[1, m : m + 1, cols], (SUBS, LANES)) for m in range(modes)]
        taps = taps_of(filt_ref, 0, cols)
        xs[...] = x_ref[:, cols].astype(F32)
        back2 = behind(xs[pl.ds(steps - 2, SUBS, stride=steps), :])
        back1 = behind(xs[pl.ds(steps - 1, SUBS, stride=steps), :])
        state = [jnp.zeros((SUBS, LANES), F32) for _ in range(modes)]
        for t in range(steps):
            now = xs[pl.ds(t, SUBS, stride=steps), :]
            gs[pl.ds(t, SUBS, stride=steps), :] = mix(taps, now, back1, back2)
            back2, back1 = back1, now
            prod = prod_ref[t * SUBS : (t + 1) * SUBS, cols]
            state = [f * s + prod for f, s in zip(fall, state)]
            y_ref[t * SUBS : (t + 1) * SUBS, cols] = functools.reduce(
                lambda p, q: p + q, [r * s for r, s in zip(res, state)]
            )
        gate_ref[:, cols] = gs[...].astype(BF16)
        for m in range(modes):
            start_ref[m * SUBS : (m + 1) * SUBS, cols] = behind(running(state[m], decay[m], steps))


SMALL = pltpu.CompilerParams(vmem_limit_bytes=16 * 2**20)


def in_vmem():
    return pl.BlockSpec(memory_space=pltpu.VMEM)


def end_part(streams, filt, modes_t, native):
    rows, width = streams.shape[1:]
    modes = modes_t.shape[1]
    steps = rows // SUBS
    tiles = width // LANES
    msg_rows = 2 * modes + 16
    return pl.pallas_call(
        functools.partial(end_kernel, steps, modes),
        in_specs=[pl.BlockSpec(memory_space=pltpu.HBM)] * 4,
        out_specs=[in_vmem()] * 5,
        out_shape=[
            pltpu.VMEM((rows, width), F32),
            pltpu.VMEM((rows, width), BF16),
            pltpu.VMEM((msg_rows, width), BF16),
            pltpu.VMEM(filt.shape, F32),
            pltpu.VMEM(modes_t.shape, F32),
        ],
        scratch_shapes=[
            pltpu.VMEM((tiles, 2, rows, LANES), BF16),
            pltpu.VMEM((1, rows), jnp.int32),
            pltpu.VMEM((2, rows, LANES), F32),
            pltpu.SemaphoreType.DMA((tiles,)),
            pltpu.SemaphoreType.DMA((4,)),
        ],
        compiler_params=SMALL,
        name="end_part",
    )(*[pltpu.with_memory_space_constraint(v, pltpu.HBM) for v in (streams, filt, modes_t, native[None, :])])


def local_part(filt, modes_t, prod, gate_stream):
    rows, width = prod.shape
    modes = modes_t.shape[1]
    return pl.pallas_call(
        functools.partial(local_kernel, rows // SUBS, modes),
        in_specs=[in_vmem()] * 4,
        out_specs=[in_vmem()] * 3,
        out_shape=[
            pltpu.VMEM((rows, width), F32),
            pltpu.VMEM((rows, width), BF16),
            pltpu.VMEM((modes * SUBS, width), F32),
        ],
        input_output_aliases={2: 0, 3: 1},
        scratch_shapes=[pltpu.VMEM((rows, LANES), F32), pltpu.VMEM((rows, LANES), F32)],
        compiler_params=SMALL,
        name="local_part",
    )(*[pltpu.with_memory_space_constraint(v, pltpu.VMEM) for v in (filt, modes_t, prod, gate_stream)])


def carry_kernel(steps, modes, stacked, count, where_ref, filt_ref, mode_ref, y_ref, gate_ref, start_ref, *rest):
    msg_refs, (out_ref, nat_ref, held, conv) = rest[:-4], rest[-4:]
    me = where_ref[0]
    rows = steps * SUBS
    base = 2 * modes

    @pl.loop(0, y_ref.shape[1] // LANES)
    def _(tile):
        cols = lane_slice(tile)
        sub = lax.broadcasted_iota(jnp.int32, (SUBS, LANES), 0)
        for k in range(count):
            if stacked:
                held[k] = msg_refs[0][k, :, cols].astype(F32)
            else:
                held[me ^ k] = msg_refs[k][:, cols].astype(F32)
        for b in range(count):
            nat_ref[b : b + 1, cols] = held[b, base + 12 : base + 13, :]
        decay = mode_ref[0, :, cols]
        taps = [taps_of(filt_ref, i, cols) for i in range(3)]

        def firsts(own, prior, keep):
            pair = []
            for i, lane in ((1, 0), (2, 2)):
                f0 = own[base + lane : base + lane + 1, :]
                f1 = own[base + lane + 1 : base + lane + 2, :]
                l2 = jnp.where(keep, prior[base + lane + 4 : base + lane + 5, :], 0.0)
                l1 = jnp.where(keep, prior[base + lane + 5 : base + lane + 6, :], 0.0)
                pair.append((mix(taps[i], f0, l1, l2), mix(taps[i], f1, f0, l1)))
            return rounded(pair[0][0] * pair[1][0]), rounded(pair[0][1] * pair[1][1])

        full = jnp.exp(-decay * float(rows))
        near0 = jnp.exp(-decay * float(rows - 1))
        near1 = jnp.exp(-decay * float(rows - 2))

        def advance(b, entering):
            own = held[b]
            p0, p1 = firsts(own, held[jnp.maximum(b - 1, 0)], b > 0)
            end = own[0:modes, :] + own[modes : 2 * modes, :] + near0 * p0 + near1 * p1
            return jnp.where(b < me, full * entering + end, entering)

        entering = jnp.zeros((modes, LANES), F32)
        if count <= 8:
            for b in range(count - 1):
                entering = advance(b, entering)
        else:
            entering = lax.fori_loop(0, count - 1, advance, entering)
        own = held[me]
        prior = held[jnp.maximum(me - 1, 0)]
        p0, p1 = firsts(own, prior, me > 0)
        later = (
            jnp.exp(-decay * float(steps)) * entering
            + jnp.exp(-decay * float(steps - 1)) * p0
            + jnp.exp(-decay * float(steps - 2)) * p1
        )
        shift = float(steps) * jnp.maximum(sub - 1, 0).astype(F32)
        fall, res, flow = [], [], []
        for m in range(modes):
            d = jnp.broadcast_to(decay[m : m + 1, :], (SUBS, LANES))
            r = jnp.broadcast_to(mode_ref[1, m : m + 1, cols], (SUBS, LANES))
            fall.append(jnp.exp(-d))
            res.append(r)
            begin = jnp.where(sub == 0, entering[m : m + 1, :], jnp.exp(-d * shift) * later[m : m + 1, :])
            flow.append(r * (start_ref[m * SUBS : (m + 1) * SUBS, cols] + begin))
        inject = (p0, p1)
        for t in range(steps):
            flow = [f * v for f, v in zip(fall, flow)]
            if t < 2:
                extra = jnp.where(sub == 0, inject[t], 0.0)
                flow = [v + r * extra for v, r in zip(flow, res)]
            conv[pl.ds(t, SUBS, stride=steps), :] = functools.reduce(
                lambda p, q: p + q, flow, y_ref[t * SUBS : (t + 1) * SUBS, cols]
            )
        g0 = own[base + 10 : base + 11, :]
        g1 = own[base + 11 : base + 12, :]
        l2 = jnp.where(me > 0, prior[base + 8 : base + 9, :], 0.0)
        l1 = jnp.where(me > 0, prior[base + 9 : base + 10, :], 0.0)
        head0 = mix(taps[0], g0, l1, l2)
        head1 = mix(taps[0], g1, g0, l1)
        gate = gate_ref[:, cols].astype(F32)
        line = lax.broadcasted_iota(jnp.int32, (16, LANES), 0)
        head = jnp.where(line == 0, rounded(head0), jnp.where(line == 1, rounded(head1), gate[0:16, :]))
        out_ref[0:16, cols] = (head * rounded(conv[0:16, :])).astype(BF16)
        out_ref[16:rows, cols] = (gate[16:rows, :] * rounded(conv[16:rows, :])).astype(BF16)


def carry_part(me, filt, modes_t, y, gate, start, msgs, stacked):
    rows, width = y.shape
    modes = modes_t.shape[1]
    steps = rows // SUBS
    count = msgs[0].shape[0] if stacked else len(msgs)
    msg_rows = msgs[0].shape[-2]
    return pl.pallas_call(
        functools.partial(carry_kernel, steps, modes, stacked, count),
        in_specs=[pl.BlockSpec(memory_space=pltpu.SMEM)] + [in_vmem()] * (5 + len(msgs)),
        out_specs=[in_vmem()] * 2,
        out_shape=[jax.ShapeDtypeStruct((rows, width), BF16), jax.ShapeDtypeStruct((count, width), F32)],
        scratch_shapes=[pltpu.VMEM((count, msg_rows, LANES), F32), pltpu.VMEM((rows, LANES), F32)],
        compiler_params=SMALL,
        cost_estimate=pl.CostEstimate(flops=rows * width * 32, bytes_accessed=rows * width * 8, transcendentals=0),
        name="carry_part",
    )(me, *[pltpu.with_memory_space_constraint(v, pltpu.VMEM) for v in (filt, modes_t, y, gate, start, *msgs)])


def bring_kernel(later_any, src_any, out_ref, sem):
    copy = pltpu.make_async_copy(src_any, out_ref, sem)
    copy.start()
    copy.wait()


def bring(later, weight):
    return pl.pallas_call(
        bring_kernel,
        in_specs=[pl.BlockSpec(memory_space=pl.ANY), pl.BlockSpec(memory_space=pltpu.HBM)],
        out_specs=in_vmem(),
        out_shape=pltpu.VMEM(weight.shape, weight.dtype),
        scratch_shapes=[pltpu.SemaphoreType.DMA],
        compiler_params=SMALL,
        name="bring",
    )(later, pltpu.with_memory_space_constraint(weight, pltpu.HBM))


def as_row(col, width):
    rows = col.shape[0]
    r = lax.broadcasted_iota(jnp.int32, (rows, width), 0)
    c = lax.broadcasted_iota(jnp.int32, (rows, width), 1)
    return jnp.sum(jnp.where(r == c, col, 0.0), axis=0, keepdims=True)


def two_rows(row, width):
    high = rounded(row)
    both = jnp.concatenate([high, row - high], axis=0)
    return jnp.concatenate([both, jnp.zeros((2, width - row.shape[1]), F32)], axis=1)


def logit_kernel(share, given, peers, where_ref, un_ref, row_ref, id_ref, nat_ref, *rest):
    slots = where_ref.shape[0] - 1
    slot_refs, rest = rest[:given], rest[given:]
    part_ref, square_ref, score_ref = rest[:3]
    msg_refs, acc = rest[3 : 3 + peers], rest[-1]
    at = 0
    for slot_ref in slot_refs:
        for k in range(slot_ref.shape[0] // share):
            acc[pl.ds(pl.multiple_of(where_ref[at] * share, share), share), :] = slot_ref[k * share : (k + 1) * share, :]
            at += 1
    values = acc[...]
    total = values.shape[0]
    square = as_row(jnp.sum(values * values, axis=1, keepdims=True), total)
    square_ref[...] = square
    part = jnp.dot(values.astype(BF16), un_ref[...], preferred_element_type=F32)
    part_ref[...] = part
    muts = row_ref.shape[0]
    vocab = part.shape[1]
    high = part.astype(BF16)
    low = (part - high.astype(F32)).astype(BF16)
    words = lax.broadcasted_iota(jnp.int32, (total, vocab), 1)
    both = high.astype(F32) + low.astype(F32)
    native = as_row(jnp.sum(jnp.where(words == nat_ref[...], both, 0.0), axis=1, keepdims=True), total)
    spots = lax.broadcasted_iota(jnp.int32, (muts, total), 1)
    hit = spots == row_ref[...]
    onehot = hit.astype(BF16)
    picked = jnp.dot(onehot, high, preferred_element_type=F32) + jnp.dot(onehot, low, preferred_element_type=F32)
    words = lax.broadcasted_iota(jnp.int32, (muts, vocab), 1)
    chosen = jnp.sum(jnp.where(words == id_ref[...], picked, 0.0), axis=1, keepdims=True)
    base = jnp.sum(jnp.where(hit, native, 0.0), axis=1, keepdims=True)
    score = as_row(chosen - base, muts)
    score_ref[...] = score
    if peers:
        me = where_ref[slots]
        extra = jnp.concatenate(
            [two_rows(square, vocab), two_rows(score, vocab), jnp.zeros((4, vocab), F32)], axis=0
        ).astype(BF16)
        for k in range(1, peers + 1):
            their = part_ref[pl.ds(pl.multiple_of((me ^ k) * share, share), share), :]
            msg_refs[k - 1][0:share, :] = their.astype(BF16)
            msg_refs[k - 1][share : share + 8, :] = extra


def logit_part(share, where, slots, un, mut_row, mut_id, mut_nat, peers):
    wide = slots[0].shape[1]
    total = share * (where.shape[0] - 1)
    vocab = un.shape[1]
    muts = mut_row.shape[0]
    whole = pl.BlockSpec(memory_space=pltpu.VMEM)
    return pl.pallas_call(
        functools.partial(logit_kernel, share, len(slots), peers),
        in_specs=[pl.BlockSpec(memory_space=pltpu.SMEM)] + [whole] * (4 + len(slots)),
        out_specs=[whole] * (3 + peers),
        out_shape=[
            jax.ShapeDtypeStruct((total, vocab), F32),
            jax.ShapeDtypeStruct((1, total), F32),
            jax.ShapeDtypeStruct((1, muts), F32),
        ]
        + [jax.ShapeDtypeStruct((share + 8, vocab), BF16)] * peers,
        scratch_shapes=[pltpu.VMEM((total, wide), F32)],
        compiler_params=SMALL,
        name="logit_part",
    )(where, un, mut_row, mut_id, mut_nat, *slots)


def final_kernel(feats, share, where_ref, log_ref, square_ref, score_ref, nat_ref, row_ref, *rest):
    msg_refs, out_ref = rest[:-1], rest[-1]
    me, piece = where_ref[0], where_ref[1]
    vocab = log_ref.shape[1]
    total = square_ref.shape[1]
    muts = score_ref.shape[1]
    width = out_ref.shape[1]
    if msg_refs:
        logits = log_ref[pl.ds(pl.multiple_of(me * share, share), share), :]
    else:
        logits = log_ref[...]
    square, score = square_ref[...], score_ref[...]
    for msg_ref in msg_refs:
        logits = logits + msg_ref[0:share, :].astype(F32)
        extra = msg_ref[share : share + 8, :].astype(F32)
        square = square + (extra[0:1, 0:total] + extra[1:2, 0:total])
        score = score + (extra[2:3, 0:muts] + extra[3:4, 0:muts])
    scale_row = lax.rsqrt(square / feats + EPS)
    r = lax.broadcasted_iota(jnp.int32, (share, total), 0)
    c = lax.broadcasted_iota(jnp.int32, (share, total), 1)
    scale = jnp.sum(jnp.where(c == r + me * share, scale_row, 0.0), axis=1, keepdims=True)
    logits = logits * scale
    top = jnp.max(logits, axis=1, keepdims=True)
    norm = top + jnp.log(jnp.sum(jnp.exp(logits - top), axis=1, keepdims=True))
    words = lax.broadcasted_iota(jnp.int32, (share, vocab), 1)
    native = nat_ref[pl.ds(pl.multiple_of(me * share, share), share), :]
    like = jnp.sum(jnp.where(words == native, logits, 0.0), axis=1, keepdims=True) - norm
    r = lax.broadcasted_iota(jnp.int32, (share, width), 0)
    c = lax.broadcasted_iota(jnp.int32, (share, width), 1)
    out_ref[0:1, :] = jnp.sum(jnp.where(c == r + piece * share, like, 0.0), axis=0, keepdims=True)
    r = lax.broadcasted_iota(jnp.int32, (muts, total), 0)
    c = lax.broadcasted_iota(jnp.int32, (muts, total), 1)
    at_mut = jnp.sum(jnp.where(c == row_ref[...], scale_row, 0.0), axis=1, keepdims=True)
    out_ref[1:2, 0:muts] = score * as_row(at_mut, muts)


def final_part(feats, share, where, logits, squares, scores, nat, mut_row, msgs, width):
    whole = pl.BlockSpec(memory_space=pltpu.VMEM)
    return pl.pallas_call(
        functools.partial(final_kernel, float(feats), share),
        in_specs=[pl.BlockSpec(memory_space=pltpu.SMEM)] + [whole] * (5 + len(msgs)),
        out_specs=whole,
        out_shape=jax.ShapeDtypeStruct((2, width), F32),
        compiler_params=SMALL,
        name="final_part",
    )(where, logits, squares, scores, nat, mut_row, *msgs)


def total_kernel(*refs):
    like_ref, score_ref = refs[-2:]
    total = functools.reduce(lambda p, q: p + q, [ref[...] for ref in refs[:-2]])
    like_ref[...] = total[0:1, 0 : like_ref.shape[1]]
    score_ref[...] = total[1:2, 0 : score_ref.shape[1]]


def total_part(pieces, rows, muts):
    whole = pl.BlockSpec(memory_space=pltpu.VMEM)
    return pl.pallas_call(
        total_kernel,
        in_specs=[whole] * len(pieces),
        out_specs=[whole] * 2,
        out_shape=[jax.ShapeDtypeStruct((1, rows), F32), jax.ShapeDtypeStruct((1, muts), F32)],
        compiler_params=SMALL,
        name="total_part",
    )(*pieces)


def choose_kernel(place_ref, *refs):
    sources, (out_ref, sem) = refs[:-2], refs[-2:]
    for k, source in enumerate(sources):

        @pl.when(place_ref[0] == k)
        def _():
            copy = pltpu.make_async_copy(source, out_ref, sem)
            copy.start()
            copy.wait()


def choose(place, sources):
    return pl.pallas_call(
        choose_kernel,
        in_specs=[pl.BlockSpec(memory_space=pltpu.SMEM)] + [pl.BlockSpec(memory_space=pltpu.HBM)] * len(sources),
        out_specs=in_vmem(),
        out_shape=pltpu.VMEM(sources[0].shape, sources[0].dtype),
        scratch_shapes=[pltpu.SemaphoreType.DMA],
        compiler_params=SMALL,
        name="choose",
    )(place, *[pltpu.with_memory_space_constraint(v, pltpu.HBM) for v in sources])


def feature_rows(unembed, norm_gain, rows_wanted, z, m):
    count, shards = lax.axis_size("ctx"), lax.axis_size("mp")
    held = unembed.shape[0]
    scaled = (unembed.astype(F32) * norm_gain[:, None]).astype(BF16)
    if held % rows_wanted != 0:
        every = lax.all_gather(scaled, "mp", axis=0, tiled=True)
        return lax.dynamic_slice_in_dim(every, z * rows_wanted, rows_wanted, 0)
    ratio = held // rows_wanted
    piece = lax.dynamic_slice_in_dim(scaled, (z % ratio) * rows_wanted, rows_wanted, 0)
    owner = [i // ratio for i in range(count)]
    place = m ^ (z // ratio)
    value, bit, holders = piece, shards // 2, [0]
    while bit:
        pairs = [(i * shards + (owner[i] ^ h), i * shards + (owner[i] ^ h ^ bit)) for i in range(count) for h in holders]
        moved = lax.ppermute(value, ("ctx", "mp"), pairs)
        known = sum((place == h).astype(jnp.int32) for h in holders) > 0
        if bit == 1:
            return choose(jnp.where(known, 0, 1).astype(jnp.int32)[None], [value, moved])
        value = jnp.where(known, value, moved)
        holders, bit = holders + [h ^ bit for h in holders], bit // 2
    return value


def half_kernel(groups, which_ref, weight_ref, *refs):
    out_ref = refs[-1]
    half = refs[0].shape[0] // 2
    rows = pl.ds(pl.multiple_of(which_ref[0] * half, half), half)
    parts, at = [], 0
    for size in groups:
        parts.append(functools.reduce(lambda p, q: p + q, [ref[rows, :] for ref in refs[at : at + size]]))
        at += size
    block = parts[0] if len(parts) == 1 else jnp.concatenate(parts, axis=0)
    out_ref[...] = jnp.dot(block, weight_ref[...], preferred_element_type=F32).astype(out_ref.dtype)


def both_kernel(groups, which_ref, weight_ref, *refs):
    parts, (send_ref, keep_ref) = refs[:-2], refs[-2:]
    half = parts[0].shape[0] // 2
    for out_ref, which in ((send_ref, 1 - which_ref[0]), (keep_ref, which_ref[0])):
        rows = pl.ds(pl.multiple_of(which * half, half), half)
        at = 0
        for k, size in enumerate(groups):
            block = functools.reduce(lambda p, q: p + q, [ref[rows, :] for ref in parts[at : at + size]])
            at += size
            value = jnp.dot(block, weight_ref[...], preferred_element_type=F32)
            out_ref[k * half : (k + 1) * half, :] = value.astype(out_ref.dtype)


def both_parts(which, weight, blocks):
    rows = len(blocks) * (blocks[0][0].shape[0] // 2)
    flat = [part for block in blocks for part in block]
    return pl.pallas_call(
        functools.partial(both_kernel, tuple(len(block) for block in blocks)),
        in_specs=[pl.BlockSpec(memory_space=pltpu.SMEM)] + [in_vmem()] * (1 + len(flat)),
        out_specs=[in_vmem()] * 2,
        out_shape=[jax.ShapeDtypeStruct((rows, weight.shape[1]), dtype) for dtype in (BF16, F32)],
        compiler_params=SMALL,
        name="both_parts",
    )(which.astype(jnp.int32)[None], weight, *flat)


def half_part(which, weight, blocks, dtype):
    rows = len(blocks) * (blocks[0][0].shape[0] // 2)
    flat = [part for block in blocks for part in block]
    return pl.pallas_call(
        functools.partial(half_kernel, tuple(len(block) for block in blocks)),
        in_specs=[pl.BlockSpec(memory_space=pltpu.SMEM)] + [in_vmem()] * (1 + len(flat)),
        out_specs=in_vmem(),
        out_shape=jax.ShapeDtypeStruct((rows, weight.shape[1]), dtype),
        compiler_params=SMALL,
        name="half_part",
    )(which.astype(jnp.int32)[None], weight, *flat)


def project(blocks, weight, m, hurry):
    shards, count = lax.axis_size("mp"), len(blocks)
    if shards == 1:
        whole = [functools.reduce(lambda p, q: p + q, block) for block in blocks]
        return jnp.dot(jnp.concatenate(whole, axis=0), weight, preferred_element_type=F32)
    bit, value = 1, None
    while bit < shards:
        upper = (m // bit) % 2
        if value is None and not hurry:
            send, keep = both_parts(upper, weight, blocks)
        elif value is None:
            send = half_part(1 - upper, weight, blocks, BF16)
            keep = half_part(upper, weight, blocks, F32)
        else:
            half = value.shape[0] // count // 2
            pieces = value.reshape(count, 2, half, value.shape[1])
            keep = lax.dynamic_index_in_dim(pieces, upper, 1, False).reshape(count * half, value.shape[1])
            send = lax.dynamic_index_in_dim(pieces, 1 - upper, 1, False).reshape(count * half, value.shape[1])
            send = send.astype(BF16)
        got = swap(send, "mp", bit)
        value = keep + got.astype(F32)
        bit *= 2
    return value


def row_piece(m):
    shards = lax.axis_size("mp")
    piece, bit = 0, 1
    while bit < shards:
        piece = piece * 2 + (m // bit) % 2
        bit *= 2
    return piece


def body(streams, short_filter, mode_params, out_weight, norm_gain, unembed, native, mut_pos, mut_ids):
    rows, _ = streams.shape[1:]
    count, shards = lax.axis_size("ctx"), lax.axis_size("mp")
    z = lax.axis_index("ctx")
    quick = count == 4
    modes_t = jnp.swapaxes(mode_params, 1, 2)
    me = z.astype(jnp.int32)[None]
    prod, gate_stream, msg, filt, modes_t = end_part(streams, short_filter, modes_t, native)
    y, gate, start = local_part(filt, modes_t, prod, gate_stream)
    if quick:
        msgs = [msg]
        for k in range(1, count):
            msgs.append(swap(msg, "ctx", k))
        gated, nat_rows = carry_part(me, filt, modes_t, y, gate, start, msgs, False)
    else:
        every = lax.all_gather(msg, "ctx")
        gated, nat_rows = carry_part(me, filt, modes_t, y, gate, start, [every], True)
    gated, nat_rows, native, mut_pos, mut_ids, z, m, norm_gain = lax.optimization_barrier(
        (gated, nat_rows, native, mut_pos, mut_ids, z, lax.axis_index("mp"), norm_gain)
    )
    un = feature_rows(unembed, norm_gain, out_weight.shape[1], z, m)
    piece = row_piece(m)
    share = rows // shards
    nat = (nat_rows[:, :rows] * 256.0 + nat_rows[:, rows : 2 * rows]).astype(jnp.int32)
    nat_col = lax.dynamic_slice_in_dim(nat, piece * share, share, 1).reshape(count * share, 1)
    block, inner = mut_pos // rows, mut_pos % rows
    mut_row = jnp.where(inner // share == piece, block * share + inner % share, -1)[:, None]
    mut_col = mut_ids[:, None]

    if quick:
        middle = [(1, 2), (2, 1)]
        beside = swap(gated, "ctx", 1)
        mid_a = lax.ppermute(gated, "ctx", middle)
        mid_b = lax.ppermute(beside, "ctx", middle)
        far_a = swap(mid_a, "ctx", 1)
        far_b = swap(mid_b, "ctx", 1)
        mid_here = bring(gated, mid_b)
        groups = [[[gated], [beside]], [[mid_a, far_a]], [[mid_here, far_b]]]
        low = z < 2
        where = [z, z ^ 1, jnp.where(low, 2, 1), jnp.where(low, 3, 0)]
    else:
        every = lax.all_gather(gated, "ctx")
        groups = [[[every[b]]] for b in range(count)]
        where = list(range(count))
    where = jnp.stack([jnp.asarray(w, jnp.int32) for w in where + [z]])
    if quick:
        out_weight = bring(gated, out_weight)
    slots = []
    for k, blocks in enumerate(groups):
        slots.append(project(blocks, out_weight, m, k != 1))
    peers = count - 1 if quick else 0
    part, squares, scores, *msgs = logit_part(share, where, slots, un, mut_row, mut_col, nat_col, peers)
    if quick:
        for k in range(1, count):
            msgs[k - 1] = swap(msgs[k - 1], "ctx", k)
    else:
        part = lax.psum_scatter(part, "ctx", scatter_dimension=0, tiled=True)
        squares = lax.psum(squares, "ctx")
        scores = lax.psum(scores, "ctx")

    spot = jnp.stack([z, piece]).astype(jnp.int32)
    feats = norm_gain.shape[0] * shards
    span = max(rows, mut_pos.shape[0])
    result = final_part(feats, share, spot, part, squares, scores, nat_col, mut_row, msgs, span)
    pieces = [result] + [swap(result, "mp", k) for k in range(1, shards)]
    like, score = total_part(pieces, rows, mut_pos.shape[0])
    return like[0], score[0]


def solution(mesh):
    in_specs = (
        P(None, ("groups", "ctx"), "mp"),
        P(None, None, "mp"),
        P(None, "mp", None),
        P("mp", "ctx"),
        P("mp"),
        P("mp", None),
        P(("groups", "ctx")),
        P("groups"),
        P("groups"),
    )
    out_specs = (P(("groups", "ctx")), P("groups"))
    return jax.shard_map(body, mesh=mesh, in_specs=in_specs, out_specs=out_specs, check_vma=False)
```

profile of v0, /device:TPU:0, one launch (start us, length us, event | category | flops | bytes accessed | tf_op | source)
XLA Modules:
  0.0 93.4 jit_solution(18110416280007689898)
XLA Ops:
  0.6 3.2 %end_part.1 = (f32[256,1024]{1,0:T(8,128)S(1)}, bf16[256,1024]{1,0:T(8,128)(2,1)S(1)}, bf16[32,1024]{1,0:T(8,128)(2,1)S(1)}, f32[3,3,1024]{2,1,0:T(4,128)S(1)}, f32[2,8,1024]{2,1,0:T(8,128)S(1)}) custom-call(bf16[3,256,1024]{2,1,0:T(8,128)(2,1)} %x_any.1, f32[3,3,1024]{2,1,0:T(4,128)} %filt_any.1, f32[2,8,1024]{2,1,0:T(8,128)} %bitcast.40, s32[1,256]{1,0:T(1,128)} %bitcast.43), custom_call_target="tpu_custom_call" | custom-call | tf_op jit(solution)/shard_map/end_part/pallas_call | solution.py:166
  3.8 3.1 %collective-permute-start = (bf16[32,1024]{1,0:T(8,128)(2,1)S(1)}, bf16[32,1024]{1,0:T(8,128)(2,1)S(1)}, u32[]{:S(2)}, u32[]{:S(2)}) collective-permute-start(bf16[32,1024]{1,0:T(8,128)(2,1)S(1)} %get-tuple-element.36.rest_0_), channel_id=1, source_target_pairs={{0,4},{4,0},{8,12},{12,8},{1,5},{5,1},{9,13},{13,9},{2,6},{6,2},{1... | collective-permute-start | bytes 196616 | tf_op jit(solution)/shard_map/ppermute | solution.py:20
  7.0 2.6 %collective-permute-start.1 = (bf16[32,1024]{1,0:T(8,128)(2,1)S(1)}, bf16[32,1024]{1,0:T(8,128)(2,1)S(1)}, u32[]{:S(2)}, u32[]{:S(2)}) collective-permute-start(bf16[32,1024]{1,0:T(8,128)(2,1)S(1)} %get-tuple-element.36.rest_0_), channel_id=1, source_target_pairs={{0,8},{4,12},{8,0},{12,4},{1,9},{5,13},{9,1},{13,5},{2,10},{6,14},... | collective-permute-start | bytes 196616 | tf_op jit(solution)/shard_map/ppermute | solution.py:20
  9.5 3.5 %local_part.1 = (f32[256,1024]{1,0:T(8,128)S(1)}, bf16[256,1024]{1,0:T(8,128)(2,1)S(1)}, f32[64,1024]{1,0:T(8,128)S(1)}) custom-call(f32[3,3,1024]{2,1,0:T(4,128)S(1)} %get-tuple-element.29.filt_ref, f32[2,8,1024]{2,1,0:T(8,128)S(1)} %get-tuple-element.30.mode_ref, ...), custom_call_target="tpu_custom_call", output_to_operand_aliasing={{0}: (2, {}), {1}: (3, {})} | custom-call | tf_op jit(solution)/shard_map/local_part/pallas_call | solution.py:192
  13.1 1.1 %collective-permute-done.1.rest_2_ = bf16[32,1024]{1,0:T(8,128)(2,1)S(1)} collective-permute-done((bf16[32,1024]{1,0:T(8,128)(2,1)S(1)}, bf16[32,1024]{1,0:T(8,128)(2,1)S(1)}, u32[]{:S(2)}, u32[]{:S(2)}) %collective-permute-start.1) | collective-permute-done | bytes 65568 | tf_op jit(solution)/shard_map/ppermute | solution.py:20
  14.2 1.4 %collective-permute-done.2.rest_3_ = bf16[32,1024]{1,0:T(8,128)(2,1)S(1)} collective-permute-done((bf16[32,1024]{1,0:T(8,128)(2,1)S(1)}, bf16[32,1024]{1,0:T(8,128)(2,1)S(1)}, u32[]{:S(2)}, u32[]{:S(2)}) %collective-permute-start.2) | collective-permute-done | bytes 65568 | tf_op jit(solution)/shard_map/ppermute | solution.py:20
  15.6 1.5 %carry_part.1 = (bf16[256,1024]{1,0:T(8,128)(2,1)S(1)}, f32[4,1024]{1,0:T(4,128)S(1)}) custom-call(s32[1]{0:T(128)} %bitcast.where_ref, f32[3,3,1024]{2,1,0:T(4,128)S(1)} %get-tuple-element.29.filt_ref, f32[2,8,1024]{2,1,0:T(8,128)S(1)} %get-tuple-element.30.mode_ref, f32[256,1024]{1,0:T(8,128)S(1)} %get-tuple-element.33.y_ref, ...), custom_call_target="tpu_custom_call" | custom-call | flops 8388608 | bytes 2097152 | tf_op jit(solution)/shard_map/carry_part/pallas_call | solution.py:299
  17.2 1.5 %collective-permute-start.8 = (bf16[256,1024]{1,0:T(8,128)(2,1)S(1)}, bf16[256,1024]{1,0:T(8,128)(2,1)}, u32[]{:S(2)}, u32[]{:S(2)}) collective-permute-start(bf16[256,1024]{1,0:T(8,128)(2,1)S(1)} %get-tuple-element.45.later_any.refs_0_), channel_id=1, source_target_pairs={{4,8},{8,4},{5,9},{9,5},{6,10},{10,6},{7,11},{11,7},{20,24},{24,20... | collective-permute-start | bytes 1572872 | tf_op jit(solution)/shard_map/ppermute | solution.py:637
  18.7 1.6 %bring.2.weight_ref = bf16[1024,1024]{1,0:T(8,128)(2,1)S(1)} custom-call(bf16[256,1024]{1,0:T(8,128)(2,1)S(1)} %get-tuple-element.45.later_any.refs_0_, bf16[1024,1024]{1,0:T(8,128)(2,1)} %src_any.1), custom_call_target="tpu_custom_call" | custom-call | tf_op jit(solution)/shard_map/bring/pallas_call | solution.py:318
  20.4 2.5 %multiply_convert_fusion = bf16[1024,512]{1,0:T(8,128)(2,1)} fusion(bf16[1024,512]{1,0:T(8,128)(2,1)} %param.14, f32[1024]{0:T(1024)S(1)} %copy-done.3), kind=kLoop, calls=%fused_computation | loop fusion | flops 1572864 | bytes 2101248 | tf_op jit(solution)/shard_map/convert_element_type | solution.py:500
  22.9 4.5 %collective-permute-start.3 = (bf16[1024,512]{1,0:T(8,128)(2,1)}, bf16[1024,512]{1,0:T(8,128)(2,1)}, u32[]{:S(2)}, u32[]{:S(2)}) collective-permute-start(bf16[1024,512]{1,0:T(8,128)(2,1)} %multiply_convert_fusion), channel_id=1, source_target_pairs={{0,2},{5,7},{10,8},{15,13},{16,18},{21,23},{26,24},{31,29}} | collective-permute-start | bytes 3145736 | tf_op jit(solution)/shard_map/ppermute | solution.py:511
  27.4 1.9 %collective-permute-done.5.refs_1_ = bf16[256,1024]{1,0:T(8,128)(2,1)S(1)} collective-permute-done((bf16[256,1024]{1,0:T(8,128)(2,1)S(1)}, bf16[256,1024]{1,0:T(8,128)(2,1)S(1)}, u32[]{:S(2)}, u32[]{:S(2)}) %collective-permute-start.5) | collective-permute-done | bytes 524320 | tf_op jit(solution)/shard_map/ppermute | solution.py:20
  29.3 1.5 %half_part.5 = bf16[256,1024]{1,0:T(8,128)(2,1)} custom-call(s32[1]{0:T(128)} %bitcast.12.which_ref, bf16[1024,1024]{1,0:T(8,128)(2,1)S(1)} %bring.2.weight_ref, bf16[256,1024]{1,0:T(8,128)(2,1)S(1)} %get-tuple-element.45.later_any.refs_0_, bf16[256,1024]{1,0:T(8,128)(2,1)S(1)} %collective-permute-done.5.refs_1_), custom_call_target="tpu_custom_call" | custom-call | tf_op jit(solution)/shard_map/half_part/pallas_call | solution.py:561
  30.8 2.2 %collective-permute-start.9 = (bf16[256,1024]{1,0:T(8,128)(2,1)}, bf16[256,1024]{1,0:T(8,128)(2,1)}, u32[]{:S(2)}, u32[]{:S(2)}) collective-permute-start(bf16[256,1024]{1,0:T(8,128)(2,1)} %collective-permute-done.8.refs_0_), channel_id=1, source_target_pairs={{0,4},{4,0},{8,12},{12,8},{1,5},{5,1},{9,13},{13,9},{2,6},{6,2},{1... | collective-permute-start | bytes 1572872 | tf_op jit(solution)/shard_map/ppermute | solution.py:20
  33.3 1.5 %collective-permute-start.12 = (bf16[256,1024]{1,0:T(8,128)(2,1)S(1)}, bf16[256,1024]{1,0:T(8,128)(2,1)}, u32[]{:S(2)}, u32[]{:S(2)}) collective-permute-start(bf16[256,1024]{1,0:T(8,128)(2,1)S(1)} %collective-permute-done.5.refs_1_), channel_id=1, source_target_pairs={{4,8},{8,4},{5,9},{9,5},{6,10},{10,6},{7,11},{11,7},{20,24},{24,20... | collective-permute-start | bytes 1572872 | tf_op jit(solution)/shard_map/ppermute | solution.py:638
  35.8 9.6 %collective-permute-done.9.refs_1_ = bf16[256,1024]{1,0:T(8,128)(2,1)} collective-permute-done((bf16[256,1024]{1,0:T(8,128)(2,1)}, bf16[256,1024]{1,0:T(8,128)(2,1)}, u32[]{:S(2)}, u32[]{:S(2)}) %collective-permute-start.9) | collective-permute-done | bytes 524320 | tf_op jit(solution)/shard_map/ppermute | solution.py:20
  45.4 1.9 %both_parts.1 = (bf16[128,1024]{1,0:T(8,128)(2,1)S(1)}, f32[128,1024]{1,0:T(8,128)S(1)}) custom-call(s32[1]{0:T(128)} %bitcast.11.which_ref, bf16[1024,1024]{1,0:T(8,128)(2,1)S(1)} %bring.2.weight_ref, bf16[256,1024]{1,0:T(8,128)(2,1)} %collective-permute-done.8.refs_0_, bf16[256,1024]{1,0:T(8,128)(2,1)} %collective-permute-done.9.refs_1_), custom_call_target="tpu_custom_call" | custom-call | tf_op jit(solution)/shard_map/both_parts/pallas_call | solution.py:548
  47.5 1.2 %convert_add_fusion = f32[256,1024]{1,0:T(8,128)S(1)} fusion(f32[256,1024]{1,0:T(8,128)S(1)} %half_part.4, bf16[256,1024]{1,0:T(8,128)(2,1)} %collective-permute-done.6), kind=kLoop, calls=%fused_computation.1 | loop fusion | flops 524288 | bytes 2621440 | tf_op jit(solution)/shard_map/add | solution.py:591
  48.7 1.6 %collective-permute-start.7 = (bf16[128,1024]{1,0:T(8,128)(2,1)S(1)}, bf16[128,1024]{1,0:T(8,128)(2,1)S(1)}, u32[]{:S(2)}, u32[]{:S(2)}) collective-permute-start(bf16[128,1024]{1,0:T(8,128)(2,1)S(1)} %bitcast.39), channel_id=1, source_target_pairs={{0,2},{1,3},{2,0},{3,1},{4,6},{5,7},{6,4},{7,5},{8,10},{9,11},{10,... | collective-permute-start | bytes 786440 | tf_op jit(solution)/shard_map/ppermute | solution.py:20
  50.3 1.1 %bring.3.refs_0_ = bf16[256,1024]{1,0:T(8,128)(2,1)S(1)} custom-call(bf16[256,1024]{1,0:T(8,128)(2,1)S(1)} %get-tuple-element.45.later_any.refs_0_, bf16[256,1024]{1,0:T(8,128)(2,1)} %collective-permute-done.12.src_any), custom_call_target="tpu_custom_call" | custom-call | tf_op jit(solution)/shard_map/bring/pallas_call | solution.py:318
  52.6 3.1 %collective-permute-start.4 = (bf16[1024,512]{1,0:T(8,128)(2,1)S(1)}, bf16[1024,512]{1,0:T(8,128)(2,1)S(1)}, u32[]{:S(2)}, u32[]{:S(2)}) collective-permute-start(bf16[1024,512]{1,0:T(8,128)(2,1)S(1)} %broadcast_select_fusion.refs_0_), channel_id=1, source_target_pairs={{0,1},{2,3},{5,4},{7,6},{10,11},{8,9},{15,14},{13,12},{16,17},{18,... | collective-permute-start | bytes 3145736 | tf_op jit(solution)/shard_map/ppermute | solution.py:511
  55.8 9.8 %collective-permute-done.13.refs_1_ = bf16[256,1024]{1,0:T(8,128)(2,1)S(1)} collective-permute-done((bf16[256,1024]{1,0:T(8,128)(2,1)}, bf16[256,1024]{1,0:T(8,128)(2,1)S(1)}, u32[]{:S(2)}, u32[]{:S(2)}) %collective-permute-start.13) | collective-permute-done | bytes 524320 | tf_op jit(solution)/shard_map/ppermute | solution.py:20
  67.9 1.2 %collective-permute-start.15 = (bf16[64,1024]{1,0:T(8,128)(2,1)S(1)}, bf16[64,1024]{1,0:T(8,128)(2,1)S(1)}, u32[]{:S(2)}, u32[]{:S(2)}) collective-permute-start(bf16[64,1024]{1,0:T(8,128)(2,1)S(1)} %fusion.1), channel_id=1, source_target_pairs={{0,2},{1,3},{2,0},{3,1},{4,6},{5,7},{6,4},{7,5},{8,10},{9,11},{10,... | collective-permute-start | bytes 393224 | tf_op jit(solution)/shard_map/ppermute | solution.py:20
  69.1 3.6 %collective-permute-done.11 = bf16[64,1024]{1,0:T(8,128)(2,1)S(1)} collective-permute-done((bf16[64,1024]{1,0:T(8,128)(2,1)S(1)}, bf16[64,1024]{1,0:T(8,128)(2,1)S(1)}, u32[]{:S(2)}, u32[]{:S(2)}) %collective-permute-start.11) | collective-permute-done | bytes 131104 | tf_op jit(solution)/shard_map/ppermute | solution.py:20
  72.7 2.3 %collective-permute-done.15 = bf16[64,1024]{1,0:T(8,128)(2,1)S(1)} collective-permute-done((bf16[64,1024]{1,0:T(8,128)(2,1)S(1)}, bf16[64,1024]{1,0:T(8,128)(2,1)S(1)}, u32[]{:S(2)}, u32[]{:S(2)}) %collective-permute-start.15) | collective-permute-done | bytes 131104 | tf_op jit(solution)/shard_map/ppermute | solution.py:20
  76.0 1.2 %choose.1.un_ref = bf16[1024,512]{1,0:T(8,128)(2,1)S(1)} custom-call(s32[1]{0:T(128)} %bitcast.8.place_ref, bf16[1024,512]{1,0:T(8,128)(2,1)} %copy-done.1, bf16[1024,512]{1,0:T(8,128)(2,1)} %copy-done.2), custom_call_target="tpu_custom_call" | custom-call | tf_op jit(solution)/shard_map/choose/pallas_call | solution.py:486
  77.3 1.6 %logit_part.1 = (f32[256,512]{1,0:T(8,128)S(1)}, f32[1,256]{1,0:T(1,128)S(1)}, f32[1,256]{1,0:T(1,128)S(1)}, bf16[72,512]{1,0:T(8,128)(2,1)S(1)}, bf16[72,512]{1...) custom-call(s32[5]{0:T(128)S(1)} %stack.29.where_ref, bf16[1024,512]{1,0:T(8,128)(2,1)S(1)} %choose.1.un_ref, ...), custom_call_target="tpu_custom_call" | custom-call | tf_op jit(solution)/shard_map/logit_part/pallas_call | solution.py:391
  79.6 1.9 %collective-permute-start.17 = (bf16[72,512]{1,0:T(8,128)(2,1)S(1)}, bf16[72,512]{1,0:T(8,128)(2,1)S(1)}, u32[]{:S(2)}, u32[]{:S(2)}) collective-permute-start(bf16[72,512]{1,0:T(8,128)(2,1)S(1)} %get-tuple-element.52), channel_id=1, source_target_pairs={{0,8},{4,12},{8,0},{12,4},{1,9},{5,13},{9,1},{13,5},{2,10},{6,14},... | collective-permute-start | bytes 221192 | tf_op jit(solution)/shard_map/ppermute | solution.py:20
  81.6 1.7 %collective-permute-start.18 = (bf16[72,512]{1,0:T(8,128)(2,1)S(1)}, bf16[72,512]{1,0:T(8,128)(2,1)S(1)}, u32[]{:S(2)}, u32[]{:S(2)}) collective-permute-start(bf16[72,512]{1,0:T(8,128)(2,1)S(1)} %get-tuple-element.53), channel_id=1, source_target_pairs={{0,12},{4,8},{8,4},{12,0},{1,13},{5,9},{9,5},{13,1},{2,14},{6,10},... | collective-permute-start | bytes 221192 | tf_op jit(solution)/shard_map/ppermute | solution.py:20
  84.0 4.2 %collective-permute-done.17.rest_1_ = bf16[72,512]{1,0:T(8,128)(2,1)S(1)} collective-permute-done((bf16[72,512]{1,0:T(8,128)(2,1)S(1)}, bf16[72,512]{1,0:T(8,128)(2,1)S(1)}, u32[]{:S(2)}, u32[]{:S(2)}) %collective-permute-start.17) | collective-permute-done | bytes 73760 | tf_op jit(solution)/shard_map/ppermute | solution.py:20
  89.8 1.2 %collective-permute-start.21 = (f32[2,256]{1,0:T(2,128)S(1)}, f32[2,256]{1,0:T(2,128)S(1)}, u32[]{:S(2)}, u32[]{:S(2)}) collective-permute-start(f32[2,256]{1,0:T(2,128)S(1)} %final_part.1.refs_0_), channel_id=1, source_target_pairs={{0,3},{1,2},{2,1},{3,0},{4,7},{5,6},{6,5},{7,4},{8,11},{9,10},{10,... | collective-permute-start | bytes 6152 | tf_op jit(solution)/shard_map/ppermute | solution.py:20
  91.0 1.8 %collective-permute-done.20.refs_2_ = f32[2,256]{1,0:T(2,128)S(1)} collective-permute-done((f32[2,256]{1,0:T(2,128)S(1)}, f32[2,256]{1,0:T(2,128)S(1)}, u32[]{:S(2)}, u32[]{:S(2)}) %collective-permute-start.20) | collective-permute-done | bytes 2080 | tf_op jit(solution)/shard_map/ppermute | solution.py:20
  (58 shorter events, 9.6 us)
Async XLA Ops:
  3.8 9.2 %collective-permute-start = (bf16[32,1024]{1,0:T(8,128)(2,1)S(1)}, bf16[32,1024]{1,0:T(8,128)(2,1)S(1)}, u32[]{:S(2)}, u32[]{:S(2)}) collective-permute-start(bf16[32,1024]{1,0:T(8,128)(2,1)S(1)} %get-tuple-element.36.rest_0_), channel_id=1, source_target_pairs={{0,4},{4,0},{8,12},{12,8},{1,5},{5,1},{9,13},{13,9},{2,6},{6,2},{1... | collective-permute-start | bytes 196616 | tf_op jit(solution)/shard_map/ppermute | solution.py:20
  7.0 7.3 %collective-permute-start.1 = (bf16[32,1024]{1,0:T(8,128)(2,1)S(1)}, bf16[32,1024]{1,0:T(8,128)(2,1)S(1)}, u32[]{:S(2)}, u32[]{:S(2)}) collective-permute-start(bf16[32,1024]{1,0:T(8,128)(2,1)S(1)} %get-tuple-element.36.rest_0_), channel_id=1, source_target_pairs={{0,8},{4,12},{8,0},{12,4},{1,9},{5,13},{9,1},{13,5},{2,10},{6,14},... | collective-permute-start | bytes 196616 | tf_op jit(solution)/shard_map/ppermute | solution.py:20
  9.5 6.1 %collective-permute-start.2 = (bf16[32,1024]{1,0:T(8,128)(2,1)S(1)}, bf16[32,1024]{1,0:T(8,128)(2,1)S(1)}, u32[]{:S(2)}, u32[]{:S(2)}) collective-permute-start(bf16[32,1024]{1,0:T(8,128)(2,1)S(1)} %get-tuple-element.36.rest_0_), channel_id=1, source_target_pairs={{0,12},{4,8},{8,4},{12,0},{1,13},{5,9},{9,5},{13,1},{2,14},{6,10},... | collective-permute-start | bytes 196616 | tf_op jit(solution)/shard_map/ppermute | solution.py:20
  17.2 12.1 %collective-permute-start.5 = (bf16[256,1024]{1,0:T(8,128)(2,1)S(1)}, bf16[256,1024]{1,0:T(8,128)(2,1)S(1)}, u32[]{:S(2)}, u32[]{:S(2)}) collective-permute-start(bf16[256,1024]{1,0:T(8,128)(2,1)S(1)} %get-tuple-element.45.later_any.refs_0_), channel_id=1, source_target_pairs={{0,4},{4,0},{8,12},{12,8},{1,5},{5,1},{9,13},{13,9},{2,6},{6,2},{1... | collective-permute-start | bytes 1572872 | tf_op jit(solution)/shard_map/ppermute | solution.py:20
  17.2 13.5 %collective-permute-start.8 = (bf16[256,1024]{1,0:T(8,128)(2,1)S(1)}, bf16[256,1024]{1,0:T(8,128)(2,1)}, u32[]{:S(2)}, u32[]{:S(2)}) collective-permute-start(bf16[256,1024]{1,0:T(8,128)(2,1)S(1)} %get-tuple-element.45.later_any.refs_0_), channel_id=1, source_target_pairs={{4,8},{8,4},{5,9},{9,5},{6,10},{10,6},{7,11},{11,7},{20,24},{24,20... | collective-permute-start | bytes 1572872 | tf_op jit(solution)/shard_map/ppermute | solution.py:637
  18.7 1.6 %copy-start.3 = (f32[1024]{0:T(1024)S(1)}, f32[1024]{0:T(1024)}, u32[]{:S(2)}) copy-start(f32[1024]{0:T(1024)} %param.13) | copy-start | bytes 12292
  22.9 11.9 %copy-start.5 = (s32[256]{0:T(256)S(1)}, s32[256]{0:T(256)}, u32[]{:S(2)}) copy-start(s32[256]{0:T(256)} %param.16) | copy-start | bytes 3076
  22.9 12.0 %copy-start.4 = (s32[256]{0:T(256)S(1)}, s32[256]{0:T(256)}, u32[]{:S(2)}) copy-start(s32[256]{0:T(256)} %param.17) | copy-start | bytes 3076
  22.9 29.3 %collective-permute-start.3 = (bf16[1024,512]{1,0:T(8,128)(2,1)}, bf16[1024,512]{1,0:T(8,128)(2,1)}, u32[]{:S(2)}, u32[]{:S(2)}) collective-permute-start(bf16[1024,512]{1,0:T(8,128)(2,1)} %multiply_convert_fusion), channel_id=1, source_target_pairs={{0,2},{5,7},{10,8},{15,13},{16,18},{21,23},{26,24},{31,29}} | collective-permute-start | bytes 3145736 | tf_op jit(solution)/shard_map/ppermute | solution.py:511
  30.8 16.7 %collective-permute-start.6 = (bf16[256,1024]{1,0:T(8,128)(2,1)}, bf16[256,1024]{1,0:T(8,128)(2,1)}, u32[]{:S(2)}, u32[]{:S(2)}) collective-permute-start(bf16[256,1024]{1,0:T(8,128)(2,1)} %half_part.5), channel_id=1, source_target_pairs={{0,1},{1,0},{2,3},{3,2},{4,5},{5,4},{6,7},{7,6},{8,9},{9,8},{10,11... | collective-permute-start | bytes 1572872 | tf_op jit(solution)/shard_map/ppermute | solution.py:20
  30.8 14.7 %collective-permute-start.9 = (bf16[256,1024]{1,0:T(8,128)(2,1)}, bf16[256,1024]{1,0:T(8,128)(2,1)}, u32[]{:S(2)}, u32[]{:S(2)}) collective-permute-start(bf16[256,1024]{1,0:T(8,128)(2,1)} %collective-permute-done.8.refs_0_), channel_id=1, source_target_pairs={{0,4},{4,0},{8,12},{12,8},{1,5},{5,1},{9,13},{13,9},{2,6},{6,2},{1... | collective-permute-start | bytes 1572872 | tf_op jit(solution)/shard_map/ppermute | solution.py:20
  33.3 17.1 %collective-permute-start.12 = (bf16[256,1024]{1,0:T(8,128)(2,1)S(1)}, bf16[256,1024]{1,0:T(8,128)(2,1)}, u32[]{:S(2)}, u32[]{:S(2)}) collective-permute-start(bf16[256,1024]{1,0:T(8,128)(2,1)S(1)} %collective-permute-done.5.refs_1_), channel_id=1, source_target_pairs={{4,8},{8,4},{5,9},{9,5},{6,10},{10,6},{7,11},{11,7},{20,24},{24,20... | collective-permute-start | bytes 1572872 | tf_op jit(solution)/shard_map/ppermute | solution.py:638
  47.4 8.4 %collective-permute-start.10 = (bf16[128,1024]{1,0:T(8,128)(2,1)S(1)}, bf16[128,1024]{1,0:T(8,128)(2,1)S(1)}, u32[]{:S(2)}, u32[]{:S(2)}) collective-permute-start(bf16[128,1024]{1,0:T(8,128)(2,1)S(1)} %get-tuple-element.47), channel_id=1, source_target_pairs={{0,1},{1,0},{2,3},{3,2},{4,5},{5,4},{6,7},{7,6},{8,9},{9,8},{10,11... | collective-permute-start | bytes 786440 | tf_op jit(solution)/shard_map/ppermute | solution.py:20
  48.7 3.5 %copy-start = (bf16[1024,512]{1,0:T(8,128)(2,1)S(1)}, bf16[1024,512]{1,0:T(8,128)(2,1)}, u32[]{:S(2)}) copy-start(bf16[1024,512]{1,0:T(8,128)(2,1)} %param.14) | copy-start | bytes 3145732
  48.7 18.1 %collective-permute-start.7 = (bf16[128,1024]{1,0:T(8,128)(2,1)S(1)}, bf16[128,1024]{1,0:T(8,128)(2,1)S(1)}, u32[]{:S(2)}, u32[]{:S(2)}) collective-permute-start(bf16[128,1024]{1,0:T(8,128)(2,1)S(1)} %bitcast.39), channel_id=1, source_target_pairs={{0,2},{1,3},{2,0},{3,1},{4,6},{5,7},{6,4},{7,5},{8,10},{9,11},{10,... | collective-permute-start | bytes 786440 | tf_op jit(solution)/shard_map/ppermute | solution.py:20
  51.4 14.3 %collective-permute-start.13 = (bf16[256,1024]{1,0:T(8,128)(2,1)}, bf16[256,1024]{1,0:T(8,128)(2,1)S(1)}, u32[]{:S(2)}, u32[]{:S(2)}) collective-permute-start(bf16[256,1024]{1,0:T(8,128)(2,1)} %collective-permute-done.12.src_any), channel_id=1, source_target_pairs={{0,4},{4,0},{8,12},{12,8},{1,5},{5,1},{9,13},{13,9},{2,6},{6,2},{1... | collective-permute-start | bytes 1572872 | tf_op jit(solution)/shard_map/ppermute | solution.py:20
  52.6 13.5 %copy-start.1 = (bf16[1024,512]{1,0:T(8,128)(2,1)}, bf16[1024,512]{1,0:T(8,128)(2,1)S(1)}, u32[]{:S(2)}) copy-start(bf16[1024,512]{1,0:T(8,128)(2,1)S(1)} %broadcast_select_fusion.refs_0_) | copy-start | bytes 3145732
  52.6 22.4 %collective-permute-start.4 = (bf16[1024,512]{1,0:T(8,128)(2,1)S(1)}, bf16[1024,512]{1,0:T(8,128)(2,1)S(1)}, u32[]{:S(2)}, u32[]{:S(2)}) collective-permute-start(bf16[1024,512]{1,0:T(8,128)(2,1)S(1)} %broadcast_select_fusion.refs_0_), channel_id=1, source_target_pairs={{0,1},{2,3},{5,4},{7,6},{10,11},{8,9},{15,14},{13,12},{16,17},{18,... | collective-permute-start | bytes 3145736 | tf_op jit(solution)/shard_map/ppermute | solution.py:511
  66.1 1.6 %collective-permute-start.14 = (bf16[128,1024]{1,0:T(8,128)(2,1)S(1)}, bf16[128,1024]{1,0:T(8,128)(2,1)S(1)}, u32[]{:S(2)}, u32[]{:S(2)}) collective-permute-start(bf16[128,1024]{1,0:T(8,128)(2,1)S(1)} %half_part.7), channel_id=1, source_target_pairs={{0,1},{1,0},{2,3},{3,2},{4,5},{5,4},{6,7},{7,6},{8,9},{9,8},{10,11... | collective-permute-start | bytes 786440 | tf_op jit(solution)/shard_map/ppermute | solution.py:20
  66.3 6.4 %collective-permute-start.11 = (bf16[64,1024]{1,0:T(8,128)(2,1)S(1)}, bf16[64,1024]{1,0:T(8,128)(2,1)S(1)}, u32[]{:S(2)}, u32[]{:S(2)}) collective-permute-start(bf16[64,1024]{1,0:T(8,128)(2,1)S(1)} %fusion), channel_id=1, source_target_pairs={{0,2},{1,3},{2,0},{3,1},{4,6},{5,7},{6,4},{7,5},{8,10},{9,11},{10,... | collective-permute-start | bytes 393224 | tf_op jit(solution)/shard_map/ppermute | solution.py:20
  67.9 7.2 %collective-permute-start.15 = (bf16[64,1024]{1,0:T(8,128)(2,1)S(1)}, bf16[64,1024]{1,0:T(8,128)(2,1)S(1)}, u32[]{:S(2)}, u32[]{:S(2)}) collective-permute-start(bf16[64,1024]{1,0:T(8,128)(2,1)S(1)} %fusion.1), channel_id=1, source_target_pairs={{0,2},{1,3},{2,0},{3,1},{4,6},{5,7},{6,4},{7,5},{8,10},{9,11},{10,... | collective-permute-start | bytes 393224 | tf_op jit(solution)/shard_map/ppermute | solution.py:20
  75.1 1.0 %copy-start.2 = (bf16[1024,512]{1,0:T(8,128)(2,1)}, bf16[1024,512]{1,0:T(8,128)(2,1)S(1)}, u32[]{:S(2)}) copy-start(bf16[1024,512]{1,0:T(8,128)(2,1)S(1)} %collective-permute-done.4.refs_1_) | copy-start | bytes 3145732
  78.8 5.2 %collective-permute-start.16 = (bf16[72,512]{1,0:T(8,128)(2,1)S(1)}, bf16[72,512]{1,0:T(8,128)(2,1)S(1)}, u32[]{:S(2)}, u32[]{:S(2)}) collective-permute-start(bf16[72,512]{1,0:T(8,128)(2,1)S(1)} %get-tuple-element.51), channel_id=1, source_target_pairs={{0,4},{4,0},{8,12},{12,8},{1,5},{5,1},{9,13},{13,9},{2,6},{6,2},{1... | collective-permute-start | bytes 221192 | tf_op jit(solution)/shard_map/ppermute | solution.py:20
  79.6 8.6 %collective-permute-start.17 = (bf16[72,512]{1,0:T(8,128)(2,1)S(1)}, bf16[72,512]{1,0:T(8,128)(2,1)S(1)}, u32[]{:S(2)}, u32[]{:S(2)}) collective-permute-start(bf16[72,512]{1,0:T(8,128)(2,1)S(1)} %get-tuple-element.52), channel_id=1, source_target_pairs={{0,8},{4,12},{8,0},{12,4},{1,9},{5,13},{9,1},{13,5},{2,10},{6,14},... | collective-permute-start | bytes 221192 | tf_op jit(solution)/shard_map/ppermute | solution.py:20
  81.6 6.6 %collective-permute-start.18 = (bf16[72,512]{1,0:T(8,128)(2,1)S(1)}, bf16[72,512]{1,0:T(8,128)(2,1)S(1)}, u32[]{:S(2)}, u32[]{:S(2)}) collective-permute-start(bf16[72,512]{1,0:T(8,128)(2,1)S(1)} %get-tuple-element.53), channel_id=1, source_target_pairs={{0,12},{4,8},{8,4},{12,0},{1,13},{5,9},{9,5},{13,1},{2,14},{6,10},... | collective-permute-start | bytes 221192 | tf_op jit(solution)/shard_map/ppermute | solution.py:20
  89.1 1.9 %collective-permute-start.19 = (f32[2,256]{1,0:T(2,128)S(1)}, f32[2,256]{1,0:T(2,128)S(1)}, u32[]{:S(2)}, u32[]{:S(2)}) collective-permute-start(f32[2,256]{1,0:T(2,128)S(1)} %final_part.1.refs_0_), channel_id=1, source_target_pairs={{0,1},{1,0},{2,3},{3,2},{4,5},{5,4},{6,7},{7,6},{8,9},{9,8},{10,11... | collective-permute-start | bytes 6152 | tf_op jit(solution)/shard_map/ppermute | solution.py:20
  89.1 3.7 %collective-permute-start.20 = (f32[2,256]{1,0:T(2,128)S(1)}, f32[2,256]{1,0:T(2,128)S(1)}, u32[]{:S(2)}, u32[]{:S(2)}) collective-permute-start(f32[2,256]{1,0:T(2,128)S(1)} %final_part.1.refs_0_), channel_id=1, source_target_pairs={{0,2},{1,3},{2,0},{3,1},{4,6},{5,7},{6,4},{7,5},{8,10},{9,11},{10,... | collective-permute-start | bytes 6152 | tf_op jit(solution)/shard_map/ppermute | solution.py:20
  89.8 3.0 %collective-permute-start.21 = (f32[2,256]{1,0:T(2,128)S(1)}, f32[2,256]{1,0:T(2,128)S(1)}, u32[]{:S(2)}, u32[]{:S(2)}) collective-permute-start(f32[2,256]{1,0:T(2,128)S(1)} %final_part.1.refs_0_), channel_id=1, source_target_pairs={{0,3},{1,2},{2,1},{3,0},{4,7},{5,6},{6,5},{7,4},{8,11},{9,10},{10,... | collective-permute-start | bytes 6152 | tf_op jit(solution)/shard_map/ppermute | solution.py:20
where the time goes:
time: 93.8 us; the launch traced here: 93.4 us
  waiting for transfers between devices  36.9 us (39%)
  starting transfers between devices  29.2 us (31%)
  Pallas kernels  20.2 us (22%)
  other arithmetic  4.53 us (5%)
  local copies, waits for them, and re-layouts  1.6 us (2%)
  between operations  1.02 us (1%)
    ppermute x18, waiting for transfers between devices, swap(): return lax.ppermute(value, axis, [(i, i ^ bit) for i in range(count)])  36.8 us
    ppermute x18, starting transfers between devices, swap(): return lax.ppermute(value, axis, [(i, i ^ bit) for i in range(count)])  18.7 us
    ppermute x2, starting transfers between devices, feature_rows(): moved = lax.ppermute(value, ('ctx', 'mp'), pairs)  7.61 us
    pallas_call x1, Pallas kernels, local_part(): pl.pallas_call(functools.partial(local_kernel, rows // SUBS, modes), in_s...  3.51 us
    pallas_call x1, Pallas kernels, end_part(): pl.pallas_call(functools.partial(end_kernel, steps, modes), in_specs=[pl....  3.2 us
    pallas_call x4, Pallas kernels, half_part(): pl.pallas_call(functools.partial(half_kernel, tuple((len(block) for block...  3.11 us
    pallas_call x2, Pallas kernels, bring(): pl.pallas_call(bring_kernel, in_specs=[pl.BlockSpec(memory_space=pl.ANY),...  2.66 us
    convert_element_type x1, other arithmetic, feature_rows(): scaled = (unembed.astype(F32) * norm_gain[:, None]).astype(BF16)  2.5 us
  transfers between devices with their start and end apart: 22, of which 11 were waited for; matrix products, arithmetic and copies ran while one was open for 6% of the time, Pallas kernels for 12%

commit v1 on v0

--- a/solution.py
+++ b/solution.py
@@ -339,69 +339,108 @@
     return jnp.concatenate([both, jnp.zeros((2, width - row.shape[1]), F32)], axis=1)
 
 
-def logit_kernel(share, given, peers, where_ref, un_ref, row_ref, id_ref, nat_ref, *rest):
-    slots = where_ref.shape[0] - 1
-    slot_refs, rest = rest[:given], rest[given:]
-    part_ref, square_ref, score_ref = rest[:3]
-    msg_refs, acc = rest[3 : 3 + peers], rest[-1]
+def partial_logits(values, un_ref, rows, id_ref, native_ids):
+    total, muts = values.shape[0], rows.shape[0]
+    square = jnp.sum(values * values, axis=1, keepdims=True)
+    part = jnp.dot(values.astype(BF16), un_ref[...], preferred_element_type=F32)
+    high = part.astype(BF16)
+    low = (part - high.astype(F32)).astype(BF16)
+    words = lax.broadcasted_iota(jnp.int32, part.shape, 1)
+    both = high.astype(F32) + low.astype(F32)
+    native = as_row(jnp.sum(jnp.where(words == native_ids, both, 0.0), axis=1, keepdims=True), total)
+    hit = lax.broadcasted_iota(jnp.int32, (muts, total), 1) == rows
+    onehot = hit.astype(BF16)
+    picked = jnp.dot(onehot, high, preferred_element_type=F32) + jnp.dot(onehot, low, preferred_element_type=F32)
+    words = lax.broadcasted_iota(jnp.int32, (muts, part.shape[1]), 1)
+    chosen = jnp.sum(jnp.where(words == id_ref[...], picked, 0.0), axis=1, keepdims=True)
+    base = jnp.sum(jnp.where(hit, native, 0.0), axis=1, keepdims=True)
+    return part, square, as_row(chosen - base, muts)
+
+
+def logit_kernel(share, count, where_ref, row_ref, id_ref, nat_ref, *rest):
+    sources, slot_refs = rest[:count], rest[count:-6]
+    part_ref, square_ref, score_ref, un_ref, acc, sem = rest[-6:]
+    for k, source in enumerate(sources):
+
+        @pl.when(where_ref[where_ref.shape[0] - 1] == k)
+        def _():
+            pltpu.make_async_copy(source, un_ref, sem).start()
+
+    if sum(ref.shape[0] for ref in slot_refs) < acc.shape[0]:
+        acc[...] = jnp.zeros_like(acc)
     at = 0
     for slot_ref in slot_refs:
         for k in range(slot_ref.shape[0] // share):
             acc[pl.ds(pl.multiple_of(where_ref[at] * share, share), share), :] = slot_ref[k * share : (k + 1) * share, :]
             at += 1
-    values = acc[...]
-    total = values.shape[0]
-    square = as_row(jnp.sum(values * values, axis=1, keepdims=True), total)
-    square_ref[...] = square
-    part = jnp.dot(values.astype(BF16), un_ref[...], preferred_element_type=F32)
+    for k, source in enumerate(sources):
+
+        @pl.when(where_ref[where_ref.shape[0] - 1] == k)
+        def _():
+            pltpu.make_async_copy(source, un_ref, sem).wait()
+
+    part, square, score = partial_logits(acc[...], un_ref, row_ref[...], id_ref, nat_ref[...])
     part_ref[...] = part
-    muts = row_ref.shape[0]
-    vocab = part.shape[1]
-    high = part.astype(BF16)
-    low = (part - high.astype(F32)).astype(BF16)
-    words = lax.broadcasted_iota(jnp.int32, (total, vocab), 1)
-    both = high.astype(F32) + low.astype(F32)
-    native = as_row(jnp.sum(jnp.where(words == nat_ref[...], both, 0.0), axis=1, keepdims=True), total)
-    spots = lax.broadcasted_iota(jnp.int32, (muts, total), 1)
-    hit = spots == row_ref[...]
-    onehot = hit.astype(BF16)
-    picked = jnp.dot(onehot, high, preferred_element_type=F32) + jnp.dot(onehot, low, preferred_element_type=F32)
-    words = lax.broadcasted_iota(jnp.int32, (muts, vocab), 1)
-    chosen = jnp.sum(jnp.where(words == id_ref[...], picked, 0.0), axis=1, keepdims=True)
-    base = jnp.sum(jnp.where(hit, native, 0.0), axis=1, keepdims=True)
-    score = as_row(chosen - base, muts)
+    square_ref[...] = as_row(square, square.shape[0])
     score_ref[...] = score
-    if peers:
-        me = where_ref[slots]
-        extra = jnp.concatenate(
-            [two_rows(square, vocab), two_rows(score, vocab), jnp.zeros((4, vocab), F32)], axis=0
-        ).astype(BF16)
-        for k in range(1, peers + 1):
-            their = part_ref[pl.ds(pl.multiple_of((me ^ k) * share, share), share), :]
-            msg_refs[k - 1][0:share, :] = their.astype(BF16)
-            msg_refs[k - 1][share : share + 8, :] = extra
-
-
-def logit_part(share, where, slots, un, mut_row, mut_id, mut_nat, peers):
-    wide = slots[0].shape[1]
-    total = share * (where.shape[0] - 1)
-    vocab = un.shape[1]
-    muts = mut_row.shape[0]
-    whole = pl.BlockSpec(memory_space=pltpu.VMEM)
-    return pl.pallas_call(
-        functools.partial(logit_kernel, share, len(slots), peers),
-        in_specs=[pl.BlockSpec(memory_space=pltpu.SMEM)] + [whole] * (4 + len(slots)),
-        out_specs=[whole] * (3 + peers),
+
+
+def logit_part(share, where, slots, sources, mut_row, mut_id, nat_col):
+    wide, (_, vocab) = slots[0].shape[1], sources[0].shape
+    total, muts = nat_col.shape[0], mut_row.shape[0]
+    return pl.pallas_call(
+        functools.partial(logit_kernel, share, len(sources)),
+        in_specs=[pl.BlockSpec(memory_space=pltpu.SMEM)]
+        + [in_vmem()] * 3
+        + [pl.BlockSpec(memory_space=pl.ANY)] * len(sources)
+        + [in_vmem()] * len(slots),
+        out_specs=[in_vmem()] * 4,
         out_shape=[
             jax.ShapeDtypeStruct((total, vocab), F32),
             jax.ShapeDtypeStruct((1, total), F32),
             jax.ShapeDtypeStruct((1, muts), F32),
-        ]
+            pltpu.VMEM(sources[0].shape, BF16),
+        ],
+        scratch_shapes=[pltpu.VMEM((total, wide), F32), pltpu.SemaphoreType.DMA],
+        compiler_params=SMALL,
+        name="logit_part",
+    )(where, mut_row, mut_id, nat_col, *sources, *slots)
+
+
+def message_kernel(share, peers, where_ref, un_ref, row_ref, id_ref, nat_ref, last_ref, part_ref, square_in, score_in, *rest):
+    square_ref, score_ref, msg_refs = rest[0], rest[1], rest[2:]
+    slots = where_ref.shape[0] - 2
+    spot, me = where_ref[slots - 1], where_ref[slots]
+    first = pl.multiple_of(spot * share, share)
+    native_ids = nat_ref[pl.ds(first, share), :]
+    part, square, score = partial_logits(last_ref[...], un_ref, row_ref[...] - first, id_ref, native_ids)
+    total, vocab = square_in.shape[1], part.shape[1]
+    r = lax.broadcasted_iota(jnp.int32, (share, total), 0)
+    c = lax.broadcasted_iota(jnp.int32, (share, total), 1)
+    square = square_in[...] + jnp.sum(jnp.where(c == r + first, square, 0.0), axis=0, keepdims=True)
+    score = score_in[...] + score
+    square_ref[...] = square
+    score_ref[...] = score
+    extra = jnp.concatenate(
+        [two_rows(square, vocab), two_rows(score, vocab), jnp.zeros((4, vocab), F32)], axis=0
+    ).astype(BF16)
+    for k in range(1, peers + 1):
+        their = part_ref[pl.ds(pl.multiple_of((me ^ k) * share, share), share), :]
+        msg_refs[k - 1][0:share, :] = jnp.where((me ^ k) == spot, part, their).astype(BF16)
+        msg_refs[k - 1][share : share + 8, :] = extra
+
+
+def message_part(share, where, last, un, mut_row, mut_id, nat_col, part, squares, scores, peers):
+    vocab = un.shape[1]
+    return pl.pallas_call(
+        functools.partial(message_kernel, share, peers),
+        in_specs=[pl.BlockSpec(memory_space=pltpu.SMEM)] + [in_vmem()] * 8,
+        out_specs=[in_vmem()] * (2 + peers),
+        out_shape=[jax.ShapeDtypeStruct(squares.shape, F32), jax.ShapeDtypeStruct(scores.shape, F32)]
         + [jax.ShapeDtypeStruct((share + 8, vocab), BF16)] * peers,
-        scratch_shapes=[pltpu.VMEM((total, wide), F32)],
-        compiler_params=SMALL,
-        name="logit_part",
-    )(where, un, mut_row, mut_id, mut_nat, *slots)
+        compiler_params=SMALL,
+        name="message_part",
+    )(where, un, mut_row, mut_id, nat_col, last, part, squares, scores)
 
 
 def final_kernel(feats, share, where_ref, log_ref, square_ref, score_ref, nat_ref, row_ref, *rest):
@@ -471,36 +510,13 @@
     )(*pieces)
 
 
-def choose_kernel(place_ref, *refs):
-    sources, (out_ref, sem) = refs[:-2], refs[-2:]
-    for k, source in enumerate(sources):
-
-        @pl.when(place_ref[0] == k)
-        def _():
-            copy = pltpu.make_async_copy(source, out_ref, sem)
-            copy.start()
-            copy.wait()
-
-
-def choose(place, sources):
-    return pl.pallas_call(
-        choose_kernel,
-        in_specs=[pl.BlockSpec(memory_space=pltpu.SMEM)] + [pl.BlockSpec(memory_space=pltpu.HBM)] * len(sources),
-        out_specs=in_vmem(),
-        out_shape=pltpu.VMEM(sources[0].shape, sources[0].dtype),
-        scratch_shapes=[pltpu.SemaphoreType.DMA],
-        compiler_params=SMALL,
-        name="choose",
-    )(place, *[pltpu.with_memory_space_constraint(v, pltpu.HBM) for v in sources])
-
-
 def feature_rows(unembed, norm_gain, rows_wanted, z, m):
     count, shards = lax.axis_size("ctx"), lax.axis_size("mp")
     held = unembed.shape[0]
     scaled = (unembed.astype(F32) * norm_gain[:, None]).astype(BF16)
     if held % rows_wanted != 0:
         every = lax.all_gather(scaled, "mp", axis=0, tiled=True)
-        return lax.dynamic_slice_in_dim(every, z * rows_wanted, rows_wanted, 0)
+        return [lax.dynamic_slice_in_dim(every, z * rows_wanted, rows_wanted, 0)], 0
     ratio = held // rows_wanted
     piece = lax.dynamic_slice_in_dim(scaled, (z % ratio) * rows_wanted, rows_wanted, 0)
     owner = [i // ratio for i in range(count)]
@@ -511,10 +527,10 @@
         moved = lax.ppermute(value, ("ctx", "mp"), pairs)
         known = sum((place == h).astype(jnp.int32) for h in holders) > 0
         if bit == 1:
-            return choose(jnp.where(known, 0, 1).astype(jnp.int32)[None], [value, moved])
+            return [value, moved], jnp.where(known, 0, 1)
         value = jnp.where(known, value, moved)
         holders, bit = holders + [h ^ bit for h in holders], bit // 2
-    return value
+    return [value], 0
 
 
 def half_kernel(groups, which_ref, weight_ref, *refs):
@@ -622,7 +638,7 @@
     gated, nat_rows, native, mut_pos, mut_ids, z, m, norm_gain = lax.optimization_barrier(
         (gated, nat_rows, native, mut_pos, mut_ids, z, lax.axis_index("mp"), norm_gain)
     )
-    un = feature_rows(unembed, norm_gain, out_weight.shape[1], z, m)
+    sources, chosen = feature_rows(unembed, norm_gain, out_weight.shape[1], z, m)
     piece = row_piece(m)
     share = rows // shards
     nat = (nat_rows[:, :rows] * 256.0 + nat_rows[:, rows : 2 * rows]).astype(jnp.int32)
@@ -646,14 +662,19 @@
         every = lax.all_gather(gated, "ctx")
         groups = [[[every[b]]] for b in range(count)]
         where = list(range(count))
-    where = jnp.stack([jnp.asarray(w, jnp.int32) for w in where + [z]])
+    where = jnp.stack([jnp.asarray(w, jnp.int32) for w in where + [z, chosen]])
     if quick:
         out_weight = bring(gated, out_weight)
     slots = []
     for k, blocks in enumerate(groups):
         slots.append(project(blocks, out_weight, m, k != 1))
-    peers = count - 1 if quick else 0
-    part, squares, scores, *msgs = logit_part(share, where, slots, un, mut_row, mut_col, nat_col, peers)
+    early = slots[:-1] if quick else slots
+    part, squares, scores, un = logit_part(share, where, early, sources, mut_row, mut_col, nat_col)
+    msgs = []
+    if quick:
+        squares, scores, *msgs = message_part(
+            share, where, slots[-1], un, mut_row, mut_col, nat_col, part, squares, scores, count - 1
+        )
     if quick:
         for k in range(1, count):
             msgs[k - 1] = swap(msgs[k - 1], "ctx", k)

time: 93.8 us -> 93 us (level)
  local copies, waits for them, and re-layouts: 1.6 us -> 0.64 us
    unnamed x12 -> x8, local copies, waits for them, and re-layouts: 0.98 us -> 0.02 us
where the time goes in v1:
time: 93 us; the launch traced here: 92.6 us
  waiting for transfers between devices  36.9 us (40%)
  starting transfers between devices  29.2 us (31%)
  Pallas kernels  20.4 us (22%)
  other arithmetic  4.49 us (5%)
  between operations  0.99 us (1%)
    ppermute x18, waiting for transfers between devices, swap(): return lax.ppermute(value, axis, [(i, i ^ bit) for i in range(count)])  36.9 us
    ppermute x18, starting transfers between devices, swap(): return lax.ppermute(value, axis, [(i, i ^ bit) for i in range(count)])  18.7 us
    ppermute x2, starting transfers between devices, feature_rows(): moved = lax.ppermute(value, ('ctx', 'mp'), pairs)  7.61 us
    pallas_call x1, Pallas kernels, local_part(): pl.pallas_call(functools.partial(local_kernel, rows // SUBS, modes), in_s...  3.51 us
    pallas_call x1, Pallas kernels, end_part(): pl.pallas_call(functools.partial(end_kernel, steps, modes), in_specs=[pl....  3.2 us
    pallas_call x4, Pallas kernels, half_part(): pl.pallas_call(functools.partial(half_kernel, tuple((len(block) for block...  3.14 us
    pallas_call x2, Pallas kernels, bring(): pl.pallas_call(bring_kernel, in_specs=[pl.BlockSpec(memory_space=pl.ANY),...  2.66 us
    convert_element_type x1, other arithmetic, feature_rows(): scaled = (unembed.astype(F32) * norm_gain[:, None]).astype(BF16)  2.49 us
  transfers between devices with their start and end apart: 22, of which 11 were waited for; matrix products, arithmetic and copies ran while one was open for 6% of the time, Pallas kernels for 12%

profile of v1, /device:TPU:0, one launch (start us, length us, event | category | flops | bytes accessed | tf_op | source)
XLA Modules:
  0.0 92.6 jit_solution(9911244616980778746)
XLA Ops:
  0.6 3.2 %end_part.1 = (f32[256,1024]{1,0:T(8,128)S(1)}, bf16[256,1024]{1,0:T(8,128)(2,1)S(1)}, bf16[32,1024]{1,0:T(8,128)(2,1)S(1)}, f32[3,3,1024]{2,1,0:T(4,128)S(1)}, f32[2,8,1024]{2,1,0:T(8,128)S(1)}) custom-call(bf16[3,256,1024]{2,1,0:T(8,128)(2,1)} %x_any.1, f32[3,3,1024]{2,1,0:T(4,128)} %filt_any.1, f32[2,8,1024]{2,1,0:T(8,128)} %bitcast.40, s32[1,256]{1,0:T(1,128)} %bitcast.43), custom_call_target="tpu_custom_call" | custom-call | tf_op jit(solution)/shard_map/end_part/pallas_call | solution.py:166
  3.8 3.1 %collective-permute-start = (bf16[32,1024]{1,0:T(8,128)(2,1)S(1)}, bf16[32,1024]{1,0:T(8,128)(2,1)S(1)}, u32[]{:S(2)}, u32[]{:S(2)}) collective-permute-start(bf16[32,1024]{1,0:T(8,128)(2,1)S(1)} %get-tuple-element.39.rest_0_), channel_id=1, source_target_pairs={{0,4},{4,0},{8,12},{12,8},{1,5},{5,1},{9,13},{13,9},{2,6},{6,2},{1... | collective-permute-start | bytes 196616 | tf_op jit(solution)/shard_map/ppermute | solution.py:20
  7.0 2.6 %collective-permute-start.1 = (bf16[32,1024]{1,0:T(8,128)(2,1)S(1)}, bf16[32,1024]{1,0:T(8,128)(2,1)S(1)}, u32[]{:S(2)}, u32[]{:S(2)}) collective-permute-start(bf16[32,1024]{1,0:T(8,128)(2,1)S(1)} %get-tuple-element.39.rest_0_), channel_id=1, source_target_pairs={{0,8},{4,12},{8,0},{12,4},{1,9},{5,13},{9,1},{13,5},{2,10},{6,14},... | collective-permute-start | bytes 196616 | tf_op jit(solution)/shard_map/ppermute | solution.py:20
  9.5 3.5 %local_part.1 = (f32[256,1024]{1,0:T(8,128)S(1)}, bf16[256,1024]{1,0:T(8,128)(2,1)S(1)}, f32[64,1024]{1,0:T(8,128)S(1)}) custom-call(f32[3,3,1024]{2,1,0:T(4,128)S(1)} %get-tuple-element.32.filt_ref, f32[2,8,1024]{2,1,0:T(8,128)S(1)} %get-tuple-element.33.mode_ref, ...), custom_call_target="tpu_custom_call", output_to_operand_aliasing={{0}: (2, {}), {1}: (3, {})} | custom-call | tf_op jit(solution)/shard_map/local_part/pallas_call | solution.py:192
  13.1 1.1 %collective-permute-done.1.rest_2_ = bf16[32,1024]{1,0:T(8,128)(2,1)S(1)} collective-permute-done((bf16[32,1024]{1,0:T(8,128)(2,1)S(1)}, bf16[32,1024]{1,0:T(8,128)(2,1)S(1)}, u32[]{:S(2)}, u32[]{:S(2)}) %collective-permute-start.1) | collective-permute-done | bytes 65568 | tf_op jit(solution)/shard_map/ppermute | solution.py:20
  14.2 1.4 %collective-permute-done.2.rest_3_ = bf16[32,1024]{1,0:T(8,128)(2,1)S(1)} collective-permute-done((bf16[32,1024]{1,0:T(8,128)(2,1)S(1)}, bf16[32,1024]{1,0:T(8,128)(2,1)S(1)}, u32[]{:S(2)}, u32[]{:S(2)}) %collective-permute-start.2) | collective-permute-done | bytes 65568 | tf_op jit(solution)/shard_map/ppermute | solution.py:20
  15.6 1.5 %carry_part.1 = (bf16[256,1024]{1,0:T(8,128)(2,1)S(1)}, f32[4,1024]{1,0:T(4,128)S(1)}) custom-call(s32[1]{0:T(128)} %bitcast.where_ref, f32[3,3,1024]{2,1,0:T(4,128)S(1)} %get-tuple-element.32.filt_ref, f32[2,8,1024]{2,1,0:T(8,128)S(1)} %get-tuple-element.33.mode_ref, f32[256,1024]{1,0:T(8,128)S(1)} %get-tuple-element.36.y_ref, ...), custom_call_target="tpu_custom_call" | custom-call | flops 8388608 | bytes 2097152 | tf_op jit(solution)/shard_map/carry_part/pallas_call | solution.py:299
  17.2 1.5 %collective-permute-start.8 = (bf16[256,1024]{1,0:T(8,128)(2,1)S(1)}, bf16[256,1024]{1,0:T(8,128)(2,1)}, u32[]{:S(2)}, u32[]{:S(2)}) collective-permute-start(bf16[256,1024]{1,0:T(8,128)(2,1)S(1)} %get-tuple-element.48.later_any.refs_0_), channel_id=1, source_target_pairs={{4,8},{8,4},{5,9},{9,5},{6,10},{10,6},{7,11},{11,7},{20,24},{24,20... | collective-permute-start | bytes 1572872 | tf_op jit(solution)/shard_map/ppermute | solution.py:653
  18.7 1.6 %bring.2.weight_ref = bf16[1024,1024]{1,0:T(8,128)(2,1)S(1)} custom-call(bf16[256,1024]{1,0:T(8,128)(2,1)S(1)} %get-tuple-element.48.later_any.refs_0_, bf16[1024,1024]{1,0:T(8,128)(2,1)} %src_any.1), custom_call_target="tpu_custom_call" | custom-call | tf_op jit(solution)/shard_map/bring/pallas_call | solution.py:318
  20.4 2.5 %multiply_convert_fusion = bf16[1024,512]{1,0:T(8,128)(2,1)} fusion(bf16[1024,512]{1,0:T(8,128)(2,1)} %param.14, f32[1024]{0:T(1024)S(1)} %copy-done.1), kind=kLoop, calls=%fused_computation | loop fusion | flops 1572864 | bytes 2101248 | tf_op jit(solution)/shard_map/convert_element_type | solution.py:516
  22.9 4.5 %collective-permute-start.3 = (bf16[1024,512]{1,0:T(8,128)(2,1)}, bf16[1024,512]{1,0:T(8,128)(2,1)}, u32[]{:S(2)}, u32[]{:S(2)}) collective-permute-start(bf16[1024,512]{1,0:T(8,128)(2,1)} %multiply_convert_fusion), channel_id=1, source_target_pairs={{0,2},{5,7},{10,8},{15,13},{16,18},{21,23},{26,24},{31,29}} | collective-permute-start | bytes 3145736 | tf_op jit(solution)/shard_map/ppermute | solution.py:527
  27.4 1.9 %collective-permute-done.5.refs_1_ = bf16[256,1024]{1,0:T(8,128)(2,1)S(1)} collective-permute-done((bf16[256,1024]{1,0:T(8,128)(2,1)S(1)}, bf16[256,1024]{1,0:T(8,128)(2,1)S(1)}, u32[]{:S(2)}, u32[]{:S(2)}) %collective-permute-start.5) | collective-permute-done | bytes 524320 | tf_op jit(solution)/shard_map/ppermute | solution.py:20
  29.3 1.5 %half_part.5 = bf16[256,1024]{1,0:T(8,128)(2,1)} custom-call(s32[1]{0:T(128)} %bitcast.12.which_ref, bf16[1024,1024]{1,0:T(8,128)(2,1)S(1)} %bring.2.weight_ref, bf16[256,1024]{1,0:T(8,128)(2,1)S(1)} %get-tuple-element.48.later_any.refs_0_, bf16[256,1024]{1,0:T(8,128)(2,1)S(1)} %collective-permute-done.5.refs_1_), custom_call_target="tpu_custom_call" | custom-call | tf_op jit(solution)/shard_map/half_part/pallas_call | solution.py:577
  30.8 2.2 %collective-permute-start.9 = (bf16[256,1024]{1,0:T(8,128)(2,1)}, bf16[256,1024]{1,0:T(8,128)(2,1)}, u32[]{:S(2)}, u32[]{:S(2)}) collective-permute-start(bf16[256,1024]{1,0:T(8,128)(2,1)} %collective-permute-done.8.refs_0_), channel_id=1, source_target_pairs={{0,4},{4,0},{8,12},{12,8},{1,5},{5,1},{9,13},{13,9},{2,6},{6,2},{1... | collective-permute-start | bytes 1572872 | tf_op jit(solution)/shard_map/ppermute | solution.py:20
  33.2 1.5 %collective-permute-start.12 = (bf16[256,1024]{1,0:T(8,128)(2,1)S(1)}, bf16[256,1024]{1,0:T(8,128)(2,1)}, u32[]{:S(2)}, u32[]{:S(2)}) collective-permute-start(bf16[256,1024]{1,0:T(8,128)(2,1)S(1)} %collective-permute-done.5.refs_1_), channel_id=1, source_target_pairs={{4,8},{8,4},{5,9},{9,5},{6,10},{10,6},{7,11},{11,7},{20,24},{24,20... | collective-permute-start | bytes 1572872 | tf_op jit(solution)/shard_map/ppermute | solution.py:654
  35.8 9.6 %collective-permute-done.9.refs_1_ = bf16[256,1024]{1,0:T(8,128)(2,1)} collective-permute-done((bf16[256,1024]{1,0:T(8,128)(2,1)}, bf16[256,1024]{1,0:T(8,128)(2,1)}, u32[]{:S(2)}, u32[]{:S(2)}) %collective-permute-start.9) | collective-permute-done | bytes 524320 | tf_op jit(solution)/shard_map/ppermute | solution.py:20
  45.4 1.9 %both_parts.1 = (bf16[128,1024]{1,0:T(8,128)(2,1)S(1)}, f32[128,1024]{1,0:T(8,128)S(1)}) custom-call(s32[1]{0:T(128)} %bitcast.11.which_ref, bf16[1024,1024]{1,0:T(8,128)(2,1)S(1)} %bring.2.weight_ref, bf16[256,1024]{1,0:T(8,128)(2,1)} %collective-permute-done.8.refs_0_, bf16[256,1024]{1,0:T(8,128)(2,1)} %collective-permute-done.9.refs_1_), custom_call_target="tpu_custom_call" | custom-call | tf_op jit(solution)/shard_map/both_parts/pallas_call | solution.py:564
  47.5 1.2 %convert_add_fusion = f32[256,1024]{1,0:T(8,128)S(1)} fusion(f32[256,1024]{1,0:T(8,128)S(1)} %half_part.4, bf16[256,1024]{1,0:T(8,128)(2,1)} %collective-permute-done.6), kind=kLoop, calls=%fused_computation.1 | loop fusion | flops 524288 | bytes 2621440 | tf_op jit(solution)/shard_map/add | solution.py:607
  48.7 1.6 %collective-permute-start.7 = (bf16[128,1024]{1,0:T(8,128)(2,1)S(1)}, bf16[128,1024]{1,0:T(8,128)(2,1)S(1)}, u32[]{:S(2)}, u32[]{:S(2)}) collective-permute-start(bf16[128,1024]{1,0:T(8,128)(2,1)S(1)} %bitcast.39), channel_id=1, source_target_pairs={{0,2},{1,3},{2,0},{3,1},{4,6},{5,7},{6,4},{7,5},{8,10},{9,11},{10,... | collective-permute-start | bytes 786440 | tf_op jit(solution)/shard_map/ppermute | solution.py:20
  50.3 1.1 %bring.3.refs_0_ = bf16[256,1024]{1,0:T(8,128)(2,1)S(1)} custom-call(bf16[256,1024]{1,0:T(8,128)(2,1)S(1)} %get-tuple-element.48.later_any.refs_0_, bf16[256,1024]{1,0:T(8,128)(2,1)} %collective-permute-done.12.src_any), custom_call_target="tpu_custom_call" | custom-call | tf_op jit(solution)/shard_map/bring/pallas_call | solution.py:318
  52.6 3.1 %collective-permute-start.4 = (bf16[1024,512]{1,0:T(8,128)(2,1)S(1)}, bf16[1024,512]{1,0:T(8,128)(2,1)S(1)}, u32[]{:S(2)}, u32[]{:S(2)}) collective-permute-start(bf16[1024,512]{1,0:T(8,128)(2,1)S(1)} %broadcast_select_fusion.rest_0_), channel_id=1, source_target_pairs={{0,1},{2,3},{5,4},{7,6},{10,11},{8,9},{15,14},{13,12},{16,17},{18,... | collective-permute-start | bytes 3145736 | tf_op jit(solution)/shard_map/ppermute | solution.py:527
  55.8 9.9 %collective-permute-done.13.refs_1_ = bf16[256,1024]{1,0:T(8,128)(2,1)S(1)} collective-permute-done((bf16[256,1024]{1,0:T(8,128)(2,1)}, bf16[256,1024]{1,0:T(8,128)(2,1)S(1)}, u32[]{:S(2)}, u32[]{:S(2)}) %collective-permute-start.13) | collective-permute-done | bytes 524320 | tf_op jit(solution)/shard_map/ppermute | solution.py:20
  67.8 1.2 %collective-permute-start.15 = (bf16[64,1024]{1,0:T(8,128)(2,1)S(1)}, bf16[64,1024]{1,0:T(8,128)(2,1)S(1)}, u32[]{:S(2)}, u32[]{:S(2)}) collective-permute-start(bf16[64,1024]{1,0:T(8,128)(2,1)S(1)} %fusion.1), channel_id=1, source_target_pairs={{0,2},{1,3},{2,0},{3,1},{4,6},{5,7},{6,4},{7,5},{8,10},{9,11},{10,... | collective-permute-start | bytes 393224 | tf_op jit(solution)/shard_map/ppermute | solution.py:20
  69.1 3.6 %collective-permute-done.11 = bf16[64,1024]{1,0:T(8,128)(2,1)S(1)} collective-permute-done((bf16[64,1024]{1,0:T(8,128)(2,1)S(1)}, bf16[64,1024]{1,0:T(8,128)(2,1)S(1)}, u32[]{:S(2)}, u32[]{:S(2)}) %collective-permute-start.11) | collective-permute-done | bytes 131104 | tf_op jit(solution)/shard_map/ppermute | solution.py:20
  72.7 2.3 %collective-permute-done.15 = bf16[64,1024]{1,0:T(8,128)(2,1)S(1)} collective-permute-done((bf16[64,1024]{1,0:T(8,128)(2,1)S(1)}, bf16[64,1024]{1,0:T(8,128)(2,1)S(1)}, u32[]{:S(2)}, u32[]{:S(2)}) %collective-permute-start.15) | collective-permute-done | bytes 131104 | tf_op jit(solution)/shard_map/ppermute | solution.py:20
  75.0 1.7 %logit_part.1 = (f32[256,512]{1,0:T(8,128)S(1)}, f32[1,256]{1,0:T(1,128)S(1)}, f32[1,256]{1,0:T(1,128)S(1)}, bf16[1024,512]{1,0:T(8,128)(2,1)S(1)}) custom-call(s32[6]{0:T(128)S(1)} %stack.33.where_ref, s32[256,1]{1,0:T(8,128)S(1)} %copy.17.row_ref, s32[256,1]{1,0:T(8,128)S(1)} %copy.18.id_ref, s32[256,1]{1,0:T(8,128)S(1)} %reshape.45.nat_ref, ...), custom_call_target="tpu_custom_call" | custom-call | tf_op jit(solution)/shard_map/logit_part/pallas_call | solution.py:391
  76.8 1.3 %message_part.1 = (f32[1,256]{1,0:T(1,128)S(1)}, f32[1,256]{1,0:T(1,128)S(1)}, bf16[72,512]{1,0:T(8,128)(2,1)S(1)}, bf16[72,512]{1,0:T(8,128)(2,1)S(1)}, bf16[72,512]{1,0:T(8,128)(2,1)S(1)}) custom-call(s32[6]{0:T(128)S(1)} %stack.33.where_ref, bf16[1024,512]{1,0:T(8,128)(2,1)S(1)} %get-tuple-element.52.un_ref, s32[256,1]{1,0:T(8,128)S(1)} %copy.17.row_ref, ...), custom_call_target="tpu_custom_call" | custom-call | tf_op jit(solution)/shard_map/message_part/pallas_call | solution.py:435
  78.8 1.9 %collective-permute-start.17 = (bf16[72,512]{1,0:T(8,128)(2,1)S(1)}, bf16[72,512]{1,0:T(8,128)(2,1)S(1)}, u32[]{:S(2)}, u32[]{:S(2)}) collective-permute-start(bf16[72,512]{1,0:T(8,128)(2,1)S(1)} %get-tuple-element.58), channel_id=1, source_target_pairs={{0,8},{4,12},{8,0},{12,4},{1,9},{5,13},{9,1},{13,5},{2,10},{6,14},... | collective-permute-start | bytes 221192 | tf_op jit(solution)/shard_map/ppermute | solution.py:20
  80.7 1.7 %collective-permute-start.18 = (bf16[72,512]{1,0:T(8,128)(2,1)S(1)}, bf16[72,512]{1,0:T(8,128)(2,1)S(1)}, u32[]{:S(2)}, u32[]{:S(2)}) collective-permute-start(bf16[72,512]{1,0:T(8,128)(2,1)S(1)} %get-tuple-element.59), channel_id=1, source_target_pairs={{0,12},{4,8},{8,4},{12,0},{1,13},{5,9},{9,5},{13,1},{2,14},{6,10},... | collective-permute-start | bytes 221192 | tf_op jit(solution)/shard_map/ppermute | solution.py:20
  83.2 4.2 %collective-permute-done.17.rest_1_ = bf16[72,512]{1,0:T(8,128)(2,1)S(1)} collective-permute-done((bf16[72,512]{1,0:T(8,128)(2,1)S(1)}, bf16[72,512]{1,0:T(8,128)(2,1)S(1)}, u32[]{:S(2)}, u32[]{:S(2)}) %collective-permute-start.17) | collective-permute-done | bytes 73760 | tf_op jit(solution)/shard_map/ppermute | solution.py:20
  88.9 1.2 %collective-permute-start.21 = (f32[2,256]{1,0:T(2,128)S(1)}, f32[2,256]{1,0:T(2,128)S(1)}, u32[]{:S(2)}, u32[]{:S(2)}) collective-permute-start(f32[2,256]{1,0:T(2,128)S(1)} %final_part.1.refs_0_), channel_id=1, source_target_pairs={{0,3},{1,2},{2,1},{3,0},{4,7},{5,6},{6,5},{7,4},{8,11},{9,10},{10,... | collective-permute-start | bytes 6152 | tf_op jit(solution)/shard_map/ppermute | solution.py:20
  90.2 1.8 %collective-permute-done.20.refs_2_ = f32[2,256]{1,0:T(2,128)S(1)} collective-permute-done((f32[2,256]{1,0:T(2,128)S(1)}, f32[2,256]{1,0:T(2,128)S(1)}, u32[]{:S(2)}, u32[]{:S(2)}) %collective-permute-start.20) | collective-permute-done | bytes 2080 | tf_op jit(solution)/shard_map/ppermute | solution.py:20
  (54 shorter events, 8.6 us)
Async XLA Ops:
  3.8 9.2 %collective-permute-start = (bf16[32,1024]{1,0:T(8,128)(2,1)S(1)}, bf16[32,1024]{1,0:T(8,128)(2,1)S(1)}, u32[]{:S(2)}, u32[]{:S(2)}) collective-permute-start(bf16[32,1024]{1,0:T(8,128)(2,1)S(1)} %get-tuple-element.39.rest_0_), channel_id=1, source_target_pairs={{0,4},{4,0},{8,12},{12,8},{1,5},{5,1},{9,13},{13,9},{2,6},{6,2},{1... | collective-permute-start | bytes 196616 | tf_op jit(solution)/shard_map/ppermute | solution.py:20
  7.0 7.3 %collective-permute-start.1 = (bf16[32,1024]{1,0:T(8,128)(2,1)S(1)}, bf16[32,1024]{1,0:T(8,128)(2,1)S(1)}, u32[]{:S(2)}, u32[]{:S(2)}) collective-permute-start(bf16[32,1024]{1,0:T(8,128)(2,1)S(1)} %get-tuple-element.39.rest_0_), channel_id=1, source_target_pairs={{0,8},{4,12},{8,0},{12,4},{1,9},{5,13},{9,1},{13,5},{2,10},{6,14},... | collective-permute-start | bytes 196616 | tf_op jit(solution)/shard_map/ppermute | solution.py:20
  9.5 6.1 %collective-permute-start.2 = (bf16[32,1024]{1,0:T(8,128)(2,1)S(1)}, bf16[32,1024]{1,0:T(8,128)(2,1)S(1)}, u32[]{:S(2)}, u32[]{:S(2)}) collective-permute-start(bf16[32,1024]{1,0:T(8,128)(2,1)S(1)} %get-tuple-element.39.rest_0_), channel_id=1, source_target_pairs={{0,12},{4,8},{8,4},{12,0},{1,13},{5,9},{9,5},{13,1},{2,14},{6,10},... | collective-permute-start | bytes 196616 | tf_op jit(solution)/shard_map/ppermute | solution.py:20
  17.2 12.1 %collective-permute-start.5 = (bf16[256,1024]{1,0:T(8,128)(2,1)S(1)}, bf16[256,1024]{1,0:T(8,128)(2,1)S(1)}, u32[]{:S(2)}, u32[]{:S(2)}) collective-permute-start(bf16[256,1024]{1,0:T(8,128)(2,1)S(1)} %get-tuple-element.48.later_any.refs_0_), channel_id=1, source_target_pairs={{0,4},{4,0},{8,12},{12,8},{1,5},{5,1},{9,13},{13,9},{2,6},{6,2},{1... | collective-permute-start | bytes 1572872 | tf_op jit(solution)/shard_map/ppermute | solution.py:20
  17.2 13.5 %collective-permute-start.8 = (bf16[256,1024]{1,0:T(8,128)(2,1)S(1)}, bf16[256,1024]{1,0:T(8,128)(2,1)}, u32[]{:S(2)}, u32[]{:S(2)}) collective-permute-start(bf16[256,1024]{1,0:T(8,128)(2,1)S(1)} %get-tuple-element.48.later_any.refs_0_), channel_id=1, source_target_pairs={{4,8},{8,4},{5,9},{9,5},{6,10},{10,6},{7,11},{11,7},{20,24},{24,20... | collective-permute-start | bytes 1572872 | tf_op jit(solution)/shard_map/ppermute | solution.py:653
  18.7 1.6 %copy-start.1 = (f32[1024]{0:T(1024)S(1)}, f32[1024]{0:T(1024)}, u32[]{:S(2)}) copy-start(f32[1024]{0:T(1024)} %param.13) | copy-start | bytes 12292
  22.9 11.8 %copy-start.3 = (s32[256]{0:T(256)S(1)}, s32[256]{0:T(256)}, u32[]{:S(2)}) copy-start(s32[256]{0:T(256)} %param.16) | copy-start | bytes 3076
  22.9 12.0 %copy-start.2 = (s32[256]{0:T(256)S(1)}, s32[256]{0:T(256)}, u32[]{:S(2)}) copy-start(s32[256]{0:T(256)} %param.17) | copy-start | bytes 3076
  22.9 29.3 %collective-permute-start.3 = (bf16[1024,512]{1,0:T(8,128)(2,1)}, bf16[1024,512]{1,0:T(8,128)(2,1)}, u32[]{:S(2)}, u32[]{:S(2)}) collective-permute-start(bf16[1024,512]{1,0:T(8,128)(2,1)} %multiply_convert_fusion), channel_id=1, source_target_pairs={{0,2},{5,7},{10,8},{15,13},{16,18},{21,23},{26,24},{31,29}} | collective-permute-start | bytes 3145736 | tf_op jit(solution)/shard_map/ppermute | solution.py:527
  30.8 16.7 %collective-permute-start.6 = (bf16[256,1024]{1,0:T(8,128)(2,1)}, bf16[256,1024]{1,0:T(8,128)(2,1)}, u32[]{:S(2)}, u32[]{:S(2)}) collective-permute-start(bf16[256,1024]{1,0:T(8,128)(2,1)} %half_part.5), channel_id=1, source_target_pairs={{0,1},{1,0},{2,3},{3,2},{4,5},{5,4},{6,7},{7,6},{8,9},{9,8},{10,11... | collective-permute-start | bytes 1572872 | tf_op jit(solution)/shard_map/ppermute | solution.py:20
  30.8 14.7 %collective-permute-start.9 = (bf16[256,1024]{1,0:T(8,128)(2,1)}, bf16[256,1024]{1,0:T(8,128)(2,1)}, u32[]{:S(2)}, u32[]{:S(2)}) collective-permute-start(bf16[256,1024]{1,0:T(8,128)(2,1)} %collective-permute-done.8.refs_0_), channel_id=1, source_target_pairs={{0,4},{4,0},{8,12},{12,8},{1,5},{5,1},{9,13},{13,9},{2,6},{6,2},{1... | collective-permute-start | bytes 1572872 | tf_op jit(solution)/shard_map/ppermute | solution.py:20
  33.2 17.0 %collective-permute-start.12 = (bf16[256,1024]{1,0:T(8,128)(2,1)S(1)}, bf16[256,1024]{1,0:T(8,128)(2,1)}, u32[]{:S(2)}, u32[]{:S(2)}) collective-permute-start(bf16[256,1024]{1,0:T(8,128)(2,1)S(1)} %collective-permute-done.5.refs_1_), channel_id=1, source_target_pairs={{4,8},{8,4},{5,9},{9,5},{6,10},{10,6},{7,11},{11,7},{20,24},{24,20... | collective-permute-start | bytes 1572872 | tf_op jit(solution)/shard_map/ppermute | solution.py:654
  47.4 8.4 %collective-permute-start.10 = (bf16[128,1024]{1,0:T(8,128)(2,1)S(1)}, bf16[128,1024]{1,0:T(8,128)(2,1)S(1)}, u32[]{:S(2)}, u32[]{:S(2)}) collective-permute-start(bf16[128,1024]{1,0:T(8,128)(2,1)S(1)} %get-tuple-element.50), channel_id=1, source_target_pairs={{0,1},{1,0},{2,3},{3,2},{4,5},{5,4},{6,7},{7,6},{8,9},{9,8},{10,11... | collective-permute-start | bytes 786440 | tf_op jit(solution)/shard_map/ppermute | solution.py:20
  48.7 3.5 %copy-start = (bf16[1024,512]{1,0:T(8,128)(2,1)S(1)}, bf16[1024,512]{1,0:T(8,128)(2,1)}, u32[]{:S(2)}) copy-start(bf16[1024,512]{1,0:T(8,128)(2,1)} %param.14) | copy-start | bytes 3145732
  48.7 18.1 %collective-permute-start.7 = (bf16[128,1024]{1,0:T(8,128)(2,1)S(1)}, bf16[128,1024]{1,0:T(8,128)(2,1)S(1)}, u32[]{:S(2)}, u32[]{:S(2)}) collective-permute-start(bf16[128,1024]{1,0:T(8,128)(2,1)S(1)} %bitcast.39), channel_id=1, source_target_pairs={{0,2},{1,3},{2,0},{3,1},{4,6},{5,7},{6,4},{7,5},{8,10},{9,11},{10,... | collective-permute-start | bytes 786440 | tf_op jit(solution)/shard_map/ppermute | solution.py:20
  51.3 14.3 %collective-permute-start.13 = (bf16[256,1024]{1,0:T(8,128)(2,1)}, bf16[256,1024]{1,0:T(8,128)(2,1)S(1)}, u32[]{:S(2)}, u32[]{:S(2)}) collective-permute-start(bf16[256,1024]{1,0:T(8,128)(2,1)} %collective-permute-done.12.src_any), channel_id=1, source_target_pairs={{0,4},{4,0},{8,12},{12,8},{1,5},{5,1},{9,13},{13,9},{2,6},{6,2},{1... | collective-permute-start | bytes 1572872 | tf_op jit(solution)/shard_map/ppermute | solution.py:20
  52.6 22.4 %collective-permute-start.4 = (bf16[1024,512]{1,0:T(8,128)(2,1)S(1)}, bf16[1024,512]{1,0:T(8,128)(2,1)S(1)}, u32[]{:S(2)}, u32[]{:S(2)}) collective-permute-start(bf16[1024,512]{1,0:T(8,128)(2,1)S(1)} %broadcast_select_fusion.rest_0_), channel_id=1, source_target_pairs={{0,1},{2,3},{5,4},{7,6},{10,11},{8,9},{15,14},{13,12},{16,17},{18,... | collective-permute-start | bytes 3145736 | tf_op jit(solution)/shard_map/ppermute | solution.py:527
  66.1 1.6 %collective-permute-start.14 = (bf16[128,1024]{1,0:T(8,128)(2,1)S(1)}, bf16[128,1024]{1,0:T(8,128)(2,1)S(1)}, u32[]{:S(2)}, u32[]{:S(2)}) collective-permute-start(bf16[128,1024]{1,0:T(8,128)(2,1)S(1)} %half_part.7), channel_id=1, source_target_pairs={{0,1},{1,0},{2,3},{3,2},{4,5},{5,4},{6,7},{7,6},{8,9},{9,8},{10,11... | collective-permute-start | bytes 786440 | tf_op jit(solution)/shard_map/ppermute | solution.py:20
  66.2 6.4 %collective-permute-start.11 = (bf16[64,1024]{1,0:T(8,128)(2,1)S(1)}, bf16[64,1024]{1,0:T(8,128)(2,1)S(1)}, u32[]{:S(2)}, u32[]{:S(2)}) collective-permute-start(bf16[64,1024]{1,0:T(8,128)(2,1)S(1)} %fusion), channel_id=1, source_target_pairs={{0,2},{1,3},{2,0},{3,1},{4,6},{5,7},{6,4},{7,5},{8,10},{9,11},{10,... | collective-permute-start | bytes 393224 | tf_op jit(solution)/shard_map/ppermute | solution.py:20
  67.8 7.2 %collective-permute-start.15 = (bf16[64,1024]{1,0:T(8,128)(2,1)S(1)}, bf16[64,1024]{1,0:T(8,128)(2,1)S(1)}, u32[]{:S(2)}, u32[]{:S(2)}) collective-permute-start(bf16[64,1024]{1,0:T(8,128)(2,1)S(1)} %fusion.1), channel_id=1, source_target_pairs={{0,2},{1,3},{2,0},{3,1},{4,6},{5,7},{6,4},{7,5},{8,10},{9,11},{10,... | collective-permute-start | bytes 393224 | tf_op jit(solution)/shard_map/ppermute | solution.py:20
  78.0 5.2 %collective-permute-start.16 = (bf16[72,512]{1,0:T(8,128)(2,1)S(1)}, bf16[72,512]{1,0:T(8,128)(2,1)S(1)}, u32[]{:S(2)}, u32[]{:S(2)}) collective-permute-start(bf16[72,512]{1,0:T(8,128)(2,1)S(1)} %get-tuple-element.57), channel_id=1, source_target_pairs={{0,4},{4,0},{8,12},{12,8},{1,5},{5,1},{9,13},{13,9},{2,6},{6,2},{1... | collective-permute-start | bytes 221192 | tf_op jit(solution)/shard_map/ppermute | solution.py:20
  78.8 8.6 %collective-permute-start.17 = (bf16[72,512]{1,0:T(8,128)(2,1)S(1)}, bf16[72,512]{1,0:T(8,128)(2,1)S(1)}, u32[]{:S(2)}, u32[]{:S(2)}) collective-permute-start(bf16[72,512]{1,0:T(8,128)(2,1)S(1)} %get-tuple-element.58), channel_id=1, source_target_pairs={{0,8},{4,12},{8,0},{12,4},{1,9},{5,13},{9,1},{13,5},{2,10},{6,14},... | collective-permute-start | bytes 221192 | tf_op jit(solution)/shard_map/ppermute | solution.py:20
  80.7 6.7 %collective-permute-start.18 = (bf16[72,512]{1,0:T(8,128)(2,1)S(1)}, bf16[72,512]{1,0:T(8,128)(2,1)S(1)}, u32[]{:S(2)}, u32[]{:S(2)}) collective-permute-start(bf16[72,512]{1,0:T(8,128)(2,1)S(1)} %get-tuple-element.59), channel_id=1, source_target_pairs={{0,12},{4,8},{8,4},{12,0},{1,13},{5,9},{9,5},{13,1},{2,14},{6,10},... | collective-permute-start | bytes 221192 | tf_op jit(solution)/shard_map/ppermute | solution.py:20
  88.3 1.9 %collective-permute-start.19 = (f32[2,256]{1,0:T(2,128)S(1)}, f32[2,256]{1,0:T(2,128)S(1)}, u32[]{:S(2)}, u32[]{:S(2)}) collective-permute-start(f32[2,256]{1,0:T(2,128)S(1)} %final_part.1.refs_0_), channel_id=1, source_target_pairs={{0,1},{1,0},{2,3},{3,2},{4,5},{5,4},{6,7},{7,6},{8,9},{9,8},{10,11... | collective-permute-start | bytes 6152 | tf_op jit(solution)/shard_map/ppermute | solution.py:20
  88.3 3.7 %collective-permute-start.20 = (f32[2,256]{1,0:T(2,128)S(1)}, f32[2,256]{1,0:T(2,128)S(1)}, u32[]{:S(2)}, u32[]{:S(2)}) collective-permute-start(f32[2,256]{1,0:T(2,128)S(1)} %final_part.1.refs_0_), channel_id=1, source_target_pairs={{0,2},{1,3},{2,0},{3,1},{4,6},{5,7},{6,4},{7,5},{8,10},{9,11},{10,... | collective-permute-start | bytes 6152 | tf_op jit(solution)/shard_map/ppermute | solution.py:20
  88.9 3.1 %collective-permute-start.21 = (f32[2,256]{1,0:T(2,128)S(1)}, f32[2,256]{1,0:T(2,128)S(1)}, u32[]{:S(2)}, u32[]{:S(2)}) collective-permute-start(f32[2,256]{1,0:T(2,128)S(1)} %final_part.1.refs_0_), channel_id=1, source_target_pairs={{0,3},{1,2},{2,1},{3,0},{4,7},{5,6},{6,5},{7,4},{8,11},{9,10},{10,... | collective-permute-start | bytes 6152 | tf_op jit(solution)/shard_map/ppermute | solution.py:20

commit v2 on v1

--- a/solution.py
+++ b/solution.py
@@ -521,16 +521,11 @@
     piece = lax.dynamic_slice_in_dim(scaled, (z % ratio) * rows_wanted, rows_wanted, 0)
     owner = [i // ratio for i in range(count)]
     place = m ^ (z // ratio)
-    value, bit, holders = piece, shards // 2, [0]
-    while bit:
-        pairs = [(i * shards + (owner[i] ^ h), i * shards + (owner[i] ^ h ^ bit)) for i in range(count) for h in holders]
-        moved = lax.ppermute(value, ("ctx", "mp"), pairs)
-        known = sum((place == h).astype(jnp.int32) for h in holders) > 0
-        if bit == 1:
-            return [value, moved], jnp.where(known, 0, 1)
-        value = jnp.where(known, value, moved)
-        holders, bit = holders + [h ^ bit for h in holders], bit // 2
-    return [value], 0
+    copies = [piece]
+    for k in range(1, shards):
+        pairs = [(i * shards + owner[i], i * shards + (owner[i] ^ k)) for i in range(count)]
+        copies.append(lax.ppermute(piece, ("ctx", "mp"), pairs))
+    return copies, place
 
 
 def half_kernel(groups, which_ref, weight_ref, *refs):
@@ -565,10 +560,37 @@
         functools.partial(both_kernel, tuple(len(block) for block in blocks)),
         in_specs=[pl.BlockSpec(memory_space=pltpu.SMEM)] + [in_vmem()] * (1 + len(flat)),
         out_specs=[in_vmem()] * 2,
-        out_shape=[jax.ShapeDtypeStruct((rows, weight.shape[1]), dtype) for dtype in (BF16, F32)],
+        out_shape=[jax.ShapeDtypeStruct((rows, weight.shape[1]), dtype) for dtype in (BF16, BF16)],
         compiler_params=SMALL,
         name="both_parts",
     )(which.astype(jnp.int32)[None], weight, *flat)
+
+
+def fetch_kernel(which_ref, weight_ref, *refs):
+    count = (len(refs) - 2) // 2
+    terms, out_ref, held, sems = refs[:count], refs[count], refs[count + 1 : -1], refs[-1]
+    half = out_ref.shape[0]
+    rows = pl.ds(pl.multiple_of(which_ref[0] * half, half), half)
+    copies = [pltpu.make_async_copy(term.at[rows, :], here, sems.at[k]) for k, (term, here) in enumerate(zip(terms, held))]
+    for copy in copies:
+        copy.start()
+    for copy in copies:
+        copy.wait()
+    block = functools.reduce(lambda p, q: p + q, [here[...] for here in held])
+    out_ref[...] = jnp.dot(block, weight_ref[...], preferred_element_type=F32).astype(out_ref.dtype)
+
+
+def fetch_half(which, weight, terms, dtype):
+    half, width = terms[0].shape[0] // 2, terms[0].shape[1]
+    return pl.pallas_call(
+        fetch_kernel,
+        in_specs=[pl.BlockSpec(memory_space=pltpu.SMEM), in_vmem()] + [pl.BlockSpec(memory_space=pl.ANY)] * len(terms),
+        out_specs=in_vmem(),
+        out_shape=jax.ShapeDtypeStruct((half, weight.shape[1]), dtype),
+        scratch_shapes=[pltpu.VMEM((half, width), BF16)] * len(terms) + [pltpu.SemaphoreType.DMA((len(terms),))],
+        compiler_params=SMALL,
+        name="fetch_half",
+    )(which.astype(jnp.int32)[None], weight, *terms)
 
 
 def half_part(which, weight, blocks, dtype):
@@ -584,7 +606,7 @@
     )(which.astype(jnp.int32)[None], weight, *flat)
 
 
-def project(blocks, weight, m, hurry):
+def project(blocks, weight, m, hurry, last):
     shards, count = lax.axis_size("mp"), len(blocks)
     if shards == 1:
         whole = [functools.reduce(lambda p, q: p + q, block) for block in blocks]
@@ -595,8 +617,9 @@
         if value is None and not hurry:
             send, keep = both_parts(upper, weight, blocks)
         elif value is None:
-            send = half_part(1 - upper, weight, blocks, BF16)
-            keep = half_part(upper, weight, blocks, F32)
+            one = len(blocks) == 1
+            send = fetch_half(1 - upper, weight, blocks[0], BF16) if one else half_part(1 - upper, weight, blocks, BF16)
+            keep = fetch_half(upper, weight, blocks[0], F32) if one else half_part(upper, weight, blocks, F32 if last else BF16)
         else:
             half = value.shape[0] // count // 2
             pieces = value.reshape(count, 2, half, value.shape[1])
@@ -604,7 +627,8 @@
             send = lax.dynamic_index_in_dim(pieces, 1 - upper, 1, False).reshape(count * half, value.shape[1])
             send = send.astype(BF16)
         got = swap(send, "mp", bit)
-        value = keep + got.astype(F32)
+        value = keep.astype(F32) + got.astype(F32)
+        value = value if last or 2 * bit >= shards else value.astype(BF16)
         bit *= 2
     return value
 
@@ -654,8 +678,7 @@
         mid_b = lax.ppermute(beside, "ctx", middle)
         far_a = swap(mid_a, "ctx", 1)
         far_b = swap(mid_b, "ctx", 1)
-        mid_here = bring(gated, mid_b)
-        groups = [[[gated], [beside]], [[mid_a, far_a]], [[mid_here, far_b]]]
+        groups = [[[gated], [beside]], [[mid_a, far_a]], [[mid_b, far_b]]]
         low = z < 2
         where = [z, z ^ 1, jnp.where(low, 2, 1), jnp.where(low, 3, 0)]
     else:
@@ -667,7 +690,7 @@
         out_weight = bring(gated, out_weight)
     slots = []
     for k, blocks in enumerate(groups):
-        slots.append(project(blocks, out_weight, m, k != 1))
+        slots.append(project(blocks, out_weight, m, k != 1, k == len(groups) - 1))
     early = slots[:-1] if quick else slots
     part, squares, scores, un = logit_part(share, where, early, sources, mut_row, mut_col, nat_col)
     msgs = []

time: 93 us -> 95.1 us (1.023)
  starting transfers between devices: 29.2 us -> 31.9 us
  Pallas kernels: 20.4 us -> 22.3 us
  other arithmetic: 4.49 us -> 2.94 us
  waiting for transfers between devices: 36.9 us -> 35.9 us
    pallas_call x0 -> x2, Pallas kernels: none -> 2.86 us  [fetch_half(): pl.pallas_call(fetch_kernel, in_specs=[pl.BlockSpec(memory_space=pltpu.SM...]
    ppermute x18, starting transfers between devices: 18.7 us -> 20.3 us  [swap(): return lax.ppermute(value, axis, [(i, i ^ bit) for i in range(count)])]
    convert_element_type x0 -> x2, other arithmetic: none -> 1.3 us  [project(): value = value if last or 2 * bit >= shards else value.astype(BF16)]
    convert_element_type x1, other arithmetic: 2.49 us -> 1.27 us  [feature_rows(): scaled = (unembed.astype(F32) * norm_gain[:, None]).astype(BF16)]
    add x6 -> x4, other arithmetic: 1.42 us -> 0.2 us  [project(): value = keep.astype(F32) + got.astype(F32)]
    ppermute x2 -> x3, starting transfers between devices: 7.61 us -> 8.71 us  [feature_rows(): copies.append(lax.ppermute(piece, ('ctx', 'mp'), pairs))]
    pallas_call x2 -> x1, Pallas kernels: 2.66 us -> 1.6 us  [bring(): pl.pallas_call(bring_kernel, in_specs=[pl.BlockSpec(memory_space=pl.ANY),...]
    pallas_call x1, Pallas kernels: 1.72 us -> 2.74 us  [logit_part(): pl.pallas_call(functools.partial(logit_kernel, share, len(sources)), in_s...]
  transfers between devices with their start and end apart: 22 -> 23, of which waited for: 11 -> 8; matrix products, arithmetic and copies ran while one was open for 6% -> 4% of each run, Pallas kernels for 12% -> 16%
where the time goes in v2:
time: 95.1 us; the launch traced here: 94.7 us
  waiting for transfers between devices  35.9 us (38%)
  starting transfers between devices  31.9 us (34%)
  Pallas kernels  22.3 us (23%)
  other arithmetic  2.94 us (3%)
  between operations  1.03 us (1%)
    ppermute x18, waiting for transfers between devices, swap(): return lax.ppermute(value, axis, [(i, i ^ bit) for i in range(count)])  35.9 us
    ppermute x18, starting transfers between devices, swap(): return lax.ppermute(value, axis, [(i, i ^ bit) for i in range(count)])  20.3 us
    ppermute x3, starting transfers between devices, feature_rows(): copies.append(lax.ppermute(piece, ('ctx', 'mp'), pairs))  8.71 us
    pallas_call x1, Pallas kernels, local_part(): pl.pallas_call(functools.partial(local_kernel, rows // SUBS, modes), in_s...  3.51 us
    pallas_call x1, Pallas kernels, end_part(): pl.pallas_call(functools.partial(end_kernel, steps, modes), in_specs=[pl....  3.2 us
    pallas_call x2, Pallas kernels, fetch_half(): pl.pallas_call(fetch_kernel, in_specs=[pl.BlockSpec(memory_space=pltpu.SM...  2.86 us
    pallas_call x1, Pallas kernels, logit_part(): pl.pallas_call(functools.partial(logit_kernel, share, len(sources)), in_s...  2.74 us
    pallas_call x2, Pallas kernels, half_part(): pl.pallas_call(functools.partial(half_kernel, tuple((len(block) for block...  2.23 us
  transfers between devices with their start and end apart: 23, of which 8 were waited for; matrix products, arithmetic and copies ran while one was open for 4% of the time, Pallas kernels for 16%

profile of v2, /device:TPU:0, one launch (start us, length us, event | category | flops | bytes accessed | tf_op | source)
XLA Modules:
  0.0 94.7 jit_solution(5122921201134590996)
XLA Ops:
  0.6 3.2 %end_part.1 = (f32[256,1024]{1,0:T(8,128)S(1)}, bf16[256,1024]{1,0:T(8,128)(2,1)S(1)}, bf16[32,1024]{1,0:T(8,128)(2,1)S(1)}, f32[3,3,1024]{2,1,0:T(4,128)S(1)}, f32[2,8,1024]{2,1,0:T(8,128)S(1)}) custom-call(bf16[3,256,1024]{2,1,0:T(8,128)(2,1)} %x_any.1, f32[3,3,1024]{2,1,0:T(4,128)} %filt_any.1, f32[2,8,1024]{2,1,0:T(8,128)} %bitcast.41, s32[1,256]{1,0:T(1,128)} %bitcast.44), custom_call_target="tpu_custom_call" | custom-call | tf_op jit(solution)/shard_map/end_part/pallas_call | solution.py:166
  3.9 3.1 %collective-permute-start = (bf16[32,1024]{1,0:T(8,128)(2,1)S(1)}, bf16[32,1024]{1,0:T(8,128)(2,1)S(1)}, u32[]{:S(2)}, u32[]{:S(2)}) collective-permute-start(bf16[32,1024]{1,0:T(8,128)(2,1)S(1)} %get-tuple-element.39.rest_0_), channel_id=1, source_target_pairs={{0,4},{4,0},{8,12},{12,8},{1,5},{5,1},{9,13},{13,9},{2,6},{6,2},{1... | collective-permute-start | bytes 196616 | tf_op jit(solution)/shard_map/ppermute | solution.py:20
  7.0 2.6 %collective-permute-start.1 = (bf16[32,1024]{1,0:T(8,128)(2,1)S(1)}, bf16[32,1024]{1,0:T(8,128)(2,1)S(1)}, u32[]{:S(2)}, u32[]{:S(2)}) collective-permute-start(bf16[32,1024]{1,0:T(8,128)(2,1)S(1)} %get-tuple-element.39.rest_0_), channel_id=1, source_target_pairs={{0,8},{4,12},{8,0},{12,4},{1,9},{5,13},{9,1},{13,5},{2,10},{6,14},... | collective-permute-start | bytes 196616 | tf_op jit(solution)/shard_map/ppermute | solution.py:20
  9.6 3.5 %local_part.1 = (f32[256,1024]{1,0:T(8,128)S(1)}, bf16[256,1024]{1,0:T(8,128)(2,1)S(1)}, f32[64,1024]{1,0:T(8,128)S(1)}) custom-call(f32[3,3,1024]{2,1,0:T(4,128)S(1)} %get-tuple-element.32.filt_ref, f32[2,8,1024]{2,1,0:T(8,128)S(1)} %get-tuple-element.33.mode_ref, ...), custom_call_target="tpu_custom_call", output_to_operand_aliasing={{0}: (2, {}), {1}: (3, {})} | custom-call | tf_op jit(solution)/shard_map/local_part/pallas_call | solution.py:192
  14.2 1.4 %collective-permute-done.2.rest_3_ = bf16[32,1024]{1,0:T(8,128)(2,1)S(1)} collective-permute-done((bf16[32,1024]{1,0:T(8,128)(2,1)S(1)}, bf16[32,1024]{1,0:T(8,128)(2,1)S(1)}, u32[]{:S(2)}, u32[]{:S(2)}) %collective-permute-start.2) | collective-permute-done | bytes 65568 | tf_op jit(solution)/shard_map/ppermute | solution.py:20
  15.6 1.5 %carry_part.1 = (bf16[256,1024]{1,0:T(8,128)(2,1)S(1)}, f32[4,1024]{1,0:T(4,128)S(1)}) custom-call(s32[1]{0:T(128)} %bitcast.where_ref, f32[3,3,1024]{2,1,0:T(4,128)S(1)} %get-tuple-element.32.filt_ref, f32[2,8,1024]{2,1,0:T(8,128)S(1)} %get-tuple-element.33.mode_ref, f32[256,1024]{1,0:T(8,128)S(1)} %get-tuple-element.36.y_ref, ...), custom_call_target="tpu_custom_call" | custom-call | flops 8388608 | bytes 2097152 | tf_op jit(solution)/shard_map/carry_part/pallas_call | solution.py:299
  17.3 1.5 %collective-permute-start.9 = (bf16[256,1024]{1,0:T(8,128)(2,1)S(1)}, bf16[256,1024]{1,0:T(8,128)(2,1)}, u32[]{:S(2)}, u32[]{:S(2)}) collective-permute-start(bf16[256,1024]{1,0:T(8,128)(2,1)S(1)} %get-tuple-element.48.later_any.refs_0_), channel_id=1, source_target_pairs={{4,8},{8,4},{5,9},{9,5},{6,10},{10,6},{7,11},{11,7},{20,24},{24,20... | collective-permute-start | bytes 1572872 | tf_op jit(solution)/shard_map/ppermute | solution.py:677
  18.7 1.3 %multiply_convert_fusion.rest_0_ = bf16[1024,512]{1,0:T(8,128)(2,1)} fusion(bf16[1024,512]{1,0:T(8,128)(2,1)S(1)} %copy-done, f32[1024]{0:T(1024)S(1)} %copy-done.1), kind=kLoop, calls=%fused_computation | loop fusion | flops 1572864 | bytes 2101248 | tf_op jit(solution)/shard_map/convert_element_type | solution.py:516
  20.0 2.3 %collective-permute-start.3 = (bf16[1024,512]{1,0:T(8,128)(2,1)}, bf16[1024,512]{1,0:T(8,128)(2,1)}, u32[]{:S(2)}, u32[]{:S(2)}) collective-permute-start(bf16[1024,512]{1,0:T(8,128)(2,1)} %multiply_convert_fusion.rest_0_), channel_id=1, source_target_pairs={{0,1},{5,4},{10,11},{15,14},{16,17},{21,20},{26,27},{31,30}} | collective-permute-start | bytes 3145736 | tf_op jit(solution)/shard_map/ppermute | solution.py:527
  22.3 3.8 %collective-permute-start.4 = (bf16[1024,512]{1,0:T(8,128)(2,1)}, bf16[1024,512]{1,0:T(8,128)(2,1)}, u32[]{:S(2)}, u32[]{:S(2)}) collective-permute-start(bf16[1024,512]{1,0:T(8,128)(2,1)} %multiply_convert_fusion.rest_0_), channel_id=1, source_target_pairs={{0,2},{5,7},{10,8},{15,13},{16,18},{21,23},{26,24},{31,29}} | collective-permute-start | bytes 3145736 | tf_op jit(solution)/shard_map/ppermute | solution.py:527
  26.0 1.6 %bring.1.weight_ref = bf16[1024,1024]{1,0:T(8,128)(2,1)S(1)} custom-call(bf16[256,1024]{1,0:T(8,128)(2,1)S(1)} %get-tuple-element.48.later_any.refs_0_, bf16[1024,1024]{1,0:T(8,128)(2,1)} %src_any.1), custom_call_target="tpu_custom_call" | custom-call | tf_op jit(solution)/shard_map/bring/pallas_call | solution.py:318
  27.7 1.6 %collective-permute-done.6.refs_1_ = bf16[256,1024]{1,0:T(8,128)(2,1)S(1)} collective-permute-done((bf16[256,1024]{1,0:T(8,128)(2,1)S(1)}, bf16[256,1024]{1,0:T(8,128)(2,1)S(1)}, u32[]{:S(2)}, u32[]{:S(2)}) %collective-permute-start.6) | collective-permute-done | bytes 524320 | tf_op jit(solution)/shard_map/ppermute | solution.py:20
  29.3 1.5 %half_part.3 = bf16[256,1024]{1,0:T(8,128)(2,1)} custom-call(s32[1]{0:T(128)} %bitcast.12.which_ref, bf16[1024,1024]{1,0:T(8,128)(2,1)S(1)} %bring.1.weight_ref, bf16[256,1024]{1,0:T(8,128)(2,1)S(1)} %get-tuple-element.48.later_any.refs_0_, bf16[256,1024]{1,0:T(8,128)(2,1)S(1)} %collective-permute-done.6.refs_1_), custom_call_target="tpu_custom_call" | custom-call | tf_op jit(solution)/shard_map/half_part/pallas_call | solution.py:599
  30.8 1.5 %collective-permute-start.13 = (bf16[256,1024]{1,0:T(8,128)(2,1)S(1)}, bf16[256,1024]{1,0:T(8,128)(2,1)}, u32[]{:S(2)}, u32[]{:S(2)}) collective-permute-start(bf16[256,1024]{1,0:T(8,128)(2,1)S(1)} %collective-permute-done.6.refs_1_), channel_id=1, source_target_pairs={{4,8},{8,4},{5,9},{9,5},{6,10},{10,6},{7,11},{11,7},{20,24},{24,20... | collective-permute-start | bytes 1572872 | tf_op jit(solution)/shard_map/ppermute | solution.py:678
  32.3 3.2 %collective-permute-start.10 = (bf16[256,1024]{1,0:T(8,128)(2,1)}, bf16[256,1024]{1,0:T(8,128)(2,1)}, u32[]{:S(2)}, u32[]{:S(2)}) collective-permute-start(bf16[256,1024]{1,0:T(8,128)(2,1)} %collective-permute-done.9.refs_0_), channel_id=1, source_target_pairs={{0,4},{4,0},{8,12},{12,8},{1,5},{5,1},{9,13},{13,9},{2,6},{6,2},{1... | collective-permute-start | bytes 1572872 | tf_op jit(solution)/shard_map/ppermute | solution.py:20
  36.8 11.3 %collective-permute-done.10.refs_1_ = bf16[256,1024]{1,0:T(8,128)(2,1)} collective-permute-done((bf16[256,1024]{1,0:T(8,128)(2,1)}, bf16[256,1024]{1,0:T(8,128)(2,1)}, u32[]{:S(2)}, u32[]{:S(2)}) %collective-permute-start.10) | collective-permute-done | bytes 524320 | tf_op jit(solution)/shard_map/ppermute | solution.py:20
  48.1 2.7 %collective-permute-start.5 = (bf16[1024,512]{1,0:T(8,128)(2,1)}, bf16[1024,512]{1,0:T(8,128)(2,1)S(1)}, u32[]{:S(2)}, u32[]{:S(2)}) collective-permute-start(bf16[1024,512]{1,0:T(8,128)(2,1)} %multiply_convert_fusion.rest_0_), channel_id=1, source_target_pairs={{0,3},{5,6},{10,9},{15,12},{16,19},{21,22},{26,25},{31,28}} | collective-permute-start | bytes 3145736 | tf_op jit(solution)/shard_map/ppermute | solution.py:527
  50.8 1.9 %both_parts.1 = (bf16[128,1024]{1,0:T(8,128)(2,1)S(1)}, bf16[128,1024]{1,0:T(8,128)(2,1)S(1)}) custom-call(s32[1]{0:T(128)} %bitcast.11.which_ref, bf16[1024,1024]{1,0:T(8,128)(2,1)S(1)} %bring.1.weight_ref, bf16[256,1024]{1,0:T(8,128)(2,1)} %collective-permute-done.9.refs_0_, bf16[256,1024]{1,0:T(8,128)(2,1)} %collective-permute-done.10.refs_1_), custom_call_target="tpu_custom_call" | custom-call | tf_op jit(solution)/shard_map/both_parts/pallas_call | solution.py:559
  52.8 2.6 %collective-permute-start.14 = (bf16[256,1024]{1,0:T(8,128)(2,1)}, bf16[256,1024]{1,0:T(8,128)(2,1)S(1)}, u32[]{:S(2)}, u32[]{:S(2)}) collective-permute-start(bf16[256,1024]{1,0:T(8,128)(2,1)} %collective-permute-done.13.refs_0_), channel_id=1, source_target_pairs={{0,4},{4,0},{8,12},{12,8},{1,5},{5,1},{9,13},{13,9},{2,6},{6,2},{1... | collective-permute-start | bytes 1572872 | tf_op jit(solution)/shard_map/ppermute | solution.py:20
  55.4 1.2 %add_convert_fusion = bf16[256,1024]{1,0:T(8,128)(2,1)S(1)} fusion(bf16[256,1024]{1,0:T(8,128)(2,1)} %collective-permute-done.7, bf16[256,1024]{1,0:T(8,128)(2,1)S(1)} %half_part.2), kind=kLoop, calls=%fused_computation.1 | loop fusion | flops 1048576 | bytes 1572864 | tf_op jit(solution)/shard_map/convert_element_type | solution.py:631
  56.9 10.9 %collective-permute-done.14.refs_1_ = bf16[256,1024]{1,0:T(8,128)(2,1)S(1)} collective-permute-done((bf16[256,1024]{1,0:T(8,128)(2,1)}, bf16[256,1024]{1,0:T(8,128)(2,1)S(1)}, u32[]{:S(2)}, u32[]{:S(2)}) %collective-permute-start.14) | collective-permute-done | bytes 524320 | tf_op jit(solution)/shard_map/ppermute | solution.py:20
  67.8 1.4 %fetch_half.3 = bf16[128,1024]{1,0:T(8,128)(2,1)S(1)} custom-call(s32[1]{0:T(128)} %bitcast.12.which_ref, bf16[1024,1024]{1,0:T(8,128)(2,1)S(1)} %bring.1.weight_ref, bf16[256,1024]{1,0:T(8,128)(2,1)} %collective-permute-done.13.refs_0_, bf16[256,1024]{1,0:T(8,128)(2,1)S(1)} %collective-permute-done.14.refs_1_), custom_call_target="tpu_custom_call" | custom-call | tf_op jit(solution)/shard_map/fetch_half/pallas_call | solution.py:585
  69.3 2.0 %collective-permute-start.12 = (bf16[64,1024]{1,0:T(8,128)(2,1)S(1)}, bf16[64,1024]{1,0:T(8,128)(2,1)S(1)}, u32[]{:S(2)}, u32[]{:S(2)}) collective-permute-start(bf16[64,1024]{1,0:T(8,128)(2,1)S(1)} %dynamic-slice_bitcast_fusion), channel_id=1, source_target_pairs={{0,2},{1,3},{2,0},{3,1},{4,6},{5,7},{6,4},{7,5},{8,10},{9,11},{10,... | collective-permute-start | bytes 393224 | tf_op jit(solution)/shard_map/ppermute | solution.py:20
  71.4 1.4 %fetch_half.2 = f32[128,1024]{1,0:T(8,128)S(1)} custom-call(s32[1]{0:T(128)} %bitcast.11.which_ref, bf16[1024,1024]{1,0:T(8,128)(2,1)S(1)} %bring.1.weight_ref, bf16[256,1024]{1,0:T(8,128)(2,1)} %collective-permute-done.13.refs_0_, bf16[256,1024]{1,0:T(8,128)(2,1)S(1)} %collective-permute-done.14.refs_1_), custom_call_target="tpu_custom_call" | custom-call | tf_op jit(solution)/shard_map/fetch_half/pallas_call | solution.py:585
  73.2 2.6 %collective-permute-done.12 = bf16[64,1024]{1,0:T(8,128)(2,1)S(1)} collective-permute-done((bf16[64,1024]{1,0:T(8,128)(2,1)S(1)}, bf16[64,1024]{1,0:T(8,128)(2,1)S(1)}, u32[]{:S(2)}, u32[]{:S(2)}) %collective-permute-start.12) | collective-permute-done | bytes 131104 | tf_op jit(solution)/shard_map/ppermute | solution.py:20
  75.8 2.7 %logit_part.1 = (f32[256,512]{1,0:T(8,128)S(1)}, f32[1,256]{1,0:T(1,128)S(1)}, f32[1,256]{1,0:T(1,128)S(1)}, bf16[1024,512]{1,0:T(8,128)(2,1)S(1)}) custom-call(s32[6]{0:T(128)S(1)} %stack.33.where_ref, s32[256,1]{1,0:T(8,128)S(1)} %copy.17.row_ref, s32[256,1]{1,0:T(8,128)S(1)} %copy.18.id_ref, s32[256,1]{1,0:T(8,128)S(1)} %reshape.49.nat_ref, ...), custom_call_target="tpu_custom_call" | custom-call | tf_op jit(solution)/shard_map/logit_part/pallas_call | solution.py:391
  78.6 1.3 %message_part.1 = (f32[1,256]{1,0:T(1,128)S(1)}, f32[1,256]{1,0:T(1,128)S(1)}, bf16[72,512]{1,0:T(8,128)(2,1)S(1)}, bf16[72,512]{1,0:T(8,128)(2,1)S(1)}, bf16[72,512]{1,0:T(8,128)(2,1)S(1)}) custom-call(s32[6]{0:T(128)S(1)} %stack.33.where_ref, bf16[1024,512]{1,0:T(8,128)(2,1)S(1)} %get-tuple-element.52.un_ref, s32[256,1]{1,0:T(8,128)S(1)} %copy.17.row_ref, ...), custom_call_target="tpu_custom_call" | custom-call | tf_op jit(solution)/shard_map/message_part/pallas_call | solution.py:435
  79.9 1.3 %collective-permute-start.17 = (bf16[72,512]{1,0:T(8,128)(2,1)S(1)}, bf16[72,512]{1,0:T(8,128)(2,1)S(1)}, u32[]{:S(2)}, u32[]{:S(2)}) collective-permute-start(bf16[72,512]{1,0:T(8,128)(2,1)S(1)} %get-tuple-element.57), channel_id=1, source_target_pairs={{0,4},{4,0},{8,12},{12,8},{1,5},{5,1},{9,13},{13,9},{2,6},{6,2},{1... | collective-permute-start | bytes 221192 | tf_op jit(solution)/shard_map/ppermute | solution.py:20
  81.2 3.1 %collective-permute-start.19 = (bf16[72,512]{1,0:T(8,128)(2,1)S(1)}, bf16[72,512]{1,0:T(8,128)(2,1)S(1)}, u32[]{:S(2)}, u32[]{:S(2)}) collective-permute-start(bf16[72,512]{1,0:T(8,128)(2,1)S(1)} %get-tuple-element.59), channel_id=1, source_target_pairs={{0,12},{4,8},{8,4},{12,0},{1,13},{5,9},{9,5},{13,1},{2,14},{6,10},... | collective-permute-start | bytes 221192 | tf_op jit(solution)/shard_map/ppermute | solution.py:20
  84.4 5.1 %collective-permute-done.18.rest_1_ = bf16[72,512]{1,0:T(8,128)(2,1)S(1)} collective-permute-done((bf16[72,512]{1,0:T(8,128)(2,1)S(1)}, bf16[72,512]{1,0:T(8,128)(2,1)S(1)}, u32[]{:S(2)}, u32[]{:S(2)}) %collective-permute-start.18) | collective-permute-done | bytes 73760 | tf_op jit(solution)/shard_map/ppermute | solution.py:20
  91.1 1.2 %collective-permute-start.22 = (f32[2,256]{1,0:T(2,128)S(1)}, f32[2,256]{1,0:T(2,128)S(1)}, u32[]{:S(2)}, u32[]{:S(2)}) collective-permute-start(f32[2,256]{1,0:T(2,128)S(1)} %final_part.1.refs_0_), channel_id=1, source_target_pairs={{0,3},{1,2},{2,1},{3,0},{4,7},{5,6},{6,5},{7,4},{8,11},{9,10},{10,... | collective-permute-start | bytes 6152 | tf_op jit(solution)/shard_map/ppermute | solution.py:20
  92.3 1.8 %collective-permute-done.21.refs_2_ = f32[2,256]{1,0:T(2,128)S(1)} collective-permute-done((f32[2,256]{1,0:T(2,128)S(1)}, f32[2,256]{1,0:T(2,128)S(1)}, u32[]{:S(2)}, u32[]{:S(2)}) %collective-permute-start.21) | collective-permute-done | bytes 2080 | tf_op jit(solution)/shard_map/ppermute | solution.py:20
  (53 shorter events, 5.6 us)
Async XLA Ops:
  3.8 14.9 %copy-start = (bf16[1024,512]{1,0:T(8,128)(2,1)S(1)}, bf16[1024,512]{1,0:T(8,128)(2,1)}, u32[]{:S(2)}) copy-start(bf16[1024,512]{1,0:T(8,128)(2,1)} %param.14) | copy-start | bytes 3145732
  3.8 14.9 %copy-start.1 = (f32[1024]{0:T(1024)S(1)}, f32[1024]{0:T(1024)}, u32[]{:S(2)}) copy-start(f32[1024]{0:T(1024)} %param.13) | copy-start | bytes 12292
  3.9 9.2 %collective-permute-start = (bf16[32,1024]{1,0:T(8,128)(2,1)S(1)}, bf16[32,1024]{1,0:T(8,128)(2,1)S(1)}, u32[]{:S(2)}, u32[]{:S(2)}) collective-permute-start(bf16[32,1024]{1,0:T(8,128)(2,1)S(1)} %get-tuple-element.39.rest_0_), channel_id=1, source_target_pairs={{0,4},{4,0},{8,12},{12,8},{1,5},{5,1},{9,13},{13,9},{2,6},{6,2},{1... | collective-permute-start | bytes 196616 | tf_op jit(solution)/shard_map/ppermute | solution.py:20
  7.0 7.3 %collective-permute-start.1 = (bf16[32,1024]{1,0:T(8,128)(2,1)S(1)}, bf16[32,1024]{1,0:T(8,128)(2,1)S(1)}, u32[]{:S(2)}, u32[]{:S(2)}) collective-permute-start(bf16[32,1024]{1,0:T(8,128)(2,1)S(1)} %get-tuple-element.39.rest_0_), channel_id=1, source_target_pairs={{0,8},{4,12},{8,0},{12,4},{1,9},{5,13},{9,1},{13,5},{2,10},{6,14},... | collective-permute-start | bytes 196616 | tf_op jit(solution)/shard_map/ppermute | solution.py:20
  9.6 6.1 %collective-permute-start.2 = (bf16[32,1024]{1,0:T(8,128)(2,1)S(1)}, bf16[32,1024]{1,0:T(8,128)(2,1)S(1)}, u32[]{:S(2)}, u32[]{:S(2)}) collective-permute-start(bf16[32,1024]{1,0:T(8,128)(2,1)S(1)} %get-tuple-element.39.rest_0_), channel_id=1, source_target_pairs={{0,12},{4,8},{8,4},{12,0},{1,13},{5,9},{9,5},{13,1},{2,14},{6,10},... | collective-permute-start | bytes 196616 | tf_op jit(solution)/shard_map/ppermute | solution.py:20
  17.2 12.1 %collective-permute-start.6 = (bf16[256,1024]{1,0:T(8,128)(2,1)S(1)}, bf16[256,1024]{1,0:T(8,128)(2,1)S(1)}, u32[]{:S(2)}, u32[]{:S(2)}) collective-permute-start(bf16[256,1024]{1,0:T(8,128)(2,1)S(1)} %get-tuple-element.48.later_any.refs_0_), channel_id=1, source_target_pairs={{0,4},{4,0},{8,12},{12,8},{1,5},{5,1},{9,13},{13,9},{2,6},{6,2},{1... | collective-permute-start | bytes 1572872 | tf_op jit(solution)/shard_map/ppermute | solution.py:20
  17.3 15.0 %collective-permute-start.9 = (bf16[256,1024]{1,0:T(8,128)(2,1)S(1)}, bf16[256,1024]{1,0:T(8,128)(2,1)}, u32[]{:S(2)}, u32[]{:S(2)}) collective-permute-start(bf16[256,1024]{1,0:T(8,128)(2,1)S(1)} %get-tuple-element.48.later_any.refs_0_), channel_id=1, source_target_pairs={{4,8},{8,4},{5,9},{9,5},{6,10},{10,6},{7,11},{11,7},{20,24},{24,20... | collective-permute-start | bytes 1572872 | tf_op jit(solution)/shard_map/ppermute | solution.py:677
  20.0 55.8 %collective-permute-start.3 = (bf16[1024,512]{1,0:T(8,128)(2,1)}, bf16[1024,512]{1,0:T(8,128)(2,1)}, u32[]{:S(2)}, u32[]{:S(2)}) collective-permute-start(bf16[1024,512]{1,0:T(8,128)(2,1)} %multiply_convert_fusion.rest_0_), channel_id=1, source_target_pairs={{0,1},{5,4},{10,11},{15,14},{16,17},{21,20},{26,27},{31,30}} | collective-permute-start | bytes 3145736 | tf_op jit(solution)/shard_map/ppermute | solution.py:527
  22.3 53.6 %collective-permute-start.4 = (bf16[1024,512]{1,0:T(8,128)(2,1)}, bf16[1024,512]{1,0:T(8,128)(2,1)}, u32[]{:S(2)}, u32[]{:S(2)}) collective-permute-start(bf16[1024,512]{1,0:T(8,128)(2,1)} %multiply_convert_fusion.rest_0_), channel_id=1, source_target_pairs={{0,2},{5,7},{10,8},{15,13},{16,18},{21,23},{26,24},{31,29}} | collective-permute-start | bytes 3145736 | tf_op jit(solution)/shard_map/ppermute | solution.py:527
  27.6 8.1 %copy-start.3 = (s32[256]{0:T(256)S(1)}, s32[256]{0:T(256)}, u32[]{:S(2)}) copy-start(s32[256]{0:T(256)} %param.16) | copy-start | bytes 3076
  27.6 8.2 %copy-start.2 = (s32[256]{0:T(256)S(1)}, s32[256]{0:T(256)}, u32[]{:S(2)}) copy-start(s32[256]{0:T(256)} %param.17) | copy-start | bytes 3076
  30.8 22.0 %collective-permute-start.7 = (bf16[256,1024]{1,0:T(8,128)(2,1)}, bf16[256,1024]{1,0:T(8,128)(2,1)}, u32[]{:S(2)}, u32[]{:S(2)}) collective-permute-start(bf16[256,1024]{1,0:T(8,128)(2,1)} %half_part.3), channel_id=1, source_target_pairs={{0,1},{1,0},{2,3},{3,2},{4,5},{5,4},{6,7},{7,6},{8,9},{9,8},{10,11... | collective-permute-start | bytes 1572872 | tf_op jit(solution)/shard_map/ppermute | solution.py:20
  30.8 21.9 %collective-permute-start.13 = (bf16[256,1024]{1,0:T(8,128)(2,1)S(1)}, bf16[256,1024]{1,0:T(8,128)(2,1)}, u32[]{:S(2)}, u32[]{:S(2)}) collective-permute-start(bf16[256,1024]{1,0:T(8,128)(2,1)S(1)} %collective-permute-done.6.refs_1_), channel_id=1, source_target_pairs={{4,8},{8,4},{5,9},{9,5},{6,10},{10,6},{7,11},{11,7},{20,24},{24,20... | collective-permute-start | bytes 1572872 | tf_op jit(solution)/shard_map/ppermute | solution.py:678
  32.3 15.8 %collective-permute-start.10 = (bf16[256,1024]{1,0:T(8,128)(2,1)}, bf16[256,1024]{1,0:T(8,128)(2,1)}, u32[]{:S(2)}, u32[]{:S(2)}) collective-permute-start(bf16[256,1024]{1,0:T(8,128)(2,1)} %collective-permute-done.9.refs_0_), channel_id=1, source_target_pairs={{0,4},{4,0},{8,12},{12,8},{1,5},{5,1},{9,13},{13,9},{2,6},{6,2},{1... | collective-permute-start | bytes 1572872 | tf_op jit(solution)/shard_map/ppermute | solution.py:20
  48.1 27.7 %collective-permute-start.5 = (bf16[1024,512]{1,0:T(8,128)(2,1)}, bf16[1024,512]{1,0:T(8,128)(2,1)S(1)}, u32[]{:S(2)}, u32[]{:S(2)}) collective-permute-start(bf16[1024,512]{1,0:T(8,128)(2,1)} %multiply_convert_fusion.rest_0_), channel_id=1, source_target_pairs={{0,3},{5,6},{10,9},{15,12},{16,19},{21,22},{26,25},{31,28}} | collective-permute-start | bytes 3145736 | tf_op jit(solution)/shard_map/ppermute | solution.py:527
  52.7 4.0 %collective-permute-start.11 = (bf16[128,1024]{1,0:T(8,128)(2,1)S(1)}, bf16[128,1024]{1,0:T(8,128)(2,1)S(1)}, u32[]{:S(2)}, u32[]{:S(2)}) collective-permute-start(bf16[128,1024]{1,0:T(8,128)(2,1)S(1)} %get-tuple-element.50), channel_id=1, source_target_pairs={{0,1},{1,0},{2,3},{3,2},{4,5},{5,4},{6,7},{7,6},{8,9},{9,8},{10,11... | collective-permute-start | bytes 786440 | tf_op jit(solution)/shard_map/ppermute | solution.py:20
  52.8 15.0 %collective-permute-start.14 = (bf16[256,1024]{1,0:T(8,128)(2,1)}, bf16[256,1024]{1,0:T(8,128)(2,1)S(1)}, u32[]{:S(2)}, u32[]{:S(2)}) collective-permute-start(bf16[256,1024]{1,0:T(8,128)(2,1)} %collective-permute-done.13.refs_0_), channel_id=1, source_target_pairs={{0,4},{4,0},{8,12},{12,8},{1,5},{5,1},{9,13},{13,9},{2,6},{6,2},{1... | collective-permute-start | bytes 1572872 | tf_op jit(solution)/shard_map/ppermute | solution.py:20
  56.7 12.6 %collective-permute-start.8 = (bf16[128,1024]{1,0:T(8,128)(2,1)S(1)}, bf16[128,1024]{1,0:T(8,128)(2,1)S(1)}, u32[]{:S(2)}, u32[]{:S(2)}) collective-permute-start(bf16[128,1024]{1,0:T(8,128)(2,1)S(1)} %bitcast.40), channel_id=1, source_target_pairs={{0,2},{1,3},{2,0},{3,1},{4,6},{5,7},{6,4},{7,5},{8,10},{9,11},{10,... | collective-permute-start | bytes 786440 | tf_op jit(solution)/shard_map/ppermute | solution.py:20
  69.2 3.6 %collective-permute-start.15 = (bf16[128,1024]{1,0:T(8,128)(2,1)S(1)}, bf16[128,1024]{1,0:T(8,128)(2,1)S(1)}, u32[]{:S(2)}, u32[]{:S(2)}) collective-permute-start(bf16[128,1024]{1,0:T(8,128)(2,1)S(1)} %fetch_half.3), channel_id=1, source_target_pairs={{0,1},{1,0},{2,3},{3,2},{4,5},{5,4},{6,7},{7,6},{8,9},{9,8},{10,11... | collective-permute-start | bytes 786440 | tf_op jit(solution)/shard_map/ppermute | solution.py:20
  69.3 6.4 %collective-permute-start.12 = (bf16[64,1024]{1,0:T(8,128)(2,1)S(1)}, bf16[64,1024]{1,0:T(8,128)(2,1)S(1)}, u32[]{:S(2)}, u32[]{:S(2)}) collective-permute-start(bf16[64,1024]{1,0:T(8,128)(2,1)S(1)} %dynamic-slice_bitcast_fusion), channel_id=1, source_target_pairs={{0,2},{1,3},{2,0},{3,1},{4,6},{5,7},{6,4},{7,5},{8,10},{9,11},{10,... | collective-permute-start | bytes 393224 | tf_op jit(solution)/shard_map/ppermute | solution.py:20
  73.0 5.6 %collective-permute-start.16 = (bf16[64,1024]{1,0:T(8,128)(2,1)S(1)}, bf16[64,1024]{1,0:T(8,128)(2,1)S(1)}, u32[]{:S(2)}, u32[]{:S(2)}) collective-permute-start(bf16[64,1024]{1,0:T(8,128)(2,1)S(1)} %fusion), channel_id=1, source_target_pairs={{0,2},{1,3},{2,0},{3,1},{4,6},{5,7},{6,4},{7,5},{8,10},{9,11},{10,... | collective-permute-start | bytes 393224 | tf_op jit(solution)/shard_map/ppermute | solution.py:20
  79.9 4.5 %collective-permute-start.17 = (bf16[72,512]{1,0:T(8,128)(2,1)S(1)}, bf16[72,512]{1,0:T(8,128)(2,1)S(1)}, u32[]{:S(2)}, u32[]{:S(2)}) collective-permute-start(bf16[72,512]{1,0:T(8,128)(2,1)S(1)} %get-tuple-element.57), channel_id=1, source_target_pairs={{0,4},{4,0},{8,12},{12,8},{1,5},{5,1},{9,13},{13,9},{2,6},{6,2},{1... | collective-permute-start | bytes 221192 | tf_op jit(solution)/shard_map/ppermute | solution.py:20
  81.2 8.3 %collective-permute-start.18 = (bf16[72,512]{1,0:T(8,128)(2,1)S(1)}, bf16[72,512]{1,0:T(8,128)(2,1)S(1)}, u32[]{:S(2)}, u32[]{:S(2)}) collective-permute-start(bf16[72,512]{1,0:T(8,128)(2,1)S(1)} %get-tuple-element.58), channel_id=1, source_target_pairs={{0,8},{4,12},{8,0},{12,4},{1,9},{5,13},{9,1},{13,5},{2,10},{6,14},... | collective-permute-start | bytes 221192 | tf_op jit(solution)/shard_map/ppermute | solution.py:20
  81.2 8.3 %collective-permute-start.19 = (bf16[72,512]{1,0:T(8,128)(2,1)S(1)}, bf16[72,512]{1,0:T(8,128)(2,1)S(1)}, u32[]{:S(2)}, u32[]{:S(2)}) collective-permute-start(bf16[72,512]{1,0:T(8,128)(2,1)S(1)} %get-tuple-element.59), channel_id=1, source_target_pairs={{0,12},{4,8},{8,4},{12,0},{1,13},{5,9},{9,5},{13,1},{2,14},{6,10},... | collective-permute-start | bytes 221192 | tf_op jit(solution)/shard_map/ppermute | solution.py:20
  90.4 1.9 %collective-permute-start.20 = (f32[2,256]{1,0:T(2,128)S(1)}, f32[2,256]{1,0:T(2,128)S(1)}, u32[]{:S(2)}, u32[]{:S(2)}) collective-permute-start(f32[2,256]{1,0:T(2,128)S(1)} %final_part.1.refs_0_), channel_id=1, source_target_pairs={{0,1},{1,0},{2,3},{3,2},{4,5},{5,4},{6,7},{7,6},{8,9},{9,8},{10,11... | collective-permute-start | bytes 6152 | tf_op jit(solution)/shard_map/ppermute | solution.py:20
  90.4 3.7 %collective-permute-start.21 = (f32[2,256]{1,0:T(2,128)S(1)}, f32[2,256]{1,0:T(2,128)S(1)}, u32[]{:S(2)}, u32[]{:S(2)}) collective-permute-start(f32[2,256]{1,0:T(2,128)S(1)} %final_part.1.refs_0_), channel_id=1, source_target_pairs={{0,2},{1,3},{2,0},{3,1},{4,6},{5,7},{6,4},{7,5},{8,10},{9,11},{10,... | collective-permute-start | bytes 6152 | tf_op jit(solution)/shard_map/ppermute | solution.py:20
  91.1 3.0 %collective-permute-start.22 = (f32[2,256]{1,0:T(2,128)S(1)}, f32[2,256]{1,0:T(2,128)S(1)}, u32[]{:S(2)}, u32[]{:S(2)}) collective-permute-start(f32[2,256]{1,0:T(2,128)S(1)} %final_part.1.refs_0_), channel_id=1, source_target_pairs={{0,3},{1,2},{2,1},{3,0},{4,7},{5,6},{6,5},{7,4},{8,11},{9,10},{10,... | collective-permute-start | bytes 6152 | tf_op jit(solution)/shard_map/ppermute | solution.py:20

commit v3 on v0

--- a/solution.py
+++ b/solution.py
@@ -503,18 +503,12 @@
         return lax.dynamic_slice_in_dim(every, z * rows_wanted, rows_wanted, 0)
     ratio = held // rows_wanted
     piece = lax.dynamic_slice_in_dim(scaled, (z % ratio) * rows_wanted, rows_wanted, 0)
-    owner = [i // ratio for i in range(count)]
-    place = m ^ (z // ratio)
-    value, bit, holders = piece, shards // 2, [0]
-    while bit:
-        pairs = [(i * shards + (owner[i] ^ h), i * shards + (owner[i] ^ h ^ bit)) for i in range(count) for h in holders]
-        moved = lax.ppermute(value, ("ctx", "mp"), pairs)
-        known = sum((place == h).astype(jnp.int32) for h in holders) > 0
-        if bit == 1:
-            return choose(jnp.where(known, 0, 1).astype(jnp.int32)[None], [value, moved])
-        value = jnp.where(known, value, moved)
-        holders, bit = holders + [h ^ bit for h in holders], bit // 2
-    return value
+    copies = [piece]
+    for k in range(1, shards):
+        owner = [i // ratio for i in range(count)]
+        pairs = [(i * shards + owner[i], i * shards + (owner[i] ^ k)) for i in range(count)]
+        copies.append(lax.ppermute(piece, ("ctx", "mp"), pairs))
+    return choose((m ^ (z // ratio)).astype(jnp.int32)[None], copies)
 
 
 def half_kernel(groups, which_ref, weight_ref, *refs):
@@ -666,7 +660,9 @@
     feats = norm_gain.shape[0] * shards
     span = max(rows, mut_pos.shape[0])
     result = final_part(feats, share, spot, part, squares, scores, nat_col, mut_row, msgs, span)
-    pieces = [result] + [swap(result, "mp", k) for k in range(1, shards)]
+    pieces = [result]
+    for k in range(1, shards):
+        pieces.append(swap(result, "mp", k))
     like, score = total_part(pieces, rows, mut_pos.shape[0])
     return like[0], score[0]
 

time: 93.8 us -> 101 us (1.077)
  starting transfers between devices: 29.2 us -> 51.4 us
  waiting for transfers between devices: 36.9 us -> 24.2 us
  other arithmetic: 4.53 us -> 2.87 us
    ppermute x18, starting transfers between devices: 18.7 us -> 40.2 us  [swap(): return lax.ppermute(value, axis, [(i, i ^ bit) for i in range(count)])]
    ppermute x18, waiting for transfers between devices: 36.8 us -> 24.2 us  [swap(): return lax.ppermute(value, axis, [(i, i ^ bit) for i in range(count)])]
    convert_element_type x1, other arithmetic: 2.5 us -> 1.26 us  [feature_rows(): scaled = (unembed.astype(F32) * norm_gain[:, None]).astype(BF16)]
    ppermute x2 -> x3, starting transfers between devices: 7.61 us -> 8.26 us  [feature_rows(): copies.append(lax.ppermute(piece, ('ctx', 'mp'), pairs))]
  transfers between devices with their start and end apart: 22 -> 23, of which waited for: 11 -> 8; matrix products, arithmetic and copies ran while one was open for 6% -> 3% of each run, Pallas kernels for 12% -> 12%
where the time goes in v3:
time: 101 us; the launch traced here: 100 us
  starting transfers between devices  51.4 us (51%)
  waiting for transfers between devices  24.2 us (24%)
  Pallas kernels  20.2 us (20%)
  other arithmetic  2.87 us (3%)
    ppermute x18, starting transfers between devices, swap(): return lax.ppermute(value, axis, [(i, i ^ bit) for i in range(count)])  40.2 us
    ppermute x18, waiting for transfers between devices, swap(): return lax.ppermute(value, axis, [(i, i ^ bit) for i in range(count)])  24.2 us
    ppermute x3, starting transfers between devices, feature_rows(): copies.append(lax.ppermute(piece, ('ctx', 'mp'), pairs))  8.26 us
    pallas_call x1, Pallas kernels, local_part(): pl.pallas_call(functools.partial(local_kernel, rows // SUBS, modes), in_s...  3.51 us
    pallas_call x1, Pallas kernels, end_part(): pl.pallas_call(functools.partial(end_kernel, steps, modes), in_specs=[pl....  3.2 us
    pallas_call x4, Pallas kernels, half_part(): pl.pallas_call(functools.partial(half_kernel, tuple((len(block) for block...  3.12 us
    pallas_call x2, Pallas kernels, bring(): pl.pallas_call(bring_kernel, in_specs=[pl.BlockSpec(memory_space=pl.ANY),...  2.65 us
  transfers between devices with their start and end apart: 23, of which 8 were waited for; matrix products, arithmetic and copies ran while one was open for 3% of the time, Pallas kernels for 12%

profile of v3, /device:TPU:0, one launch (start us, length us, event | category | flops | bytes accessed | tf_op | source)
XLA Modules:
  0.0 100.3 jit_solution(16871885588671363824)
XLA Ops:
  0.6 3.2 %end_part.1 = (f32[256,1024]{1,0:T(8,128)S(1)}, bf16[256,1024]{1,0:T(8,128)(2,1)S(1)}, bf16[32,1024]{1,0:T(8,128)(2,1)S(1)}, f32[3,3,1024]{2,1,0:T(4,128)S(1)}, f32[2,8,1024]{2,1,0:T(8,128)S(1)}) custom-call(bf16[3,256,1024]{2,1,0:T(8,128)(2,1)} %x_any.1, f32[3,3,1024]{2,1,0:T(4,128)} %filt_any.1, f32[2,8,1024]{2,1,0:T(8,128)} %bitcast.40, s32[1,256]{1,0:T(1,128)} %bitcast.43), custom_call_target="tpu_custom_call" | custom-call | tf_op jit(solution)/shard_map/end_part/pallas_call | solution.py:166
  3.9 3.1 %collective-permute-start = (bf16[32,1024]{1,0:T(8,128)(2,1)S(1)}, bf16[32,1024]{1,0:T(8,128)(2,1)S(1)}, u32[]{:S(2)}, u32[]{:S(2)}) collective-permute-start(bf16[32,1024]{1,0:T(8,128)(2,1)S(1)} %get-tuple-element.36.rest_0_), channel_id=1, source_target_pairs={{0,4},{4,0},{8,12},{12,8},{1,5},{5,1},{9,13},{13,9},{2,6},{6,2},{1... | collective-permute-start | bytes 196616 | tf_op jit(solution)/shard_map/ppermute | solution.py:20
  7.0 2.6 %collective-permute-start.1 = (bf16[32,1024]{1,0:T(8,128)(2,1)S(1)}, bf16[32,1024]{1,0:T(8,128)(2,1)S(1)}, u32[]{:S(2)}, u32[]{:S(2)}) collective-permute-start(bf16[32,1024]{1,0:T(8,128)(2,1)S(1)} %get-tuple-element.36.rest_0_), channel_id=1, source_target_pairs={{0,8},{4,12},{8,0},{12,4},{1,9},{5,13},{9,1},{13,5},{2,10},{6,14},... | collective-permute-start | bytes 196616 | tf_op jit(solution)/shard_map/ppermute | solution.py:20
  9.6 3.5 %local_part.1 = (f32[256,1024]{1,0:T(8,128)S(1)}, bf16[256,1024]{1,0:T(8,128)(2,1)S(1)}, f32[64,1024]{1,0:T(8,128)S(1)}) custom-call(f32[3,3,1024]{2,1,0:T(4,128)S(1)} %get-tuple-element.29.filt_ref, f32[2,8,1024]{2,1,0:T(8,128)S(1)} %get-tuple-element.30.mode_ref, ...), custom_call_target="tpu_custom_call", output_to_operand_aliasing={{0}: (2, {}), {1}: (3, {})} | custom-call | tf_op jit(solution)/shard_map/local_part/pallas_call | solution.py:192
  13.1 1.1 %collective-permute-done.1.rest_2_ = bf16[32,1024]{1,0:T(8,128)(2,1)S(1)} collective-permute-done((bf16[32,1024]{1,0:T(8,128)(2,1)S(1)}, bf16[32,1024]{1,0:T(8,128)(2,1)S(1)}, u32[]{:S(2)}, u32[]{:S(2)}) %collective-permute-start.1) | collective-permute-done | bytes 65568 | tf_op jit(solution)/shard_map/ppermute | solution.py:20
  14.2 1.4 %collective-permute-done.2.rest_3_ = bf16[32,1024]{1,0:T(8,128)(2,1)S(1)} collective-permute-done((bf16[32,1024]{1,0:T(8,128)(2,1)S(1)}, bf16[32,1024]{1,0:T(8,128)(2,1)S(1)}, u32[]{:S(2)}, u32[]{:S(2)}) %collective-permute-start.2) | collective-permute-done | bytes 65568 | tf_op jit(solution)/shard_map/ppermute | solution.py:20
  15.6 1.5 %carry_part.1 = (bf16[256,1024]{1,0:T(8,128)(2,1)S(1)}, f32[4,1024]{1,0:T(4,128)S(1)}) custom-call(s32[1]{0:T(128)} %bitcast.where_ref, f32[3,3,1024]{2,1,0:T(4,128)S(1)} %get-tuple-element.29.filt_ref, f32[2,8,1024]{2,1,0:T(8,128)S(1)} %get-tuple-element.30.mode_ref, f32[256,1024]{1,0:T(8,128)S(1)} %get-tuple-element.33.y_ref, ...), custom_call_target="tpu_custom_call" | custom-call | flops 8388608 | bytes 2097152 | tf_op jit(solution)/shard_map/carry_part/pallas_call | solution.py:299
  17.2 1.5 %collective-permute-start.9 = (bf16[256,1024]{1,0:T(8,128)(2,1)S(1)}, bf16[256,1024]{1,0:T(8,128)(2,1)}, u32[]{:S(2)}, u32[]{:S(2)}) collective-permute-start(bf16[256,1024]{1,0:T(8,128)(2,1)S(1)} %get-tuple-element.45.later_any.refs_0_), channel_id=1, source_target_pairs={{4,8},{8,4},{5,9},{9,5},{6,10},{10,6},{7,11},{11,7},{20,24},{24,20... | collective-permute-start | bytes 1572872 | tf_op jit(solution)/shard_map/ppermute | solution.py:631
  18.7 2.7 %collective-permute-start.6 = (bf16[256,1024]{1,0:T(8,128)(2,1)S(1)}, bf16[256,1024]{1,0:T(8,128)(2,1)S(1)}, u32[]{:S(2)}, u32[]{:S(2)}) collective-permute-start(bf16[256,1024]{1,0:T(8,128)(2,1)S(1)} %get-tuple-element.45.later_any.refs_0_), channel_id=1, source_target_pairs={{0,4},{4,0},{8,12},{12,8},{1,5},{5,1},{9,13},{13,9},{2,6},{6,2},{1... | collective-permute-start | bytes 1572872 | tf_op jit(solution)/shard_map/ppermute | solution.py:20
  21.3 10.8 %collective-permute-start.10 = (bf16[256,1024]{1,0:T(8,128)(2,1)}, bf16[256,1024]{1,0:T(8,128)(2,1)}, u32[]{:S(2)}, u32[]{:S(2)}) collective-permute-start(bf16[256,1024]{1,0:T(8,128)(2,1)} %collective-permute-done.9.refs_0_), channel_id=1, source_target_pairs={{0,4},{4,0},{8,12},{12,8},{1,5},{5,1},{9,13},{13,9},{2,6},{6,2},{1... | collective-permute-start | bytes 1572872 | tf_op jit(solution)/shard_map/ppermute | solution.py:20
  32.1 1.3 %multiply_convert_fusion.refs_0_ = bf16[1024,512]{1,0:T(8,128)(2,1)} fusion(bf16[1024,512]{1,0:T(8,128)(2,1)S(1)} %copy-done, f32[1024]{0:T(1024)S(1)} %copy-done.1), kind=kLoop, calls=%fused_computation | loop fusion | flops 1572864 | bytes 2101248 | tf_op jit(solution)/shard_map/convert_element_type | solution.py:500
  33.4 2.3 %collective-permute-start.3 = (bf16[1024,512]{1,0:T(8,128)(2,1)}, bf16[1024,512]{1,0:T(8,128)(2,1)}, u32[]{:S(2)}, u32[]{:S(2)}) collective-permute-start(bf16[1024,512]{1,0:T(8,128)(2,1)} %multiply_convert_fusion.refs_0_), channel_id=1, source_target_pairs={{0,1},{5,4},{10,11},{15,14},{16,17},{21,20},{26,27},{31,30}} | collective-permute-start | bytes 3145736 | tf_op jit(solution)/shard_map/ppermute | solution.py:510
  35.7 3.7 %collective-permute-start.4 = (bf16[1024,512]{1,0:T(8,128)(2,1)}, bf16[1024,512]{1,0:T(8,128)(2,1)}, u32[]{:S(2)}, u32[]{:S(2)}) collective-permute-start(bf16[1024,512]{1,0:T(8,128)(2,1)} %multiply_convert_fusion.refs_0_), channel_id=1, source_target_pairs={{0,2},{5,7},{10,8},{15,13},{16,18},{21,23},{26,24},{31,29}} | collective-permute-start | bytes 3145736 | tf_op jit(solution)/shard_map/ppermute | solution.py:510
  39.4 2.3 %collective-permute-start.5 = (bf16[1024,512]{1,0:T(8,128)(2,1)}, bf16[1024,512]{1,0:T(8,128)(2,1)}, u32[]{:S(2)}, u32[]{:S(2)}) collective-permute-start(bf16[1024,512]{1,0:T(8,128)(2,1)} %multiply_convert_fusion.refs_0_), channel_id=1, source_target_pairs={{0,3},{5,6},{10,9},{15,12},{16,19},{21,22},{26,25},{31,28}} | collective-permute-start | bytes 3145736 | tf_op jit(solution)/shard_map/ppermute | solution.py:510
  41.7 1.6 %bring.2.weight_ref = bf16[1024,1024]{1,0:T(8,128)(2,1)S(1)} custom-call(bf16[256,1024]{1,0:T(8,128)(2,1)S(1)} %get-tuple-element.45.later_any.refs_0_, bf16[1024,1024]{1,0:T(8,128)(2,1)} %src_any.1), custom_call_target="tpu_custom_call" | custom-call | tf_op jit(solution)/shard_map/bring/pallas_call | solution.py:318
  43.3 1.5 %half_part.5 = bf16[256,1024]{1,0:T(8,128)(2,1)} custom-call(s32[1]{0:T(128)} %bitcast.12.which_ref, bf16[1024,1024]{1,0:T(8,128)(2,1)S(1)} %bring.2.weight_ref, bf16[256,1024]{1,0:T(8,128)(2,1)S(1)} %get-tuple-element.45.later_any.refs_0_, bf16[256,1024]{1,0:T(8,128)(2,1)S(1)} %collective-permute-done.6.refs_1_), custom_call_target="tpu_custom_call" | custom-call | tf_op jit(solution)/shard_map/half_part/pallas_call | solution.py:555
  44.8 1.5 %collective-permute-start.13 = (bf16[256,1024]{1,0:T(8,128)(2,1)S(1)}, bf16[256,1024]{1,0:T(8,128)(2,1)}, u32[]{:S(2)}, u32[]{:S(2)}) collective-permute-start(bf16[256,1024]{1,0:T(8,128)(2,1)S(1)} %collective-permute-done.6.refs_1_), channel_id=1, source_target_pairs={{4,8},{8,4},{5,9},{9,5},{6,10},{10,6},{7,11},{11,7},{20,24},{24,20... | collective-permute-start | bytes 1572872 | tf_op jit(solution)/shard_map/ppermute | solution.py:632
  47.7 1.9 %both_parts.1 = (bf16[128,1024]{1,0:T(8,128)(2,1)S(1)}, f32[128,1024]{1,0:T(8,128)S(1)}) custom-call(s32[1]{0:T(128)} %bitcast.11.which_ref, bf16[1024,1024]{1,0:T(8,128)(2,1)S(1)} %bring.2.weight_ref, bf16[256,1024]{1,0:T(8,128)(2,1)} %collective-permute-done.9.refs_0_, bf16[256,1024]{1,0:T(8,128)(2,1)} %collective-permute-done.10.refs_1_), custom_call_target="tpu_custom_call" | custom-call | tf_op jit(solution)/shard_map/both_parts/pallas_call | solution.py:542
  50.2 10.1 %collective-permute-start.14 = (bf16[256,1024]{1,0:T(8,128)(2,1)}, bf16[256,1024]{1,0:T(8,128)(2,1)S(1)}, u32[]{:S(2)}, u32[]{:S(2)}) collective-permute-start(bf16[256,1024]{1,0:T(8,128)(2,1)} %collective-permute-done.13.src_any), channel_id=1, source_target_pairs={{0,4},{4,0},{8,12},{12,8},{1,5},{5,1},{9,13},{13,9},{2,6},{6,2},{1... | collective-permute-start | bytes 1572872 | tf_op jit(solution)/shard_map/ppermute | solution.py:20
  60.3 1.2 %convert_add_fusion = f32[256,1024]{1,0:T(8,128)S(1)} fusion(f32[256,1024]{1,0:T(8,128)S(1)} %half_part.4, bf16[256,1024]{1,0:T(8,128)(2,1)} %collective-permute-done.7), kind=kLoop, calls=%fused_computation.1 | loop fusion | flops 524288 | bytes 2621440 | tf_op jit(solution)/shard_map/add | solution.py:585
  62.7 1.5 %collective-permute-start.8 = (bf16[128,1024]{1,0:T(8,128)(2,1)S(1)}, bf16[128,1024]{1,0:T(8,128)(2,1)S(1)}, u32[]{:S(2)}, u32[]{:S(2)}) collective-permute-start(bf16[128,1024]{1,0:T(8,128)(2,1)S(1)} %bitcast.39), channel_id=1, source_target_pairs={{0,2},{1,3},{2,0},{3,1},{4,6},{5,7},{6,4},{7,5},{8,10},{9,11},{10,... | collective-permute-start | bytes 786440 | tf_op jit(solution)/shard_map/ppermute | solution.py:20
  64.2 1.2 %choose.1.un_ref = bf16[1024,512]{1,0:T(8,128)(2,1)S(1)} custom-call(s32[1]{0:T(128)} %bitcast.8.place_ref, bf16[1024,512]{1,0:T(8,128)(2,1)} %multiply_convert_fusion.refs_0_, bf16[1024,512]{1,0:T(8,128)(2,1)} %collective-permute-done.3.refs_1_, bf16[1024,512]{1,0:T(8,128)(2,1)} %collective-permute-done.4.refs_2_, ...), custom_call_target="tpu_custom_call" | custom-call | tf_op jit(solution)/shard_map/choose/pallas_call | solution.py:486
  65.5 7.6 %collective-permute-done.14.refs_1_ = bf16[256,1024]{1,0:T(8,128)(2,1)S(1)} collective-permute-done((bf16[256,1024]{1,0:T(8,128)(2,1)}, bf16[256,1024]{1,0:T(8,128)(2,1)S(1)}, u32[]{:S(2)}, u32[]{:S(2)}) %collective-permute-start.14) | collective-permute-done | bytes 524320 | tf_op jit(solution)/shard_map/ppermute | solution.py:20
  73.7 1.5 %collective-permute-start.12 = (bf16[64,1024]{1,0:T(8,128)(2,1)S(1)}, bf16[64,1024]{1,0:T(8,128)(2,1)S(1)}, u32[]{:S(2)}, u32[]{:S(2)}) collective-permute-start(bf16[64,1024]{1,0:T(8,128)(2,1)S(1)} %fusion), channel_id=1, source_target_pairs={{0,2},{1,3},{2,0},{3,1},{4,6},{5,7},{6,4},{7,5},{8,10},{9,11},{10,... | collective-permute-start | bytes 393224 | tf_op jit(solution)/shard_map/ppermute | solution.py:20
  76.7 3.4 %collective-permute-done.12 = bf16[64,1024]{1,0:T(8,128)(2,1)S(1)} collective-permute-done((bf16[64,1024]{1,0:T(8,128)(2,1)S(1)}, bf16[64,1024]{1,0:T(8,128)(2,1)S(1)}, u32[]{:S(2)}, u32[]{:S(2)}) %collective-permute-start.12) | collective-permute-done | bytes 131104 | tf_op jit(solution)/shard_map/ppermute | solution.py:20
  80.2 2.3 %collective-permute-done.16 = bf16[64,1024]{1,0:T(8,128)(2,1)S(1)} collective-permute-done((bf16[64,1024]{1,0:T(8,128)(2,1)S(1)}, bf16[64,1024]{1,0:T(8,128)(2,1)S(1)}, u32[]{:S(2)}, u32[]{:S(2)}) %collective-permute-start.16) | collective-permute-done | bytes 131104 | tf_op jit(solution)/shard_map/ppermute | solution.py:20
  82.5 1.6 %logit_part.1 = (f32[256,512]{1,0:T(8,128)S(1)}, f32[1,256]{1,0:T(1,128)S(1)}, f32[1,256]{1,0:T(1,128)S(1)}, bf16[72,512]{1,0:T(8,128)(2,1)S(1)}, bf16[72,512]{1...) custom-call(s32[5]{0:T(128)S(1)} %stack.29.where_ref, bf16[1024,512]{1,0:T(8,128)(2,1)S(1)} %choose.1.un_ref, ...), custom_call_target="tpu_custom_call" | custom-call | tf_op jit(solution)/shard_map/logit_part/pallas_call | solution.py:391
  84.1 1.8 %collective-permute-start.17 = (bf16[72,512]{1,0:T(8,128)(2,1)S(1)}, bf16[72,512]{1,0:T(8,128)(2,1)S(1)}, u32[]{:S(2)}, u32[]{:S(2)}) collective-permute-start(bf16[72,512]{1,0:T(8,128)(2,1)S(1)} %get-tuple-element.51), channel_id=1, source_target_pairs={{0,4},{4,0},{8,12},{12,8},{1,5},{5,1},{9,13},{13,9},{2,6},{6,2},{1... | collective-permute-start | bytes 221192 | tf_op jit(solution)/shard_map/ppermute | solution.py:20
  87.0 1.5 %collective-permute-start.19 = (bf16[72,512]{1,0:T(8,128)(2,1)S(1)}, bf16[72,512]{1,0:T(8,128)(2,1)S(1)}, u32[]{:S(2)}, u32[]{:S(2)}) collective-permute-start(bf16[72,512]{1,0:T(8,128)(2,1)S(1)} %get-tuple-element.53), channel_id=1, source_target_pairs={{0,12},{4,8},{8,4},{12,0},{1,13},{5,9},{9,5},{13,1},{2,14},{6,10},... | collective-permute-start | bytes 221192 | tf_op jit(solution)/shard_map/ppermute | solution.py:20
  88.6 5.8 %collective-permute-done.18.rest_1_ = bf16[72,512]{1,0:T(8,128)(2,1)S(1)} collective-permute-done((bf16[72,512]{1,0:T(8,128)(2,1)S(1)}, bf16[72,512]{1,0:T(8,128)(2,1)S(1)}, u32[]{:S(2)}, u32[]{:S(2)}) %collective-permute-start.18) | collective-permute-done | bytes 73760 | tf_op jit(solution)/shard_map/ppermute | solution.py:20
  95.3 1.4 %collective-permute-start.21 = (f32[2,256]{1,0:T(2,128)S(1)}, f32[2,256]{1,0:T(2,128)S(1)}, u32[]{:S(2)}, u32[]{:S(2)}) collective-permute-start(f32[2,256]{1,0:T(2,128)S(1)} %final_part.1.refs_0_), channel_id=1, source_target_pairs={{0,2},{1,3},{2,0},{3,1},{4,6},{5,7},{6,4},{7,5},{8,10},{9,11},{10,... | collective-permute-start | bytes 6152 | tf_op jit(solution)/shard_map/ppermute | solution.py:20
  97.1 1.8 %collective-permute-done.21.refs_2_ = f32[2,256]{1,0:T(2,128)S(1)} collective-permute-done((f32[2,256]{1,0:T(2,128)S(1)}, f32[2,256]{1,0:T(2,128)S(1)}, u32[]{:S(2)}, u32[]{:S(2)}) %collective-permute-start.21) | collective-permute-done | bytes 2080 | tf_op jit(solution)/shard_map/ppermute | solution.py:20
  (55 shorter events, 9.2 us)
Async XLA Ops:
  3.8 28.3 %copy-start = (bf16[1024,512]{1,0:T(8,128)(2,1)S(1)}, bf16[1024,512]{1,0:T(8,128)(2,1)}, u32[]{:S(2)}) copy-start(bf16[1024,512]{1,0:T(8,128)(2,1)} %param.14) | copy-start | bytes 3145732
  3.8 28.3 %copy-start.1 = (f32[1024]{0:T(1024)S(1)}, f32[1024]{0:T(1024)}, u32[]{:S(2)}) copy-start(f32[1024]{0:T(1024)} %param.13) | copy-start | bytes 12292
  3.9 9.2 %collective-permute-start = (bf16[32,1024]{1,0:T(8,128)(2,1)S(1)}, bf16[32,1024]{1,0:T(8,128)(2,1)S(1)}, u32[]{:S(2)}, u32[]{:S(2)}) collective-permute-start(bf16[32,1024]{1,0:T(8,128)(2,1)S(1)} %get-tuple-element.36.rest_0_), channel_id=1, source_target_pairs={{0,4},{4,0},{8,12},{12,8},{1,5},{5,1},{9,13},{13,9},{2,6},{6,2},{1... | collective-permute-start | bytes 196616 | tf_op jit(solution)/shard_map/ppermute | solution.py:20
  7.0 7.3 %collective-permute-start.1 = (bf16[32,1024]{1,0:T(8,128)(2,1)S(1)}, bf16[32,1024]{1,0:T(8,128)(2,1)S(1)}, u32[]{:S(2)}, u32[]{:S(2)}) collective-permute-start(bf16[32,1024]{1,0:T(8,128)(2,1)S(1)} %get-tuple-element.36.rest_0_), channel_id=1, source_target_pairs={{0,8},{4,12},{8,0},{12,4},{1,9},{5,13},{9,1},{13,5},{2,10},{6,14},... | collective-permute-start | bytes 196616 | tf_op jit(solution)/shard_map/ppermute | solution.py:20
  9.6 6.1 %collective-permute-start.2 = (bf16[32,1024]{1,0:T(8,128)(2,1)S(1)}, bf16[32,1024]{1,0:T(8,128)(2,1)S(1)}, u32[]{:S(2)}, u32[]{:S(2)}) collective-permute-start(bf16[32,1024]{1,0:T(8,128)(2,1)S(1)} %get-tuple-element.36.rest_0_), channel_id=1, source_target_pairs={{0,12},{4,8},{8,4},{12,0},{1,13},{5,9},{9,5},{13,1},{2,14},{6,10},... | collective-permute-start | bytes 196616 | tf_op jit(solution)/shard_map/ppermute | solution.py:20
  17.2 4.1 %collective-permute-start.9 = (bf16[256,1024]{1,0:T(8,128)(2,1)S(1)}, bf16[256,1024]{1,0:T(8,128)(2,1)}, u32[]{:S(2)}, u32[]{:S(2)}) collective-permute-start(bf16[256,1024]{1,0:T(8,128)(2,1)S(1)} %get-tuple-element.45.later_any.refs_0_), channel_id=1, source_target_pairs={{4,8},{8,4},{5,9},{9,5},{6,10},{10,6},{7,11},{11,7},{20,24},{24,20... | collective-permute-start | bytes 1572872 | tf_op jit(solution)/shard_map/ppermute | solution.py:631
  18.7 24.6 %collective-permute-start.6 = (bf16[256,1024]{1,0:T(8,128)(2,1)S(1)}, bf16[256,1024]{1,0:T(8,128)(2,1)S(1)}, u32[]{:S(2)}, u32[]{:S(2)}) collective-permute-start(bf16[256,1024]{1,0:T(8,128)(2,1)S(1)} %get-tuple-element.45.later_any.refs_0_), channel_id=1, source_target_pairs={{0,4},{4,0},{8,12},{12,8},{1,5},{5,1},{9,13},{13,9},{2,6},{6,2},{1... | collective-permute-start | bytes 1572872 | tf_op jit(solution)/shard_map/ppermute | solution.py:20
  21.3 23.5 %collective-permute-start.10 = (bf16[256,1024]{1,0:T(8,128)(2,1)}, bf16[256,1024]{1,0:T(8,128)(2,1)}, u32[]{:S(2)}, u32[]{:S(2)}) collective-permute-start(bf16[256,1024]{1,0:T(8,128)(2,1)} %collective-permute-done.9.refs_0_), channel_id=1, source_target_pairs={{0,4},{4,0},{8,12},{12,8},{1,5},{5,1},{9,13},{13,9},{2,6},{6,2},{1... | collective-permute-start | bytes 1572872 | tf_op jit(solution)/shard_map/ppermute | solution.py:20
  33.4 29.3 %collective-permute-start.3 = (bf16[1024,512]{1,0:T(8,128)(2,1)}, bf16[1024,512]{1,0:T(8,128)(2,1)}, u32[]{:S(2)}, u32[]{:S(2)}) collective-permute-start(bf16[1024,512]{1,0:T(8,128)(2,1)} %multiply_convert_fusion.refs_0_), channel_id=1, source_target_pairs={{0,1},{5,4},{10,11},{15,14},{16,17},{21,20},{26,27},{31,30}} | collective-permute-start | bytes 3145736 | tf_op jit(solution)/shard_map/ppermute | solution.py:510
  35.7 28.5 %collective-permute-start.4 = (bf16[1024,512]{1,0:T(8,128)(2,1)}, bf16[1024,512]{1,0:T(8,128)(2,1)}, u32[]{:S(2)}, u32[]{:S(2)}) collective-permute-start(bf16[1024,512]{1,0:T(8,128)(2,1)} %multiply_convert_fusion.refs_0_), channel_id=1, source_target_pairs={{0,2},{5,7},{10,8},{15,13},{16,18},{21,23},{26,24},{31,29}} | collective-permute-start | bytes 3145736 | tf_op jit(solution)/shard_map/ppermute | solution.py:510
  39.4 24.8 %collective-permute-start.5 = (bf16[1024,512]{1,0:T(8,128)(2,1)}, bf16[1024,512]{1,0:T(8,128)(2,1)}, u32[]{:S(2)}, u32[]{:S(2)}) collective-permute-start(bf16[1024,512]{1,0:T(8,128)(2,1)} %multiply_convert_fusion.refs_0_), channel_id=1, source_target_pairs={{0,3},{5,6},{10,9},{15,12},{16,19},{21,22},{26,25},{31,28}} | collective-permute-start | bytes 3145736 | tf_op jit(solution)/shard_map/ppermute | solution.py:510
  43.3 3.3 %copy-start.3 = (s32[256]{0:T(256)S(1)}, s32[256]{0:T(256)}, u32[]{:S(2)}) copy-start(s32[256]{0:T(256)} %param.16) | copy-start | bytes 3076
  43.3 3.4 %copy-start.2 = (s32[256]{0:T(256)S(1)}, s32[256]{0:T(256)}, u32[]{:S(2)}) copy-start(s32[256]{0:T(256)} %param.17) | copy-start | bytes 3076
  44.8 5.4 %collective-permute-start.7 = (bf16[256,1024]{1,0:T(8,128)(2,1)}, bf16[256,1024]{1,0:T(8,128)(2,1)}, u32[]{:S(2)}, u32[]{:S(2)}) collective-permute-start(bf16[256,1024]{1,0:T(8,128)(2,1)} %half_part.5), channel_id=1, source_target_pairs={{0,1},{1,0},{2,3},{3,2},{4,5},{5,4},{6,7},{7,6},{8,9},{9,8},{10,11... | collective-permute-start | bytes 1572872 | tf_op jit(solution)/shard_map/ppermute | solution.py:20
  44.8 4.8 %collective-permute-start.13 = (bf16[256,1024]{1,0:T(8,128)(2,1)S(1)}, bf16[256,1024]{1,0:T(8,128)(2,1)}, u32[]{:S(2)}, u32[]{:S(2)}) collective-permute-start(bf16[256,1024]{1,0:T(8,128)(2,1)S(1)} %collective-permute-done.6.refs_1_), channel_id=1, source_target_pairs={{4,8},{8,4},{5,9},{9,5},{6,10},{10,6},{7,11},{11,7},{20,24},{24,20... | collective-permute-start | bytes 1572872 | tf_op jit(solution)/shard_map/ppermute | solution.py:632
  49.6 15.8 %collective-permute-start.11 = (bf16[128,1024]{1,0:T(8,128)(2,1)S(1)}, bf16[128,1024]{1,0:T(8,128)(2,1)S(1)}, u32[]{:S(2)}, u32[]{:S(2)}) collective-permute-start(bf16[128,1024]{1,0:T(8,128)(2,1)S(1)} %get-tuple-element.47), channel_id=1, source_target_pairs={{0,1},{1,0},{2,3},{3,2},{4,5},{5,4},{6,7},{7,6},{8,9},{9,8},{10,11... | collective-permute-start | bytes 786440 | tf_op jit(solution)/shard_map/ppermute | solution.py:20
  50.2 22.9 %collective-permute-start.14 = (bf16[256,1024]{1,0:T(8,128)(2,1)}, bf16[256,1024]{1,0:T(8,128)(2,1)S(1)}, u32[]{:S(2)}, u32[]{:S(2)}) collective-permute-start(bf16[256,1024]{1,0:T(8,128)(2,1)} %collective-permute-done.13.src_any), channel_id=1, source_target_pairs={{0,4},{4,0},{8,12},{12,8},{1,5},{5,1},{9,13},{13,9},{2,6},{6,2},{1... | collective-permute-start | bytes 1572872 | tf_op jit(solution)/shard_map/ppermute | solution.py:20
  62.7 12.4 %collective-permute-start.8 = (bf16[128,1024]{1,0:T(8,128)(2,1)S(1)}, bf16[128,1024]{1,0:T(8,128)(2,1)S(1)}, u32[]{:S(2)}, u32[]{:S(2)}) collective-permute-start(bf16[128,1024]{1,0:T(8,128)(2,1)S(1)} %bitcast.39), channel_id=1, source_target_pairs={{0,2},{1,3},{2,0},{3,1},{4,6},{5,7},{6,4},{7,5},{8,10},{9,11},{10,... | collective-permute-start | bytes 786440 | tf_op jit(solution)/shard_map/ppermute | solution.py:20
  73.6 2.1 %collective-permute-start.15 = (bf16[128,1024]{1,0:T(8,128)(2,1)S(1)}, bf16[128,1024]{1,0:T(8,128)(2,1)S(1)}, u32[]{:S(2)}, u32[]{:S(2)}) collective-permute-start(bf16[128,1024]{1,0:T(8,128)(2,1)S(1)} %half_part.7), channel_id=1, source_target_pairs={{0,1},{1,0},{2,3},{3,2},{4,5},{5,4},{6,7},{7,6},{8,9},{9,8},{10,11... | collective-permute-start | bytes 786440 | tf_op jit(solution)/shard_map/ppermute | solution.py:20
  73.7 6.4 %collective-permute-start.12 = (bf16[64,1024]{1,0:T(8,128)(2,1)S(1)}, bf16[64,1024]{1,0:T(8,128)(2,1)S(1)}, u32[]{:S(2)}, u32[]{:S(2)}) collective-permute-start(bf16[64,1024]{1,0:T(8,128)(2,1)S(1)} %fusion), channel_id=1, source_target_pairs={{0,2},{1,3},{2,0},{3,1},{4,6},{5,7},{6,4},{7,5},{8,10},{9,11},{10,... | collective-permute-start | bytes 393224 | tf_op jit(solution)/shard_map/ppermute | solution.py:20
  75.8 6.7 %collective-permute-start.16 = (bf16[64,1024]{1,0:T(8,128)(2,1)S(1)}, bf16[64,1024]{1,0:T(8,128)(2,1)S(1)}, u32[]{:S(2)}, u32[]{:S(2)}) collective-permute-start(bf16[64,1024]{1,0:T(8,128)(2,1)S(1)} %fusion.1), channel_id=1, source_target_pairs={{0,2},{1,3},{2,0},{3,1},{4,6},{5,7},{6,4},{7,5},{8,10},{9,11},{10,... | collective-permute-start | bytes 393224 | tf_op jit(solution)/shard_map/ppermute | solution.py:20
  84.1 4.5 %collective-permute-start.17 = (bf16[72,512]{1,0:T(8,128)(2,1)S(1)}, bf16[72,512]{1,0:T(8,128)(2,1)S(1)}, u32[]{:S(2)}, u32[]{:S(2)}) collective-permute-start(bf16[72,512]{1,0:T(8,128)(2,1)S(1)} %get-tuple-element.51), channel_id=1, source_target_pairs={{0,4},{4,0},{8,12},{12,8},{1,5},{5,1},{9,13},{13,9},{2,6},{6,2},{1... | collective-permute-start | bytes 221192 | tf_op jit(solution)/shard_map/ppermute | solution.py:20
  85.9 8.5 %collective-permute-start.18 = (bf16[72,512]{1,0:T(8,128)(2,1)S(1)}, bf16[72,512]{1,0:T(8,128)(2,1)S(1)}, u32[]{:S(2)}, u32[]{:S(2)}) collective-permute-start(bf16[72,512]{1,0:T(8,128)(2,1)S(1)} %get-tuple-element.52), channel_id=1, source_target_pairs={{0,8},{4,12},{8,0},{12,4},{1,9},{5,13},{9,1},{13,5},{2,10},{6,14},... | collective-permute-start | bytes 221192 | tf_op jit(solution)/shard_map/ppermute | solution.py:20
  87.0 7.4 %collective-permute-start.19 = (bf16[72,512]{1,0:T(8,128)(2,1)S(1)}, bf16[72,512]{1,0:T(8,128)(2,1)S(1)}, u32[]{:S(2)}, u32[]{:S(2)}) collective-permute-start(bf16[72,512]{1,0:T(8,128)(2,1)S(1)} %get-tuple-element.53), channel_id=1, source_target_pairs={{0,12},{4,8},{8,4},{12,0},{1,13},{5,9},{9,5},{13,1},{2,14},{6,10},... | collective-permute-start | bytes 221192 | tf_op jit(solution)/shard_map/ppermute | solution.py:20
  95.2 1.9 %collective-permute-start.20 = (f32[2,256]{1,0:T(2,128)S(1)}, f32[2,256]{1,0:T(2,128)S(1)}, u32[]{:S(2)}, u32[]{:S(2)}) collective-permute-start(f32[2,256]{1,0:T(2,128)S(1)} %final_part.1.refs_0_), channel_id=1, source_target_pairs={{0,1},{1,0},{2,3},{3,2},{4,5},{5,4},{6,7},{7,6},{8,9},{9,8},{10,11... | collective-permute-start | bytes 6152 | tf_op jit(solution)/shard_map/ppermute | solution.py:20
  95.3 3.7 %collective-permute-start.21 = (f32[2,256]{1,0:T(2,128)S(1)}, f32[2,256]{1,0:T(2,128)S(1)}, u32[]{:S(2)}, u32[]{:S(2)}) collective-permute-start(f32[2,256]{1,0:T(2,128)S(1)} %final_part.1.refs_0_), channel_id=1, source_target_pairs={{0,2},{1,3},{2,0},{3,1},{4,6},{5,7},{6,4},{7,5},{8,10},{9,11},{10,... | collective-permute-start | bytes 6152 | tf_op jit(solution)/shard_map/ppermute | solution.py:20
  96.7 3.0 %collective-permute-start.22 = (f32[2,256]{1,0:T(2,128)S(1)}, f32[2,256]{1,0:T(2,128)S(1)}, u32[]{:S(2)}, u32[]{:S(2)}) collective-permute-start(f32[2,256]{1,0:T(2,128)S(1)} %final_part.1.refs_0_), channel_id=1, source_target_pairs={{0,3},{1,2},{2,1},{3,0},{4,7},{5,6},{6,5},{7,4},{8,11},{9,10},{10,... | collective-permute-start | bytes 6152 | tf_op jit(solution)/shard_map/ppermute | solution.py:20
